TPU v7x, 1024 devices: a whole 4x4x32 slice. The times are simulated.
1024 devices in a mesh: section: 32 (over x, z_hi, y), tp: 32 (over z_lo, core).
Axes of the slice: x: 4, y: 4, z: 32 (z_hi: 2, z_lo: 16; z = z_hi * 16 + z_lo), core: 2. Of those that a mesh axis runs over, the one named last changes fastest.
Arguments:
- head_outputs: bfloat16 [32, 128, 8192], P('section', None, 'tp'), may hold values from -6 to 6
- residual: bfloat16 [32, 128, 8192], P('section', 'tp'), may hold values from -38 to 38
- out_weight: bfloat16 [8192, 8192], P('tp'), may hold values from -0.0625 to 0.0625
- norm_gain: bfloat16 [8192], replicated, may hold values from 0.099609375 to 1.8984375
- prior_peak: float32 [32], P('section'), may hold values from 6 to 48
- qkv_weight: bfloat16 [8192, 9216], P(None, 'tp'), may hold values from -0.0625 to 0.0625
Outputs:
- stream: bfloat16 [32, 128, 8192], P('section', 'tp')
- projected: bfloat16 [32, 128, 9216], P('section', None, 'tp')
- group_peak: float32 [32], P('section')
All inputs are finite; a program needn't handle non-finite values.
Results may differ from a plain program's by a relative error of at most 0.02.
Values may be sent and summed in bfloat16 or wider, within the bound.
No kernel may reach another device: no remote copies, remote signals or barrier semaphores. Data moves between devices by JAX's collectives and lax.ppermute only.
A program may use at most 64 MiB of HBM per device.

v0:
```python
import functools
import jax
import jax.numpy as jnp
from jax import lax
from jax.experimental import pallas as pl
from jax.experimental.pallas import tpu as pltpu
from jax.sharding import PartitionSpec as P

epsilon = 1e-05
ceiling = 448.0

TP = 32
CHIPS = 16
ROWS = 8
TOK = 128
D = 8192
HALF = 4096
TAIL = 128
f32 = jnp.float32
bf16 = jnp.bfloat16


def across(x, d):
    return lax.ppermute(x, "tp", [(i, i ^ (2 * d)) for i in range(TP)])


def other_core(x):
    return lax.ppermute(x, "tp", [(i, i ^ 1) for i in range(TP)])


def next_section(x, sections):
    pairs = []
    for s in range(sections):
        shift = 16 if s % 4 == 3 else 0
        for t in range(TP):
            pairs.append((s * TP + t, ((s + 1) % sections) * TP + (t ^ shift)))
    return lax.ppermute(x, ("section", "tp"), pairs)


def shuffle(z):
    row = lax.broadcasted_iota(jnp.int32, (TOK, TOK), 0)
    col = lax.broadcasted_iota(jnp.int32, (TOK, TOK), 1)
    return jnp.where((row ^ (z * ROWS)) == col, 1.0, 0.0).astype(bf16)


N_TILE = 2048


def out_proj_body(ids, heads, weight, resid, out, rows):
    z = ids[0]
    core = ids[1]

    @pl.when(pl.program_id(0) == 0)
    def _():
        rows[...] = jnp.dot(shuffle(z), heads[...], preferred_element_type=f32).astype(bf16)

    product = jnp.dot(rows[...], weight[...], preferred_element_type=f32)
    out[...] = product.astype(out.dtype)
    mine = resid[...].astype(f32)
    zero = jnp.zeros_like(mine)
    eight = jnp.where(core == 0, jnp.concatenate([mine, zero], 0), jnp.concatenate([zero, mine], 0))
    out[0:ROWS, :] = (product[0:ROWS, :] + eight).astype(out.dtype)


def out_proj(ids, which, heads, weight, resid, dtype):
    tiles = HALF // N_TILE
    return pl.pallas_call(
        out_proj_body,
        out_shape=jax.ShapeDtypeStruct((TOK, HALF), dtype),
        grid_spec=pltpu.PrefetchScalarGridSpec(
            num_scalar_prefetch=1,
            grid=(tiles,),
            in_specs=[
                pl.BlockSpec((TOK, 256), lambda i, ids: (0, 0)),
                pl.BlockSpec((256, N_TILE), lambda i, ids: (0, ids[which] * tiles + i)),
                pl.BlockSpec((4, N_TILE), lambda i, ids: (0, ids[which] * tiles + i)),
            ],
            out_specs=pl.BlockSpec((TOK, N_TILE), lambda i, ids: (0, i)),
            scratch_shapes=[pltpu.VMEM((TOK, 256), bf16)],
        ),
        name="out_proj",
    )(ids, heads, weight, resid)


def cast_body(ids, own, twin, gain, peak_in, payload, peaks):
    wide = own[...].astype(f32)
    wide_twin = twin[...].astype(f32)
    total = jnp.sum(wide * wide, axis=-1, keepdims=True) + jnp.sum(wide_twin * wide_twin, axis=-1, keepdims=True)
    normed = wide * lax.rsqrt(total / D + epsilon) * gain[...].astype(f32)
    unit = jnp.full((ROWS, TAIL), peak_in[0] / ceiling, f32).astype(bf16)
    payload[:, 0:HALF] = jnp.clip(normed / unit[:, 0:1].astype(f32), -ceiling, ceiling).astype(bf16)
    payload[:, HALF:] = unit
    peak = jnp.max(jnp.max(jnp.abs(normed), axis=1, keepdims=True), axis=0, keepdims=True)
    peak = jnp.broadcast_to(peak, (ROWS, TAIL))
    high = peak.astype(bf16)
    low = (peak - high.astype(f32)).astype(bf16)
    lane = lax.broadcasted_iota(jnp.int32, (ROWS, TAIL), 1)
    peaks[...] = jnp.where(lane == 0, high.astype(f32), low.astype(f32)).astype(bf16)


def cast(ids, own, twin, gain, prior_peak):
    return pl.pallas_call(
        cast_body,
        out_shape=(
            jax.ShapeDtypeStruct((ROWS, HALF + TAIL), bf16),
            jax.ShapeDtypeStruct((ROWS, TAIL), bf16),
        ),
        grid_spec=pltpu.PrefetchScalarGridSpec(
            num_scalar_prefetch=1,
            grid=(1,),
            in_specs=[
                pl.BlockSpec((ROWS, HALF), lambda i, ids: (0, 0)),
                pl.BlockSpec((ROWS, HALF), lambda i, ids: (0, 0)),
                pl.BlockSpec((1, HALF), lambda i, ids: (0, ids[1])),
                pl.BlockSpec(memory_space=pltpu.SMEM),
            ],
            out_specs=[
                pl.BlockSpec((ROWS, HALF + TAIL), lambda i, ids: (0, 0)),
                pl.BlockSpec((ROWS, TAIL), lambda i, ids: (0, 0)),
            ],
        ),
        name="cast",
    )(ids, own, twin, gain.reshape(1, D), prior_peak)


K_TILE = 2048


def first_half_body(ids, weight, a, out):
    part = lax.dot_general(weight[...], a[...], (((1,), (1,)), ((), ())), preferred_element_type=f32)

    @pl.when(pl.program_id(0) == 0)
    def _():
        out[...] = part

    @pl.when(pl.program_id(0) > 0)
    def _():
        out[...] += part


def first_half(ids, weight, a):
    steps = HALF // K_TILE
    n = weight.shape[0]
    return pl.pallas_call(
        first_half_body,
        out_shape=jax.ShapeDtypeStruct((n, TOK), f32),
        grid_spec=pltpu.PrefetchScalarGridSpec(
            num_scalar_prefetch=1,
            grid=(steps,),
            in_specs=[
                pl.BlockSpec((n, K_TILE), lambda i, ids: (0, ids[1] * steps + i)),
                pl.BlockSpec((TOK, K_TILE), lambda i, ids: (0, i)),
            ],
            out_specs=pl.BlockSpec((n, TOK), lambda i, ids: (0, 0)),
        ),
        name="first_half",
    )(ids, weight, a)


def both_parts(tail):
    wide = tail.astype(f32)
    return wide[:, 0:1] + wide[:, 1:2]


def second_half_body(ids, weight, a, start, unit, tail, tail_twin, out, peak, acc):
    i = pl.program_id(0)
    part = lax.dot_general(weight[...], a[...], (((1,), (1,)), ((), ())), preferred_element_type=f32)

    @pl.when(i == 0)
    def _():
        acc[...] = start[...] + part

    @pl.when(i > 0)
    def _():
        acc[...] += part

    @pl.when(i == pl.num_programs(0) - 1)
    def _():
        scaled = (acc[...] * unit[0:1, 0:1].astype(f32)).astype(bf16)
        out[...] = jnp.dot(scaled, shuffle(ids[3]), preferred_element_type=f32).astype(bf16)
        ends = jnp.maximum(both_parts(tail[...]), both_parts(tail_twin[...]))
        peak[0] = jnp.max(ends)


def second_half(ids, weight, a, start, unit, twin):
    steps = HALF // K_TILE
    n = weight.shape[0]
    return pl.pallas_call(
        second_half_body,
        out_shape=(jax.ShapeDtypeStruct((n, TOK), bf16), jax.ShapeDtypeStruct((1,), f32)),
        grid_spec=pltpu.PrefetchScalarGridSpec(
            num_scalar_prefetch=1,
            grid=(steps,),
            in_specs=[
                pl.BlockSpec((n, K_TILE), lambda i, ids: (0, ids[2] * steps + i)),
                pl.BlockSpec((TOK, K_TILE), lambda i, ids: (0, i)),
                pl.BlockSpec((n, TOK), lambda i, ids: (0, 0)),
                pl.BlockSpec((ROWS, TAIL), lambda i, ids: (0, HALF // TAIL)),
                pl.BlockSpec((TOK, TAIL), lambda i, ids: (0, HALF // TAIL)),
                pl.BlockSpec((TOK, TAIL), lambda i, ids: (0, HALF // TAIL)),
            ],
            out_specs=[
                pl.BlockSpec((n, TOK), lambda i, ids: (0, 0)),
                pl.BlockSpec(memory_space=pltpu.SMEM),
            ],
            scratch_shapes=[pltpu.VMEM((n, TOK), f32)],
        ),
        name="second_half",
    )(ids, weight, a, start, unit, twin, a)


def cat(*blocks):
    return jnp.concatenate(blocks, axis=0)


def split(x):
    return [x[k * ROWS : (k + 1) * ROWS] for k in range(x.shape[0] // ROWS)]


def reduce_rounds(kept, incoming):
    def send(d, *which):
        got = across(cat(*[p[o].astype(bf16) for o in which]), d)
        return [g.astype(f32) for g in split(got)]

    last = slice(15 * ROWS, 16 * ROWS)
    first_out = (kept[last] + incoming[last].astype(f32)).astype(bf16)
    first_out, kept, incoming = lax.optimization_barrier((first_out, kept, incoming))
    p = [k + i.astype(f32) for k, i in zip(split(kept), split(incoming))]
    a = across(first_out, 1).astype(f32)
    b13, b11, b7 = send(1, 13, 11, 7)
    p[14] = p[14] + a
    (b14,) = send(2, 14)
    c9, c5, c3 = send(1, 9, 5, 3)
    p[10] = p[10] + b11
    p[6] = p[6] + b7
    c10, c6 = send(2, 10, 6)
    p[12] = p[12] + b13 + b14
    (c12,) = send(4, 12)
    p[4] = p[4] + c5 + c6
    p[2] = p[2] + c3
    (d4,) = send(4, 4)
    (d2,) = send(2, 2)
    (d1,) = send(1, 1)
    p[8] = p[8] + c9 + c10 + c12
    (d8,) = send(8, 8)
    return p[0] + d1 + d2 + d4 + d8


def gather_rounds(own):
    b = {0: own}
    for d in (8, 4, 2, 1):
        b[d] = across(own, d)
    b[12] = across(b[8], 4)
    b[10], b[6] = split(across(cat(b[8], b[4]), 2))
    b[9], b[5], b[3] = split(across(cat(b[8], b[4], b[2]), 1))
    b[14] = across(b[12], 2)
    b[13], b[11], b[7] = split(across(cat(b[12], b[10], b[6]), 1))
    b[15] = across(b[14], 1)
    return cat(*[b[o] for o in range(CHIPS)])


def shards(sections, head_outputs, residual, out_weight, norm_gain, prior_peak, qkv_weight):
    heads = head_outputs[0]
    resid = residual[0]
    section = lax.axis_index("section")
    place = lax.axis_index("tp")
    z = place // 2
    core = place % 2
    label = z ^ jnp.where(section % 4 == 0, 8, 0)
    ids = jnp.stack([z, core, 1 - core, label]).astype(jnp.int32)

    outgoing = out_proj(ids, 2, heads, out_weight, resid, bf16)
    incoming = other_core(outgoing)
    kept = out_proj(ids, 1, heads, out_weight, resid, f32)
    own = lax.reduce_precision(reduce_rounds(kept, incoming), 8, 7).astype(bf16)
    twin = other_core(own)
    outbound, peaks = cast(ids, own, twin, norm_gain, prior_peak)
    arrived = next_section(outbound, sections)

    payload = jnp.concatenate([arrived[:, :HALF], peaks], axis=1)
    mine = gather_rounds(payload)
    theirs = other_core(mine)

    weight = qkv_weight.T
    started = first_half(ids, weight, mine)
    columns, group_peak = second_half(ids, weight, theirs, started, arrived, mine)
    projected = columns.T

    first_row = core == 0
    own_rows = jnp.where(first_row, own[0:4], own[4:8])
    twin_rows = jnp.where(first_row, twin[0:4], twin[4:8])
    stream = jnp.where(
        first_row,
        jnp.concatenate([own_rows, twin_rows], axis=1),
        jnp.concatenate([twin_rows, own_rows], axis=1),
    )
    return (stream[None], projected[None], group_peak)


def solution(mesh):
    return jax.shard_map(
        functools.partial(shards, mesh.shape["section"]),
        mesh=mesh,
        in_specs=(
            P("section", None, "tp"),
            P("section", "tp", None),
            P("tp", None),
            P(),
            P("section"),
            P(None, "tp"),
        ),
        out_specs=(P("section", "tp", None), P("section", None, "tp"), P("section")),
        check_vma=False,
    )
```

profile of v0, /device:TPU:1, one launch (start us, length us, event | category | flops | bytes accessed | tf_op | source)
XLA Modules:
  0.0 187.3 jit_solution(13537949134724450641)
XLA Ops:
  0.7 0.7 pad_add_fusion.ids
  1.3 3.6 %out_proj.3 = bf16[128,4096]{1,0:T(8,128)(2,1)} custom-call(s32[4]{0:T(128)} %pad_add_fusion.ids, bf16[128,256]{1,0:T(8,128)(2,1)} %bitcast.16, bf16[256,8192]{1,0:T(8,128)(2,1)} %weight.3, bf16[4,8192]{1,0:T(4,128)(2,1)} %bitcast.18), custom_call_target="tpu_custom_call" | custom-call | tf_op jit(solution)/shard_map/out_proj/pallas_call | solution.py:67
  4.9 16.0 %collective-permute-start = (bf16[128,4096]{1,0:T(8,128)(2,1)}, bf16[128,4096]{1,0:T(8,128)(2,1)S(1)}, u32[]{:S(2)}, u32[]{:S(2)}) collective-permute-start(bf16[128,4096]{1,0:T(8,128)(2,1)} %out_proj.3), channel_id=1, source_target_pairs={{0,1},{1,0},{2,3},{3,2},{4,5},{5,4},{6,7},{7,6},{8,9},{9,8},{10,11... | collective-permute-start | bytes 3145736 | tf_op jit(solution)/shard_map/ppermute | solution.py:28
  20.9 3.7 %out_proj.2 = f32[128,4096]{1,0:T(8,128)} custom-call(s32[4]{0:T(128)} %pad_add_fusion.ids, bf16[128,256]{1,0:T(8,128)(2,1)} %bitcast.17, bf16[256,8192]{1,0:T(8,128)(2,1)} %weight.3, bf16[4,8192]{1,0:T(4,128)(2,1)} %bitcast.19), custom_call_target="tpu_custom_call" | custom-call | tf_op jit(solution)/shard_map/out_proj/pallas_call | solution.py:67
  24.7 0.9 fusion
  25.6 1.9 %collective-permute-start.7 = (bf16[8,4096]{1,0:T(8,128)(2,1)S(1)}, bf16[8,4096]{1,0:T(8,128)(2,1)S(1)}, u32[]{:S(2)}, u32[]{:S(2)}) collective-permute-start(bf16[8,4096]{1,0:T(8,128)(2,1)S(1)} %fusion), channel_id=1, source_target_pairs={{0,2},{1,3},{2,0},{3,1},{4,6},{5,7},{6,4},{7,5},{8,10},{9,11},{10,... | collective-permute-start | bytes 196616 | tf_op jit(solution)/shard_map/ppermute | solution.py:24
  27.5 3.6 %collective-permute-done.7 = bf16[8,4096]{1,0:T(8,128)(2,1)S(1)} collective-permute-done((bf16[8,4096]{1,0:T(8,128)(2,1)S(1)}, bf16[8,4096]{1,0:T(8,128)(2,1)S(1)}, u32[]{:S(2)}, u32[]{:S(2)}) %collective-permute-start.7) | collective-permute-done | bytes 65568 | tf_op jit(solution)/shard_map/ppermute | solution.py:24
  31.1 1.4 add_convert_fusion.13
  32.5 2.2 %collective-permute-start.4 = (bf16[24,4096]{1,0:T(8,128)(2,1)S(1)}, bf16[24,4096]{1,0:T(8,128)(2,1)S(1)}, u32[]{:S(2)}, u32[]{:S(2)}) collective-permute-start(bf16[24,4096]{1,0:T(8,128)(2,1)S(1)} %pad_maximum_fusion.3), channel_id=1, source_target_pairs={{0,2},{1,3},{2,0},{3,1},{4,6},{5,7},{6,4},{7,5},{8,10},{9,11},{10,... | collective-permute-start | bytes 589832 | tf_op jit(solution)/shard_map/ppermute | solution.py:24
  34.7 1.9 %collective-permute-start.8 = (bf16[8,4096]{1,0:T(8,128)(2,1)S(1)}, bf16[8,4096]{1,0:T(8,128)(2,1)S(1)}, u32[]{:S(2)}, u32[]{:S(2)}) collective-permute-start(bf16[8,4096]{1,0:T(8,128)(2,1)S(1)} %get-tuple-element.24), channel_id=1, source_target_pairs={{0,4},{1,5},{2,6},{3,7},{4,0},{5,1},{6,2},{7,3},{8,12},{9,13},{10,... | collective-permute-start | bytes 196616 | tf_op jit(solution)/shard_map/ppermute | solution.py:24
  36.7 3.1 %collective-permute-start.2 = (bf16[24,4096]{1,0:T(8,128)(2,1)S(1)}, bf16[24,4096]{1,0:T(8,128)(2,1)S(1)}, u32[]{:S(2)}, u32[]{:S(2)}) collective-permute-start(bf16[24,4096]{1,0:T(8,128)(2,1)S(1)} %pad_maximum_fusion.2), channel_id=1, source_target_pairs={{0,2},{1,3},{2,0},{3,1},{4,6},{5,7},{6,4},{7,5},{8,10},{9,11},{10,... | collective-permute-start | bytes 589832 | tf_op jit(solution)/shard_map/ppermute | solution.py:24
  39.8 1.0 collective-permute-done.8
  40.7 0.0 collective-permute-done.4
  40.8 1.1 add_convert_fusion.5
  41.9 0.0 copy-start.6
  41.9 3.8 %collective-permute-start.5 = (bf16[16,4096]{1,0:T(8,128)(2,1)S(1)}, bf16[16,4096]{1,0:T(8,128)(2,1)S(1)}, u32[]{:S(2)}, u32[]{:S(2)}) collective-permute-start(bf16[16,4096]{1,0:T(8,128)(2,1)S(1)} %pad_maximum_fusion.5), channel_id=1, source_target_pairs={{0,4},{1,5},{2,6},{3,7},{4,0},{5,1},{6,2},{7,3},{8,12},{9,13},{10,... | collective-permute-start | bytes 393224 | tf_op jit(solution)/shard_map/ppermute | solution.py:24
  45.7 1.9 %collective-permute-start.9 = (bf16[8,4096]{1,0:T(8,128)(2,1)S(1)}, bf16[8,4096]{1,0:T(8,128)(2,1)S(1)}, u32[]{:S(2)}, u32[]{:S(2)}) collective-permute-start(bf16[8,4096]{1,0:T(8,128)(2,1)S(1)} %get-tuple-element.21), channel_id=1, source_target_pairs={{0,8},{1,9},{2,10},{3,11},{4,12},{5,13},{6,14},{7,15},{8,0},{9,1},... | collective-permute-start | bytes 196616 | tf_op jit(solution)/shard_map/ppermute | solution.py:24
  47.6 1.9 %collective-permute-start.1 = (bf16[8,4096]{1,0:T(8,128)(2,1)S(1)}, bf16[8,4096]{1,0:T(8,128)(2,1)S(1)}, u32[]{:S(2)}, u32[]{:S(2)}) collective-permute-start(bf16[8,4096]{1,0:T(8,128)(2,1)S(1)} %get-tuple-element.23), channel_id=1, source_target_pairs={{0,2},{1,3},{2,0},{3,1},{4,6},{5,7},{6,4},{7,5},{8,10},{9,11},{10,... | collective-permute-start | bytes 196616 | tf_op jit(solution)/shard_map/ppermute | solution.py:24
  49.5 0.0 collective-permute-done.2
  49.5 6.7 %collective-permute-done.9 = bf16[8,4096]{1,0:T(8,128)(2,1)S(1)} collective-permute-done((bf16[8,4096]{1,0:T(8,128)(2,1)S(1)}, bf16[8,4096]{1,0:T(8,128)(2,1)S(1)}, u32[]{:S(2)}, u32[]{:S(2)}) %collective-permute-start.9) | collective-permute-done | bytes 65568 | tf_op jit(solution)/shard_map/ppermute | solution.py:24
  56.3 0.0 collective-permute-done.5
  56.3 1.1 add_convert_fusion.3
  57.4 6.7 %collective-permute-start.10 = (bf16[8,4096]{1,0:T(8,128)(2,1)S(1)}, bf16[8,4096]{1,0:T(8,128)(2,1)S(1)}, u32[]{:S(2)}, u32[]{:S(2)}) collective-permute-start(bf16[8,4096]{1,0:T(8,128)(2,1)S(1)} %get-tuple-element.18), channel_id=1, source_target_pairs={{0,16},{1,17},{2,18},{3,19},{4,20},{5,21},{6,22},{7,23},{8,24},{9,... | collective-permute-start | bytes 196616 | tf_op jit(solution)/shard_map/ppermute | solution.py:24
  64.1 5.3 %collective-permute-start.3 = (bf16[8,4096]{1,0:T(8,128)(2,1)S(1)}, bf16[8,4096]{1,0:T(8,128)(2,1)S(1)}, u32[]{:S(2)}, u32[]{:S(2)}) collective-permute-start(bf16[8,4096]{1,0:T(8,128)(2,1)S(1)} %get-tuple-element.19), channel_id=1, source_target_pairs={{0,4},{1,5},{2,6},{3,7},{4,0},{5,1},{6,2},{7,3},{8,12},{9,13},{10,... | collective-permute-start | bytes 196616 | tf_op jit(solution)/shard_map/ppermute | solution.py:24
  69.5 2.9 %collective-permute-start.6 = (bf16[8,4096]{1,0:T(8,128)(2,1)S(1)}, bf16[8,4096]{1,0:T(8,128)(2,1)S(1)}, u32[]{:S(2)}, u32[]{:S(2)}) collective-permute-start(bf16[8,4096]{1,0:T(8,128)(2,1)S(1)} %get-tuple-element.17), channel_id=1, source_target_pairs={{0,8},{1,9},{2,10},{3,11},{4,12},{5,13},{6,14},{7,15},{8,0},{9,1},... | collective-permute-start | bytes 196616 | tf_op jit(solution)/shard_map/ppermute | solution.py:24
  72.3 0.0 collective-permute-done.1
  72.3 7.3 %collective-permute-done.10 = bf16[8,4096]{1,0:T(8,128)(2,1)S(1)} collective-permute-done((bf16[8,4096]{1,0:T(8,128)(2,1)S(1)}, bf16[8,4096]{1,0:T(8,128)(2,1)S(1)}, u32[]{:S(2)}, u32[]{:S(2)}) %collective-permute-start.10) | collective-permute-done | bytes 65568 | tf_op jit(solution)/shard_map/ppermute | solution.py:24
  79.6 0.0 collective-permute-done.3
  79.6 2.2 %collective-permute-done.6 = bf16[8,4096]{1,0:T(8,128)(2,1)S(1)} collective-permute-done((bf16[8,4096]{1,0:T(8,128)(2,1)S(1)}, bf16[8,4096]{1,0:T(8,128)(2,1)S(1)}, u32[]{:S(2)}, u32[]{:S(2)}) %collective-permute-start.6) | collective-permute-done | bytes 65568 | tf_op jit(solution)/shard_map/ppermute | solution.py:24
  81.9 1.0 reduce-precision_convert_fusion.own
  82.8 5.5 %collective-permute-start.11 = (bf16[8,4096]{1,0:T(8,128)(2,1)S(1)}, bf16[8,4096]{1,0:T(8,128)(2,1)S(1)}, u32[]{:S(2)}, u32[]{:S(2)}) collective-permute-start(bf16[8,4096]{1,0:T(8,128)(2,1)S(1)} %reduce-precision_convert_fusion.own), channel_id=1, source_target_pairs={{0,1},{1,0},{2,3},{3,2},{4,5},{5,4},{6,7},{7,6},{8,9},{9,8},{10,11... | collective-permute-start | bytes 196616 | tf_op jit(solution)/shard_map/ppermute | solution.py:28
  88.3 0.6 reshape.64.gain
  89.6 0.0 collective-permute-done.11.twin
  89.6 0.0 copy-start.4
  89.6 0.6 copy-done.4
  90.2 2.3 %cast.1 = (bf16[8,4224]{1,0:T(8,128)(2,1)}, bf16[8,128]{1,0:T(8,128)(2,1)}) custom-call(s32[4]{0:T(128)} %pad_add_fusion.ids, bf16[8,4096]{1,0:T(8,128)(2,1)} %copy-done.2, bf16[8,4096]{1,0:T(8,128)(2,1)} %copy-done.4, bf16[1,8192]{1,0:T(2,128)(2,1)} %reshape.64.gain, f32[1]{0:T(128)S(6)} %copy.24.peak_in), custom_call_target="tpu_custom_call" | custom-call | tf_op jit(solution)/shard_map/cast/pallas_call | solution.py:102
  92.6 1.9 %collective-permute-start.12 = (bf16[8,4224]{1,0:T(8,128)(2,1)}, bf16[8,4224]{1,0:T(8,128)(2,1)S(1)}, u32[]{:S(2)}, u32[]{:S(2)}) collective-permute-start(bf16[8,4224]{1,0:T(8,128)(2,1)} %get-tuple-element.13), channel_id=1, source_target_pairs={{0,32},{1,33},{2,34},{3,35},{4,36},{5,37},{6,38},{7,39},{8,40},{9,... | collective-permute-start | bytes 202760 | tf_op jit(solution)/shard_map/ppermute | solution.py:37
  94.5 16.9 %collective-permute-done.12.unit = bf16[8,4224]{1,0:T(8,128)(2,1)S(1)} collective-permute-done((bf16[8,4224]{1,0:T(8,128)(2,1)}, bf16[8,4224]{1,0:T(8,128)(2,1)S(1)}, u32[]{:S(2)}, u32[]{:S(2)}) %collective-permute-start.12) | collective-permute-done | bytes 67616 | tf_op jit(solution)/shard_map/ppermute | solution.py:37
  111.4 0.7 pad_maximum_fusion.6
  112.1 15.4 %collective-permute-start.15 = (bf16[8,4224]{1,0:T(8,128)(2,1)S(1)}, bf16[8,4224]{1,0:T(8,128)(2,1)S(1)}, u32[]{:S(2)}, u32[]{:S(2)}) collective-permute-start(bf16[8,4224]{1,0:T(8,128)(2,1)S(1)} %get-tuple-element.31), channel_id=1, source_target_pairs={{0,16},{1,17},{2,18},{3,19},{4,20},{5,21},{6,22},{7,23},{8,24},{9,... | collective-permute-start | bytes 202760 | tf_op jit(solution)/shard_map/ppermute | solution.py:24
  127.5 1.9 %collective-permute-start.16 = (bf16[8,4224]{1,0:T(8,128)(2,1)S(1)}, bf16[8,4224]{1,0:T(8,128)(2,1)S(1)}, u32[]{:S(2)}, u32[]{:S(2)}) collective-permute-start(bf16[8,4224]{1,0:T(8,128)(2,1)S(1)} %get-tuple-element.31), channel_id=1, source_target_pairs={{0,8},{1,9},{2,10},{3,11},{4,12},{5,13},{6,14},{7,15},{8,0},{9,1},... | collective-permute-start | bytes 202760 | tf_op jit(solution)/shard_map/ppermute | solution.py:24
  129.4 0.9 fusion.2
  130.4 1.9 %collective-permute-start.14 = (bf16[8,4224]{1,0:T(8,128)(2,1)S(1)}, bf16[8,4224]{1,0:T(8,128)(2,1)S(1)}, u32[]{:S(2)}, u32[]{:S(2)}) collective-permute-start(bf16[8,4224]{1,0:T(8,128)(2,1)S(1)} %get-tuple-element.31), channel_id=1, source_target_pairs={{0,4},{1,5},{2,6},{3,7},{4,0},{5,1},{6,2},{7,3},{8,12},{9,13},{10,... | collective-permute-start | bytes 202760 | tf_op jit(solution)/shard_map/ppermute | solution.py:24
  132.3 1.9 %collective-permute-start.13 = (bf16[8,4224]{1,0:T(8,128)(2,1)S(1)}, bf16[8,4224]{1,0:T(8,128)(2,1)S(1)}, u32[]{:S(2)}, u32[]{:S(2)}) collective-permute-start(bf16[8,4224]{1,0:T(8,128)(2,1)S(1)} %get-tuple-element.31), channel_id=1, source_target_pairs={{0,2},{1,3},{2,0},{3,1},{4,6},{5,7},{6,4},{7,5},{8,10},{9,11},{10,... | collective-permute-start | bytes 202760 | tf_op jit(solution)/shard_map/ppermute | solution.py:24
  134.2 0.0 collective-permute-done.15
  134.2 4.9 %collective-permute-done.16 = bf16[8,4224]{1,0:T(8,128)(2,1)S(1)} collective-permute-done((bf16[8,4224]{1,0:T(8,128)(2,1)S(1)}, bf16[8,4224]{1,0:T(8,128)(2,1)S(1)}, u32[]{:S(2)}, u32[]{:S(2)}) %collective-permute-start.16) | collective-permute-done | bytes 67616 | tf_op jit(solution)/shard_map/ppermute | solution.py:24
  139.1 1.9 %collective-permute-start.18 = (bf16[16,4224]{1,0:T(8,128)(2,1)S(1)}, bf16[16,4224]{1,0:T(8,128)(2,1)S(1)}, u32[]{:S(2)}, u32[]{:S(2)}) collective-permute-start(bf16[16,4224]{1,0:T(8,128)(2,1)S(1)} %pad_maximum_fusion.4), channel_id=1, source_target_pairs={{0,4},{1,5},{2,6},{3,7},{4,0},{5,1},{6,2},{7,3},{8,12},{9,13},{10,... | collective-permute-start | bytes 405512 | tf_op jit(solution)/shard_map/ppermute | solution.py:24
  141.0 0.0 collective-permute-done.14
  141.1 1.9 %collective-permute-start.17 = (bf16[24,4224]{1,0:T(8,128)(2,1)S(1)}, bf16[24,4224]{1,0:T(8,128)(2,1)S(1)}, u32[]{:S(2)}, u32[]{:S(2)}) collective-permute-start(bf16[24,4224]{1,0:T(8,128)(2,1)S(1)} %pad_maximum_fusion), channel_id=1, source_target_pairs={{0,2},{1,3},{2,0},{3,1},{4,6},{5,7},{6,4},{7,5},{8,10},{9,11},{10,... | collective-permute-start | bytes 608264 | tf_op jit(solution)/shard_map/ppermute | solution.py:24
  143.0 6.2 %collective-permute-start.19 = (bf16[8,4224]{1,0:T(8,128)(2,1)S(1)}, bf16[8,4224]{1,0:T(8,128)(2,1)S(1)}, u32[]{:S(2)}, u32[]{:S(2)}) collective-permute-start(bf16[8,4224]{1,0:T(8,128)(2,1)S(1)} %collective-permute-done.15), channel_id=1, source_target_pairs={{0,8},{1,9},{2,10},{3,11},{4,12},{5,13},{6,14},{7,15},{8,0},{9,1},... | collective-permute-start | bytes 202760 | tf_op jit(solution)/shard_map/ppermute | solution.py:24
  149.2 0.0 collective-permute-done.13
  149.2 2.8 %collective-permute-done.19 = bf16[8,4224]{1,0:T(8,128)(2,1)S(1)} collective-permute-done((bf16[8,4224]{1,0:T(8,128)(2,1)S(1)}, bf16[8,4224]{1,0:T(8,128)(2,1)S(1)}, u32[]{:S(2)}, u32[]{:S(2)}) %collective-permute-start.19) | collective-permute-done | bytes 67616 | tf_op jit(solution)/shard_map/ppermute | solution.py:24
  152.0 4.3 %collective-permute-start.21 = (bf16[8,4224]{1,0:T(8,128)(2,1)S(1)}, bf16[8,4224]{1,0:T(8,128)(2,1)S(1)}, u32[]{:S(2)}, u32[]{:S(2)}) collective-permute-start(bf16[8,4224]{1,0:T(8,128)(2,1)S(1)} %collective-permute-done.19), channel_id=1, source_target_pairs={{0,4},{1,5},{2,6},{3,7},{4,0},{5,1},{6,2},{7,3},{8,12},{9,13},{10,... | collective-permute-start | bytes 202760 | tf_op jit(solution)/shard_map/ppermute | solution.py:24
  156.4 0.0 copy-start.5
  156.4 1.9 %collective-permute-done.21 = bf16[8,4224]{1,0:T(8,128)(2,1)S(1)} collective-permute-done((bf16[8,4224]{1,0:T(8,128)(2,1)S(1)}, bf16[8,4224]{1,0:T(8,128)(2,1)S(1)}, u32[]{:S(2)}, u32[]{:S(2)}) %collective-permute-start.21) | collective-permute-done | bytes 67616 | tf_op jit(solution)/shard_map/ppermute | solution.py:24
  158.3 5.8 %collective-permute-start.22 = (bf16[8,4224]{1,0:T(8,128)(2,1)S(1)}, bf16[8,4224]{1,0:T(8,128)(2,1)S(1)}, u32[]{:S(2)}, u32[]{:S(2)}) collective-permute-start(bf16[8,4224]{1,0:T(8,128)(2,1)S(1)} %collective-permute-done.21), channel_id=1, source_target_pairs={{0,2},{1,3},{2,0},{3,1},{4,6},{5,7},{6,4},{7,5},{8,10},{9,11},{10,... | collective-permute-start | bytes 202760 | tf_op jit(solution)/shard_map/ppermute | solution.py:24
  164.1 0.0 collective-permute-done.18
  164.2 1.9 %collective-permute-start.20 = (bf16[24,4224]{1,0:T(8,128)(2,1)S(1)}, bf16[24,4224]{1,0:T(8,128)(2,1)S(1)}, u32[]{:S(2)}, u32[]{:S(2)}) collective-permute-start(bf16[24,4224]{1,0:T(8,128)(2,1)S(1)} %pad_maximum_fusion.1), channel_id=1, source_target_pairs={{0,2},{1,3},{2,0},{3,1},{4,6},{5,7},{6,4},{7,5},{8,10},{9,11},{10,... | collective-permute-start | bytes 608264 | tf_op jit(solution)/shard_map/ppermute | solution.py:24
  166.2 4.5 %collective-permute-done.20 = bf16[24,4224]{1,0:T(8,128)(2,1)S(1)} collective-permute-done((bf16[24,4224]{1,0:T(8,128)(2,1)S(1)}, bf16[24,4224]{1,0:T(8,128)(2,1)S(1)}, u32[]{:S(2)}, u32[]{:S(2)}) %collective-permute-start.20) | collective-permute-done | bytes 202784 | tf_op jit(solution)/shard_map/ppermute | solution.py:24
  170.8 7.0 %collective-permute-start.23 = (bf16[128,4224]{1,0:T(8,128)(2,1)S(1)}, bf16[128,4224]{1,0:T(8,128)(2,1)S(1)}, u32[]{:S(2)}, u32[]{:S(2)}) collective-permute-start(bf16[128,4224]{1,0:T(8,128)(2,1)S(1)} %constant_dynamic-update-slice_fusion.a.tail), channel_id=1, source_target_pairs={{0,1},{1,0},{2,3},{3,2},{4,5},{5,4},{6,7},{7,6},{8,9},{9,8},{10,11... | collective-permute-start | bytes 3244040 | tf_op jit(solution)/shard_map/ppermute | solution.py:28
  177.8 0.7 maximum_select_fusion
  178.5 3.7 %first_half.1.start = f32[288,128]{1,0:T(8,128)} custom-call(s32[4]{0:T(128)} %pad_add_fusion.ids, bf16[288,8192]{1,0:T(8,128)(2,1)} %bitcast.14, bf16[128,4224]{1,0:T(8,128)(2,1)} %copy-done), custom_call_target="tpu_custom_call" | custom-call | tf_op jit(solution)/shard_map/first_half/pallas_call | solution.py:144
  182.2 1.0 copy-done.1
  183.2 4.1 %second_half.1 = (bf16[288,128]{1,0:T(8,128)(2,1)}, f32[1]{0:T(128)}) custom-call(s32[4]{0:T(128)} %pad_add_fusion.ids, bf16[288,8192]{1,0:T(8,128)(2,1)} %bitcast.15, bf16[128,4224]{1,0:T(8,128)(2,1)} %copy-done.1, f32[288,128]{1,0:T(8,128)} %first_half.1.start, bf16[8,4224]{1,0:T(8,128)(2,1)} %copy-done.3, bf16[128,4224]{1,0:T(8,128)(2,1)} %copy-done, ...), custom_call_target="tpu_custom_call" | custom-call | tf_op jit(solution)/shard_map/second_half/pallas_call | solution.py:188
  (36 shorter events, 0.4 us)
Async XLA Ops:
  4.9 19.8 %collective-permute-start = (bf16[128,4096]{1,0:T(8,128)(2,1)}, bf16[128,4096]{1,0:T(8,128)(2,1)S(1)}, u32[]{:S(2)}, u32[]{:S(2)}) collective-permute-start(bf16[128,4096]{1,0:T(8,128)(2,1)} %out_proj.3), channel_id=1, source_target_pairs={{0,1},{1,0},{2,3},{3,2},{4,5},{5,4},{6,7},{7,6},{8,9},{9,8},{10,11... | collective-permute-start | bytes 3145736 | tf_op jit(solution)/shard_map/ppermute | solution.py:28
  25.6 5.5 %collective-permute-start.7 = (bf16[8,4096]{1,0:T(8,128)(2,1)S(1)}, bf16[8,4096]{1,0:T(8,128)(2,1)S(1)}, u32[]{:S(2)}, u32[]{:S(2)}) collective-permute-start(bf16[8,4096]{1,0:T(8,128)(2,1)S(1)} %fusion), channel_id=1, source_target_pairs={{0,2},{1,3},{2,0},{3,1},{4,6},{5,7},{6,4},{7,5},{8,10},{9,11},{10,... | collective-permute-start | bytes 196616 | tf_op jit(solution)/shard_map/ppermute | solution.py:24
  32.5 8.2 %collective-permute-start.4 = (bf16[24,4096]{1,0:T(8,128)(2,1)S(1)}, bf16[24,4096]{1,0:T(8,128)(2,1)S(1)}, u32[]{:S(2)}, u32[]{:S(2)}) collective-permute-start(bf16[24,4096]{1,0:T(8,128)(2,1)S(1)} %pad_maximum_fusion.3), channel_id=1, source_target_pairs={{0,2},{1,3},{2,0},{3,1},{4,6},{5,7},{6,4},{7,5},{8,10},{9,11},{10,... | collective-permute-start | bytes 589832 | tf_op jit(solution)/shard_map/ppermute | solution.py:24
  34.7 6.0 %collective-permute-start.8 = (bf16[8,4096]{1,0:T(8,128)(2,1)S(1)}, bf16[8,4096]{1,0:T(8,128)(2,1)S(1)}, u32[]{:S(2)}, u32[]{:S(2)}) collective-permute-start(bf16[8,4096]{1,0:T(8,128)(2,1)S(1)} %get-tuple-element.24), channel_id=1, source_target_pairs={{0,4},{1,5},{2,6},{3,7},{4,0},{5,1},{6,2},{7,3},{8,12},{9,13},{10,... | collective-permute-start | bytes 196616 | tf_op jit(solution)/shard_map/ppermute | solution.py:24
  36.7 12.8 %collective-permute-start.2 = (bf16[24,4096]{1,0:T(8,128)(2,1)S(1)}, bf16[24,4096]{1,0:T(8,128)(2,1)S(1)}, u32[]{:S(2)}, u32[]{:S(2)}) collective-permute-start(bf16[24,4096]{1,0:T(8,128)(2,1)S(1)} %pad_maximum_fusion.2), channel_id=1, source_target_pairs={{0,2},{1,3},{2,0},{3,1},{4,6},{5,7},{6,4},{7,5},{8,10},{9,11},{10,... | collective-permute-start | bytes 589832 | tf_op jit(solution)/shard_map/ppermute | solution.py:24
  41.9 46.4 %copy-start.6 = (bf16[8192]{0:T(1024)(128)(2,1)S(1)}, bf16[8192]{0:T(1024)(128)(2,1)}, u32[]{:S(2)}) copy-start(bf16[8192]{0:T(1024)(128)(2,1)} %param.9) | copy-start | bytes 49156
  41.9 14.4 %collective-permute-start.5 = (bf16[16,4096]{1,0:T(8,128)(2,1)S(1)}, bf16[16,4096]{1,0:T(8,128)(2,1)S(1)}, u32[]{:S(2)}, u32[]{:S(2)}) collective-permute-start(bf16[16,4096]{1,0:T(8,128)(2,1)S(1)} %pad_maximum_fusion.5), channel_id=1, source_target_pairs={{0,4},{1,5},{2,6},{3,7},{4,0},{5,1},{6,2},{7,3},{8,12},{9,13},{10,... | collective-permute-start | bytes 393224 | tf_op jit(solution)/shard_map/ppermute | solution.py:24
  45.7 10.6 %collective-permute-start.9 = (bf16[8,4096]{1,0:T(8,128)(2,1)S(1)}, bf16[8,4096]{1,0:T(8,128)(2,1)S(1)}, u32[]{:S(2)}, u32[]{:S(2)}) collective-permute-start(bf16[8,4096]{1,0:T(8,128)(2,1)S(1)} %get-tuple-element.21), channel_id=1, source_target_pairs={{0,8},{1,9},{2,10},{3,11},{4,12},{5,13},{6,14},{7,15},{8,0},{9,1},... | collective-permute-start | bytes 196616 | tf_op jit(solution)/shard_map/ppermute | solution.py:24
  47.6 24.7 %collective-permute-start.1 = (bf16[8,4096]{1,0:T(8,128)(2,1)S(1)}, bf16[8,4096]{1,0:T(8,128)(2,1)S(1)}, u32[]{:S(2)}, u32[]{:S(2)}) collective-permute-start(bf16[8,4096]{1,0:T(8,128)(2,1)S(1)} %get-tuple-element.23), channel_id=1, source_target_pairs={{0,2},{1,3},{2,0},{3,1},{4,6},{5,7},{6,4},{7,5},{8,10},{9,11},{10,... | collective-permute-start | bytes 196616 | tf_op jit(solution)/shard_map/ppermute | solution.py:24
  57.4 22.2 %collective-permute-start.10 = (bf16[8,4096]{1,0:T(8,128)(2,1)S(1)}, bf16[8,4096]{1,0:T(8,128)(2,1)S(1)}, u32[]{:S(2)}, u32[]{:S(2)}) collective-permute-start(bf16[8,4096]{1,0:T(8,128)(2,1)S(1)} %get-tuple-element.18), channel_id=1, source_target_pairs={{0,16},{1,17},{2,18},{3,19},{4,20},{5,21},{6,22},{7,23},{8,24},{9,... | collective-permute-start | bytes 196616 | tf_op jit(solution)/shard_map/ppermute | solution.py:24
  64.1 15.5 %collective-permute-start.3 = (bf16[8,4096]{1,0:T(8,128)(2,1)S(1)}, bf16[8,4096]{1,0:T(8,128)(2,1)S(1)}, u32[]{:S(2)}, u32[]{:S(2)}) collective-permute-start(bf16[8,4096]{1,0:T(8,128)(2,1)S(1)} %get-tuple-element.19), channel_id=1, source_target_pairs={{0,4},{1,5},{2,6},{3,7},{4,0},{5,1},{6,2},{7,3},{8,12},{9,13},{10,... | collective-permute-start | bytes 196616 | tf_op jit(solution)/shard_map/ppermute | solution.py:24
  69.5 12.4 %collective-permute-start.6 = (bf16[8,4096]{1,0:T(8,128)(2,1)S(1)}, bf16[8,4096]{1,0:T(8,128)(2,1)S(1)}, u32[]{:S(2)}, u32[]{:S(2)}) collective-permute-start(bf16[8,4096]{1,0:T(8,128)(2,1)S(1)} %get-tuple-element.17), channel_id=1, source_target_pairs={{0,8},{1,9},{2,10},{3,11},{4,12},{5,13},{6,14},{7,15},{8,0},{9,1},... | collective-permute-start | bytes 196616 | tf_op jit(solution)/shard_map/ppermute | solution.py:24
  82.8 6.8 %copy-start.2 = (bf16[8,4096]{1,0:T(8,128)(2,1)}, bf16[8,4096]{1,0:T(8,128)(2,1)S(1)}, u32[]{:S(2)}) copy-start(bf16[8,4096]{1,0:T(8,128)(2,1)S(1)} %reduce-precision_convert_fusion.own) | copy-start | bytes 196612
  82.8 6.8 %collective-permute-start.11 = (bf16[8,4096]{1,0:T(8,128)(2,1)S(1)}, bf16[8,4096]{1,0:T(8,128)(2,1)S(1)}, u32[]{:S(2)}, u32[]{:S(2)}) collective-permute-start(bf16[8,4096]{1,0:T(8,128)(2,1)S(1)} %reduce-precision_convert_fusion.own), channel_id=1, source_target_pairs={{0,1},{1,0},{2,3},{3,2},{4,5},{5,4},{6,7},{7,6},{8,9},{9,8},{10,11... | collective-permute-start | bytes 196616 | tf_op jit(solution)/shard_map/ppermute | solution.py:28
  89.6 0.6 copy-start.4
  92.6 18.8 %collective-permute-start.12 = (bf16[8,4224]{1,0:T(8,128)(2,1)}, bf16[8,4224]{1,0:T(8,128)(2,1)S(1)}, u32[]{:S(2)}, u32[]{:S(2)}) collective-permute-start(bf16[8,4224]{1,0:T(8,128)(2,1)} %get-tuple-element.13), channel_id=1, source_target_pairs={{0,32},{1,33},{2,34},{3,35},{4,36},{5,37},{6,38},{7,39},{8,40},{9,... | collective-permute-start | bytes 202760 | tf_op jit(solution)/shard_map/ppermute | solution.py:37
  111.4 54.8 %copy-start.3 = (bf16[8,4224]{1,0:T(8,128)(2,1)}, bf16[8,4224]{1,0:T(8,128)(2,1)S(1)}, u32[]{:S(2)}) copy-start(bf16[8,4224]{1,0:T(8,128)(2,1)S(1)} %collective-permute-done.12.unit) | copy-start | bytes 202756
  112.1 22.1 %collective-permute-start.15 = (bf16[8,4224]{1,0:T(8,128)(2,1)S(1)}, bf16[8,4224]{1,0:T(8,128)(2,1)S(1)}, u32[]{:S(2)}, u32[]{:S(2)}) collective-permute-start(bf16[8,4224]{1,0:T(8,128)(2,1)S(1)} %get-tuple-element.31), channel_id=1, source_target_pairs={{0,16},{1,17},{2,18},{3,19},{4,20},{5,21},{6,22},{7,23},{8,24},{9,... | collective-permute-start | bytes 202760 | tf_op jit(solution)/shard_map/ppermute | solution.py:24
  127.5 11.6 %collective-permute-start.16 = (bf16[8,4224]{1,0:T(8,128)(2,1)S(1)}, bf16[8,4224]{1,0:T(8,128)(2,1)S(1)}, u32[]{:S(2)}, u32[]{:S(2)}) collective-permute-start(bf16[8,4224]{1,0:T(8,128)(2,1)S(1)} %get-tuple-element.31), channel_id=1, source_target_pairs={{0,8},{1,9},{2,10},{3,11},{4,12},{5,13},{6,14},{7,15},{8,0},{9,1},... | collective-permute-start | bytes 202760 | tf_op jit(solution)/shard_map/ppermute | solution.py:24
  130.4 10.7 %collective-permute-start.14 = (bf16[8,4224]{1,0:T(8,128)(2,1)S(1)}, bf16[8,4224]{1,0:T(8,128)(2,1)S(1)}, u32[]{:S(2)}, u32[]{:S(2)}) collective-permute-start(bf16[8,4224]{1,0:T(8,128)(2,1)S(1)} %get-tuple-element.31), channel_id=1, source_target_pairs={{0,4},{1,5},{2,6},{3,7},{4,0},{5,1},{6,2},{7,3},{8,12},{9,13},{10,... | collective-permute-start | bytes 202760 | tf_op jit(solution)/shard_map/ppermute | solution.py:24
  132.3 16.9 %collective-permute-start.13 = (bf16[8,4224]{1,0:T(8,128)(2,1)S(1)}, bf16[8,4224]{1,0:T(8,128)(2,1)S(1)}, u32[]{:S(2)}, u32[]{:S(2)}) collective-permute-start(bf16[8,4224]{1,0:T(8,128)(2,1)S(1)} %get-tuple-element.31), channel_id=1, source_target_pairs={{0,2},{1,3},{2,0},{3,1},{4,6},{5,7},{6,4},{7,5},{8,10},{9,11},{10,... | collective-permute-start | bytes 202760 | tf_op jit(solution)/shard_map/ppermute | solution.py:24
  139.1 25.0 %collective-permute-start.18 = (bf16[16,4224]{1,0:T(8,128)(2,1)S(1)}, bf16[16,4224]{1,0:T(8,128)(2,1)S(1)}, u32[]{:S(2)}, u32[]{:S(2)}) collective-permute-start(bf16[16,4224]{1,0:T(8,128)(2,1)S(1)} %pad_maximum_fusion.4), channel_id=1, source_target_pairs={{0,4},{1,5},{2,6},{3,7},{4,0},{5,1},{6,2},{7,3},{8,12},{9,13},{10,... | collective-permute-start | bytes 405512 | tf_op jit(solution)/shard_map/ppermute | solution.py:24
  141.1 25.0 %collective-permute-start.17 = (bf16[24,4224]{1,0:T(8,128)(2,1)S(1)}, bf16[24,4224]{1,0:T(8,128)(2,1)S(1)}, u32[]{:S(2)}, u32[]{:S(2)}) collective-permute-start(bf16[24,4224]{1,0:T(8,128)(2,1)S(1)} %pad_maximum_fusion), channel_id=1, source_target_pairs={{0,2},{1,3},{2,0},{3,1},{4,6},{5,7},{6,4},{7,5},{8,10},{9,11},{10,... | collective-permute-start | bytes 608264 | tf_op jit(solution)/shard_map/ppermute | solution.py:24
  143.0 9.0 %collective-permute-start.19 = (bf16[8,4224]{1,0:T(8,128)(2,1)S(1)}, bf16[8,4224]{1,0:T(8,128)(2,1)S(1)}, u32[]{:S(2)}, u32[]{:S(2)}) collective-permute-start(bf16[8,4224]{1,0:T(8,128)(2,1)S(1)} %collective-permute-done.15), channel_id=1, source_target_pairs={{0,8},{1,9},{2,10},{3,11},{4,12},{5,13},{6,14},{7,15},{8,0},{9,1},... | collective-permute-start | bytes 202760 | tf_op jit(solution)/shard_map/ppermute | solution.py:24
  152.0 6.3 %collective-permute-start.21 = (bf16[8,4224]{1,0:T(8,128)(2,1)S(1)}, bf16[8,4224]{1,0:T(8,128)(2,1)S(1)}, u32[]{:S(2)}, u32[]{:S(2)}) collective-permute-start(bf16[8,4224]{1,0:T(8,128)(2,1)S(1)} %collective-permute-done.19), channel_id=1, source_target_pairs={{0,4},{1,5},{2,6},{3,7},{4,0},{5,1},{6,2},{7,3},{8,12},{9,13},{10,... | collective-permute-start | bytes 202760 | tf_op jit(solution)/shard_map/ppermute | solution.py:24
  156.4 21.4 %copy-start.5 = (bf16[8,4096]{1,0:T(8,128)(2,1)S(1)}, bf16[8,4096]{1,0:T(8,128)(2,1)}, u32[]{:S(2)}) copy-start(bf16[8,4096]{1,0:T(8,128)(2,1)} %copy-done.4) | copy-start | bytes 196612
  158.3 12.4 %collective-permute-start.22 = (bf16[8,4224]{1,0:T(8,128)(2,1)S(1)}, bf16[8,4224]{1,0:T(8,128)(2,1)S(1)}, u32[]{:S(2)}, u32[]{:S(2)}) collective-permute-start(bf16[8,4224]{1,0:T(8,128)(2,1)S(1)} %collective-permute-done.21), channel_id=1, source_target_pairs={{0,2},{1,3},{2,0},{3,1},{4,6},{5,7},{6,4},{7,5},{8,10},{9,11},{10,... | collective-permute-start | bytes 202760 | tf_op jit(solution)/shard_map/ppermute | solution.py:24
  164.2 6.5 %collective-permute-start.20 = (bf16[24,4224]{1,0:T(8,128)(2,1)S(1)}, bf16[24,4224]{1,0:T(8,128)(2,1)S(1)}, u32[]{:S(2)}, u32[]{:S(2)}) collective-permute-start(bf16[24,4224]{1,0:T(8,128)(2,1)S(1)} %pad_maximum_fusion.1), channel_id=1, source_target_pairs={{0,2},{1,3},{2,0},{3,1},{4,6},{5,7},{6,4},{7,5},{8,10},{9,11},{10,... | collective-permute-start | bytes 608264 | tf_op jit(solution)/shard_map/ppermute | solution.py:24
  170.8 7.7 %copy-start = (bf16[128,4224]{1,0:T(8,128)(2,1)}, bf16[128,4224]{1,0:T(8,128)(2,1)S(1)}, u32[]{:S(2)}) copy-start(bf16[128,4224]{1,0:T(8,128)(2,1)S(1)} %constant_dynamic-update-slice_fusion.a.tail) | copy-start | bytes 3244036
  170.8 11.4 %collective-permute-start.23 = (bf16[128,4224]{1,0:T(8,128)(2,1)S(1)}, bf16[128,4224]{1,0:T(8,128)(2,1)S(1)}, u32[]{:S(2)}, u32[]{:S(2)}) collective-permute-start(bf16[128,4224]{1,0:T(8,128)(2,1)S(1)} %constant_dynamic-update-slice_fusion.a.tail), channel_id=1, source_target_pairs={{0,1},{1,0},{2,3},{3,2},{4,5},{5,4},{6,7},{7,6},{8,9},{9,8},{10,11... | collective-permute-start | bytes 3244040 | tf_op jit(solution)/shard_map/ppermute | solution.py:28
  182.2 1.0 copy-start.1
where the time goes:
time: 188 us; the launch traced here: 187 us
  starting transfers between devices  105 us (56%)
  waiting for transfers between devices  51.8 us (28%)
  Pallas kernels  17.5 us (9%)
  other arithmetic  8.6 us (5%)
  local copies, waits for them, and re-layouts  2.45 us (1%)
    ppermute x20, starting transfers between devices, across(): return lax.ppermute(x, 'tp', [(i, i ^ 2 * d) for i in range(TP)])  74.8 us
    ppermute x20, waiting for transfers between devices, across(): return lax.ppermute(x, 'tp', [(i, i ^ 2 * d) for i in range(TP)])  34.9 us
    ppermute x3, starting transfers between devices, other_core(): return lax.ppermute(x, 'tp', [(i, i ^ 1) for i in range(TP)])  28.4 us
    ppermute x1, waiting for transfers between devices, next_section(): return lax.ppermute(x, ('section', 'tp'), pairs)  16.9 us
    pallas_call x2, Pallas kernels, out_proj(): pl.pallas_call(out_proj_body, out_shape=jax.ShapeDtypeStruct((TOK, HALF),...  7.3 us
    pallas_call x1, Pallas kernels, second_half(): pl.pallas_call(second_half_body, out_shape=(jax.ShapeDtypeStruct((n, TOK)...  4.07 us
  transfers between devices with their start and end apart: 24, of which 10 were waited for; matrix products, arithmetic and copies ran while one was open for 3% of the time, Pallas kernels for 4%

commit v1 on v0

--- a/solution.py
+++ b/solution.py
@@ -78,6 +78,7 @@
             out_specs=pl.BlockSpec((TOK, N_TILE), lambda i, ids: (0, i)),
             scratch_shapes=[pltpu.VMEM((TOK, 256), bf16)],
         ),
+        compiler_params=pltpu.CompilerParams(vmem_limit_bytes=16 << 20),
         name="out_proj",
     )(ids, heads, weight, resid)
 
@@ -109,52 +110,71 @@
             num_scalar_prefetch=1,
             grid=(1,),
             in_specs=[
-                pl.BlockSpec((ROWS, HALF), lambda i, ids: (0, 0)),
-                pl.BlockSpec((ROWS, HALF), lambda i, ids: (0, 0)),
+                pl.BlockSpec(memory_space=pltpu.VMEM),
+                pl.BlockSpec(memory_space=pltpu.VMEM),
                 pl.BlockSpec((1, HALF), lambda i, ids: (0, ids[1])),
                 pl.BlockSpec(memory_space=pltpu.SMEM),
             ],
-            out_specs=[
-                pl.BlockSpec((ROWS, HALF + TAIL), lambda i, ids: (0, 0)),
-                pl.BlockSpec((ROWS, TAIL), lambda i, ids: (0, 0)),
-            ],
+            out_specs=[pl.BlockSpec(memory_space=pltpu.VMEM), pl.BlockSpec(memory_space=pltpu.VMEM)],
         ),
+        compiler_params=pltpu.CompilerParams(vmem_limit_bytes=8 << 20),
         name="cast",
     )(ids, own, twin, gain.reshape(1, D), prior_peak)
 
 
+def on_chip(x):
+    return pltpu.with_memory_space_constraint(x, pltpu.VMEM)
+
+
+def prefetch_body(source, target, sem):
+    copy = pltpu.make_async_copy(source, target, sem)
+    copy.start()
+    copy.wait()
+
+
+def prefetch(weight):
+    return pl.pallas_call(
+        prefetch_body,
+        out_shape=jax.ShapeDtypeStruct(weight.shape, weight.dtype),
+        in_specs=[pl.BlockSpec(memory_space=pltpu.HBM)],
+        out_specs=pl.BlockSpec(memory_space=pltpu.VMEM),
+        scratch_shapes=[pltpu.SemaphoreType.DMA],
+        compiler_params=pltpu.CompilerParams(vmem_limit_bytes=8 << 20),
+        name="prefetch",
+    )(pltpu.with_memory_space_constraint(weight, pltpu.HBM))
+
+
 K_TILE = 2048
+NT_DIMS = (((1,), (1,)), ((), ()))
+
+
+def half_product(weight, a, half):
+    total = None
+    for i in range(HALF // K_TILE):
+        at = pl.multiple_of(half * HALF + i * K_TILE, K_TILE)
+        tile = a[:, i * K_TILE : (i + 1) * K_TILE]
+        part = lax.dot_general(weight[:, pl.ds(at, K_TILE)], tile, NT_DIMS, preferred_element_type=f32)
+        total = part if total is None else total + part
+    return total
 
 
 def first_half_body(ids, weight, a, out):
-    part = lax.dot_general(weight[...], a[...], (((1,), (1,)), ((), ())), preferred_element_type=f32)
-
-    @pl.when(pl.program_id(0) == 0)
-    def _():
-        out[...] = part
-
-    @pl.when(pl.program_id(0) > 0)
-    def _():
-        out[...] += part
+    out[...] = half_product(weight, a, ids[1])
 
 
 def first_half(ids, weight, a):
-    steps = HALF // K_TILE
-    n = weight.shape[0]
     return pl.pallas_call(
         first_half_body,
-        out_shape=jax.ShapeDtypeStruct((n, TOK), f32),
-        grid_spec=pltpu.PrefetchScalarGridSpec(
-            num_scalar_prefetch=1,
-            grid=(steps,),
-            in_specs=[
-                pl.BlockSpec((n, K_TILE), lambda i, ids: (0, ids[1] * steps + i)),
-                pl.BlockSpec((TOK, K_TILE), lambda i, ids: (0, i)),
-            ],
-            out_specs=pl.BlockSpec((n, TOK), lambda i, ids: (0, 0)),
-        ),
+        out_shape=jax.ShapeDtypeStruct((weight.shape[0], TOK), f32),
+        in_specs=[
+            pl.BlockSpec(memory_space=pltpu.SMEM),
+            pl.BlockSpec(memory_space=pltpu.VMEM),
+            pl.BlockSpec(memory_space=pltpu.VMEM),
+        ],
+        out_specs=pl.BlockSpec(memory_space=pltpu.VMEM),
+        compiler_params=pltpu.CompilerParams(vmem_limit_bytes=16 << 20),
         name="first_half",
-    )(ids, weight, a)
+    )(ids, on_chip(weight), a)
 
 
 def both_parts(tail):
@@ -162,51 +182,25 @@
     return wide[:, 0:1] + wide[:, 1:2]
 
 
-def second_half_body(ids, weight, a, start, unit, tail, tail_twin, out, peak, acc):
-    i = pl.program_id(0)
-    part = lax.dot_general(weight[...], a[...], (((1,), (1,)), ((), ())), preferred_element_type=f32)
-
-    @pl.when(i == 0)
-    def _():
-        acc[...] = start[...] + part
-
-    @pl.when(i > 0)
-    def _():
-        acc[...] += part
-
-    @pl.when(i == pl.num_programs(0) - 1)
-    def _():
-        scaled = (acc[...] * unit[0:1, 0:1].astype(f32)).astype(bf16)
-        out[...] = jnp.dot(scaled, shuffle(ids[3]), preferred_element_type=f32).astype(bf16)
-        ends = jnp.maximum(both_parts(tail[...]), both_parts(tail_twin[...]))
-        peak[0] = jnp.max(ends)
-
-
-def second_half(ids, weight, a, start, unit, twin):
-    steps = HALF // K_TILE
-    n = weight.shape[0]
+def second_half_body(ids, weight, a, start, arrived, twin, out, peak):
+    total = start[...] + half_product(weight, a, ids[2])
+    scaled = (total * arrived[0:1, HALF : HALF + 1].astype(f32)).astype(bf16)
+    out[...] = jnp.dot(scaled, shuffle(ids[3]), preferred_element_type=f32).astype(bf16)
+    peak[0] = jnp.max(jnp.maximum(both_parts(a[:, HALF:]), both_parts(twin[:, HALF:])))
+
+
+def second_half(ids, weight, a, start, arrived, twin):
     return pl.pallas_call(
         second_half_body,
-        out_shape=(jax.ShapeDtypeStruct((n, TOK), bf16), jax.ShapeDtypeStruct((1,), f32)),
-        grid_spec=pltpu.PrefetchScalarGridSpec(
-            num_scalar_prefetch=1,
-            grid=(steps,),
-            in_specs=[
-                pl.BlockSpec((n, K_TILE), lambda i, ids: (0, ids[2] * steps + i)),
-                pl.BlockSpec((TOK, K_TILE), lambda i, ids: (0, i)),
-                pl.BlockSpec((n, TOK), lambda i, ids: (0, 0)),
-                pl.BlockSpec((ROWS, TAIL), lambda i, ids: (0, HALF // TAIL)),
-                pl.BlockSpec((TOK, TAIL), lambda i, ids: (0, HALF // TAIL)),
-                pl.BlockSpec((TOK, TAIL), lambda i, ids: (0, HALF // TAIL)),
-            ],
-            out_specs=[
-                pl.BlockSpec((n, TOK), lambda i, ids: (0, 0)),
-                pl.BlockSpec(memory_space=pltpu.SMEM),
-            ],
-            scratch_shapes=[pltpu.VMEM((n, TOK), f32)],
-        ),
+        out_shape=(jax.ShapeDtypeStruct((weight.shape[0], TOK), bf16), jax.ShapeDtypeStruct((1,), f32)),
+        in_specs=[pl.BlockSpec(memory_space=pltpu.SMEM)] + [pl.BlockSpec(memory_space=pltpu.VMEM)] * 5,
+        out_specs=[
+            pl.BlockSpec(memory_space=pltpu.VMEM),
+            pl.BlockSpec(memory_space=pltpu.SMEM),
+        ],
+        compiler_params=pltpu.CompilerParams(vmem_limit_bytes=16 << 20),
         name="second_half",
-    )(ids, weight, a, start, unit, twin, a)
+    )(ids, on_chip(weight), a, start, arrived, twin)
 
 
 def cat(*blocks):
@@ -217,33 +211,47 @@
     return [x[k * ROWS : (k + 1) * ROWS] for k in range(x.shape[0] // ROWS)]
 
 
+def apart(first, *rest):
+    return lax.optimization_barrier((first, *rest))
+
+
+def packed(*blocks):
+    return cat(*[b.astype(bf16) for b in blocks])
+
+
+def unpacked(x):
+    return [g.astype(f32) for g in split(x)]
+
+
 def reduce_rounds(kept, incoming):
-    def send(d, *which):
-        got = across(cat(*[p[o].astype(bf16) for o in which]), d)
-        return [g.astype(f32) for g in split(got)]
-
-    last = slice(15 * ROWS, 16 * ROWS)
-    first_out = (kept[last] + incoming[last].astype(f32)).astype(bf16)
-    first_out, kept, incoming = lax.optimization_barrier((first_out, kept, incoming))
-    p = [k + i.astype(f32) for k, i in zip(split(kept), split(incoming))]
-    a = across(first_out, 1).astype(f32)
-    b13, b11, b7 = send(1, 13, 11, 7)
-    p[14] = p[14] + a
-    (b14,) = send(2, 14)
-    c9, c5, c3 = send(1, 9, 5, 3)
-    p[10] = p[10] + b11
-    p[6] = p[6] + b7
-    c10, c6 = send(2, 10, 6)
-    p[12] = p[12] + b13 + b14
-    (c12,) = send(4, 12)
-    p[4] = p[4] + c5 + c6
-    p[2] = p[2] + c3
-    (d4,) = send(4, 4)
-    (d2,) = send(2, 2)
-    (d1,) = send(1, 1)
-    p[8] = p[8] + c9 + c10 + c12
-    (d8,) = send(8, 8)
-    return p[0] + d1 + d2 + d4 + d8
+    def block(o):
+        rows = slice(o * ROWS, (o + 1) * ROWS)
+        return kept[rows] + incoming[rows].astype(f32)
+
+    out15, kept, incoming = apart(block(15).astype(bf16), kept, incoming)
+    a15 = across(out15, 1)
+    out13, kept, incoming = apart(packed(block(13), block(11), block(7)), kept, incoming)
+    a13 = across(out13, 1)
+    out9, kept, incoming = apart(packed(block(9), block(5), block(3)), kept, incoming)
+    a9 = across(out9, 1)
+    out14, kept, incoming = apart(packed(block(14) + a15.astype(f32)), kept, incoming)
+    a14 = across(out14, 2)
+    b13, b11, b7 = unpacked(a13)
+    out12, b11, b7, kept, incoming = apart(packed(block(12) + b13 + a14.astype(f32)), b11, b7, kept, incoming)
+    a12 = across(out12, 4)
+    out10, kept, incoming = apart(packed(block(10) + b11, block(6) + b7), kept, incoming)
+    a10 = across(out10, 2)
+    c9, c5, c3 = unpacked(a9)
+    out2, out1, c9, c5, kept, incoming = apart(
+        packed(block(2) + c3), packed(block(1)), c9, c5, kept, incoming
+    )
+    a2 = across(out2, 2)
+    a1 = across(out1, 1)
+    c10, c6 = unpacked(a10)
+    out8, c5, c6, kept, incoming = apart(packed(block(8) + c9 + c10 + a12.astype(f32)), c5, c6, kept, incoming)
+    a8 = across(out8, 8)
+    a4 = across(packed(block(4) + c5 + c6), 4)
+    return block(0) + a1.astype(f32) + a2.astype(f32) + a4.astype(f32) + a8.astype(f32)
 
 
 def gather_rounds(own):
@@ -251,7 +259,8 @@
     for d in (8, 4, 2, 1):
         b[d] = across(own, d)
     b[12] = across(b[8], 4)
-    b[10], b[6] = split(across(cat(b[8], b[4]), 2))
+    two = cat(b[8], b[4])
+    b[10], b[6] = split(across(two, 2))
     b[9], b[5], b[3] = split(across(cat(b[8], b[4], b[2]), 1))
     b[14] = across(b[12], 2)
     b[13], b[11], b[7] = split(across(cat(b[12], b[10], b[6]), 1))
@@ -269,6 +278,8 @@
     label = z ^ jnp.where(section % 4 == 0, 8, 0)
     ids = jnp.stack([z, core, 1 - core, label]).astype(jnp.int32)
 
+    weight = prefetch(qkv_weight.T)
+    heads, resid, out_weight = [pltpu.with_memory_space_constraint(v, pltpu.HBM) for v in (heads, resid, out_weight)]
     outgoing = out_proj(ids, 2, heads, out_weight, resid, bf16)
     incoming = other_core(outgoing)
     kept = out_proj(ids, 1, heads, out_weight, resid, f32)
@@ -281,7 +292,6 @@
     mine = gather_rounds(payload)
     theirs = other_core(mine)
 
-    weight = qkv_weight.T
     started = first_half(ids, weight, mine)
     columns, group_peak = second_half(ids, weight, theirs, started, arrived, mine)
     projected = columns.T

time: 188 us -> 175 us (0.931)
  other arithmetic: 8.6 us -> 1.32 us
  waiting for transfers between devices: 51.8 us -> 57.9 us
  Pallas kernels: 17.5 us -> 11.9 us
  starting transfers between devices: 105 us -> 101 us
  local copies, waits for them, and re-layouts: 2.45 us -> 0.22 us
    ppermute x20, waiting for transfers between devices: 34.9 us -> 43.5 us  [across(): return lax.ppermute(x, 'tp', [(i, i ^ 2 * d) for i in range(TP)])]
    ppermute x3, starting transfers between devices: 28.4 us -> 24.1 us  [other_core(): return lax.ppermute(x, 'tp', [(i, i ^ 1) for i in range(TP)])]
    convert_element_type x4 -> x12, other arithmetic: 4.54 us -> 0.35 us  [the longest x8 0.28 us: packed(): return cat(*[b.astype(bf16) for b in blocks])]
    ppermute x1, waiting for transfers between devices: 16.9 us -> 13.9 us  [next_section(): return lax.ppermute(x, ('section', 'tp'), pairs)]
    pallas_call x2 -> x3, Pallas kernels: 7.81 us -> 5.77 us  [the longest x1 2.35 us: prefetch(): pl.pallas_call(prefetch_body, out_shape=jax.ShapeDtypeStruct(weight.shape...]
    pallas_call x2, Pallas kernels: 7.3 us -> 5.4 us  [out_proj(): pl.pallas_call(out_proj_body, out_shape=jax.ShapeDtypeStruct((TOK, HALF),...]
  transfers between devices with their start and end apart: 24 -> 24, of which waited for: 10 -> 11; matrix products, arithmetic and copies ran while one was open for 3% -> 1% of each run, Pallas kernels for 4% -> 4%
where the time goes in v1:
time: 175 us; the launch traced here: 174 us
  starting transfers between devices  101 us (58%)
  waiting for transfers between devices  57.9 us (33%)
  Pallas kernels  11.9 us (7%)
  between operations  1.84 us (1%)
    ppermute x20, starting transfers between devices, across(): return lax.ppermute(x, 'tp', [(i, i ^ 2 * d) for i in range(TP)])  74.7 us
    ppermute x20, waiting for transfers between devices, across(): return lax.ppermute(x, 'tp', [(i, i ^ 2 * d) for i in range(TP)])  43.5 us
    ppermute x3, starting transfers between devices, other_core(): return lax.ppermute(x, 'tp', [(i, i ^ 1) for i in range(TP)])  24.1 us
    ppermute x1, waiting for transfers between devices, next_section(): return lax.ppermute(x, ('section', 'tp'), pairs)  13.9 us
    pallas_call x2, Pallas kernels, out_proj(): pl.pallas_call(out_proj_body, out_shape=jax.ShapeDtypeStruct((TOK, HALF),...  5.4 us
  transfers between devices with their start and end apart: 24, of which 11 were waited for; matrix products, arithmetic and copies ran while one was open for 1% of the time, Pallas kernels for 4%

profile of v1, /device:TPU:1, one launch (start us, length us, event | category | flops | bytes accessed | tf_op | source)
XLA Modules:
  0.0 173.9 jit_solution(17648560216436914280)
XLA Ops:
  0.7 0.1 pad_add_fusion.ids
  0.7 2.7 %out_proj.3 = bf16[128,4096]{1,0:T(8,128)(2,1)S(1)} custom-call(s32[4]{0:T(128)S(1)} %pad_add_fusion.ids, bf16[128,256]{1,0:T(8,128)(2,1)} %bitcast.15, bf16[256,8192]{1,0:T(8,128)(2,1)} %weight.3, bf16[4,8192]{1,0:T(4,128)(2,1)} %bitcast.17), custom_call_target="tpu_custom_call" | custom-call | tf_op jit(solution)/shard_map/out_proj/pallas_call | solution.py:67
  3.4 16.0 %collective-permute-start = (bf16[128,4096]{1,0:T(8,128)(2,1)S(1)}, bf16[128,4096]{1,0:T(8,128)(2,1)S(1)}, u32[]{:S(2)}, u32[]{:S(2)}) collective-permute-start(bf16[128,4096]{1,0:T(8,128)(2,1)S(1)} %out_proj.3), channel_id=1, source_target_pairs={{0,1},{1,0},{2,3},{3,2},{4,5},{5,4},{6,7},{7,6},{8,9},{9,8},{10,11... | collective-permute-start | bytes 3145736 | tf_op jit(solution)/shard_map/ppermute | solution.py:28
  19.4 2.7 %out_proj.2 = f32[128,4096]{1,0:T(8,128)S(1)} custom-call(s32[4]{0:T(128)S(1)} %pad_add_fusion.ids, bf16[128,256]{1,0:T(8,128)(2,1)} %bitcast.16, bf16[256,8192]{1,0:T(8,128)(2,1)} %weight.3, bf16[4,8192]{1,0:T(4,128)(2,1)} %bitcast.18), custom_call_target="tpu_custom_call" | custom-call | tf_op jit(solution)/shard_map/out_proj/pallas_call | solution.py:67
  22.2 0.0 collective-permute-done
  22.2 1.9 %collective-permute-start.1 = (bf16[8,4096]{1,0:T(8,128)(2,1)S(1)}, bf16[8,4096]{1,0:T(8,128)(2,1)S(1)}, u32[]{:S(2)}, u32[]{:S(2)}) collective-permute-start(bf16[8,4096]{1,0:T(8,128)(2,1)S(1)} %fusion), channel_id=1, source_target_pairs={{0,2},{1,3},{2,0},{3,1},{4,6},{5,7},{6,4},{7,5},{8,10},{9,11},{10,... | collective-permute-start | bytes 196616 | tf_op jit(solution)/shard_map/ppermute | solution.py:24
  24.3 3.4 %collective-permute-start.4 = (bf16[24,4096]{1,0:T(8,128)(2,1)S(1)}, bf16[24,4096]{1,0:T(8,128)(2,1)S(1)}, u32[]{:S(2)}, u32[]{:S(2)}) collective-permute-start(bf16[24,4096]{1,0:T(8,128)(2,1)S(1)} %pad_maximum_fusion.3), channel_id=1, source_target_pairs={{0,2},{1,3},{2,0},{3,1},{4,6},{5,7},{6,4},{7,5},{8,10},{9,11},{10,... | collective-permute-start | bytes 589832 | tf_op jit(solution)/shard_map/ppermute | solution.py:24
  27.7 1.9 %collective-permute-start.2 = (bf16[24,4096]{1,0:T(8,128)(2,1)S(1)}, bf16[24,4096]{1,0:T(8,128)(2,1)S(1)}, u32[]{:S(2)}, u32[]{:S(2)}) collective-permute-start(bf16[24,4096]{1,0:T(8,128)(2,1)S(1)} %pad_maximum_fusion.2), channel_id=1, source_target_pairs={{0,2},{1,3},{2,0},{3,1},{4,6},{5,7},{6,4},{7,5},{8,10},{9,11},{10,... | collective-permute-start | bytes 589832 | tf_op jit(solution)/shard_map/ppermute | solution.py:24
  29.6 0.0 collective-permute-done.1
  29.6 1.9 %collective-permute-start.3 = (bf16[8,4096]{1,0:T(8,128)(2,1)S(1)}, bf16[8,4096]{1,0:T(8,128)(2,1)S(1)}, u32[]{:S(2)}, u32[]{:S(2)}) collective-permute-start(bf16[8,4096]{1,0:T(8,128)(2,1)S(1)} %add_convert_fusion.7), channel_id=1, source_target_pairs={{0,4},{1,5},{2,6},{3,7},{4,0},{5,1},{6,2},{7,3},{8,12},{9,13},{10,... | collective-permute-start | bytes 196616 | tf_op jit(solution)/shard_map/ppermute | solution.py:24
  31.6 6.7 %collective-permute-done.2 = bf16[24,4096]{1,0:T(8,128)(2,1)S(1)} collective-permute-done((bf16[24,4096]{1,0:T(8,128)(2,1)S(1)}, bf16[24,4096]{1,0:T(8,128)(2,1)S(1)}, u32[]{:S(2)}, u32[]{:S(2)}) %collective-permute-start.2) | collective-permute-done | bytes 196640 | tf_op jit(solution)/shard_map/ppermute | solution.py:24
  38.3 0.0 collective-permute-done.3
  38.4 1.9 %collective-permute-start.6 = (bf16[8,4096]{1,0:T(8,128)(2,1)S(1)}, bf16[8,4096]{1,0:T(8,128)(2,1)S(1)}, u32[]{:S(2)}, u32[]{:S(2)}) collective-permute-start(bf16[8,4096]{1,0:T(8,128)(2,1)S(1)} %add_convert_fusion.6), channel_id=1, source_target_pairs={{0,8},{1,9},{2,10},{3,11},{4,12},{5,13},{6,14},{7,15},{8,0},{9,1},... | collective-permute-start | bytes 196616 | tf_op jit(solution)/shard_map/ppermute | solution.py:24
  40.3 3.6 %collective-permute-start.5 = (bf16[16,4096]{1,0:T(8,128)(2,1)S(1)}, bf16[16,4096]{1,0:T(8,128)(2,1)S(1)}, u32[]{:S(2)}, u32[]{:S(2)}) collective-permute-start(bf16[16,4096]{1,0:T(8,128)(2,1)S(1)} %pad_maximum_fusion.5), channel_id=1, source_target_pairs={{0,4},{1,5},{2,6},{3,7},{4,0},{5,1},{6,2},{7,3},{8,12},{9,13},{10,... | collective-permute-start | bytes 393224 | tf_op jit(solution)/shard_map/ppermute | solution.py:24
  44.0 0.0 collective-permute-done.4
  44.0 0.0 copy-start
  44.1 1.9 %collective-permute-start.7 = (bf16[8,4096]{1,0:T(8,128)(2,1)S(1)}, bf16[8,4096]{1,0:T(8,128)(2,1)S(1)}, u32[]{:S(2)}, u32[]{:S(2)}) collective-permute-start(bf16[8,4096]{1,0:T(8,128)(2,1)S(1)} %get-tuple-element.64), channel_id=1, source_target_pairs={{0,2},{1,3},{2,0},{3,1},{4,6},{5,7},{6,4},{7,5},{8,10},{9,11},{10,... | collective-permute-start | bytes 196616 | tf_op jit(solution)/shard_map/ppermute | solution.py:24
  46.0 2.5 %collective-permute-start.8 = (bf16[8,4096]{1,0:T(8,128)(2,1)S(1)}, bf16[8,4096]{1,0:T(8,128)(2,1)S(1)}, u32[]{:S(2)}, u32[]{:S(2)}) collective-permute-start(bf16[8,4096]{1,0:T(8,128)(2,1)S(1)} %get-tuple-element.65), channel_id=1, source_target_pairs={{0,4},{1,5},{2,6},{3,7},{4,0},{5,1},{6,2},{7,3},{8,12},{9,13},{10,... | collective-permute-start | bytes 196616 | tf_op jit(solution)/shard_map/ppermute | solution.py:24
  48.5 5.8 %collective-permute-done.5 = bf16[16,4096]{1,0:T(8,128)(2,1)S(1)} collective-permute-done((bf16[16,4096]{1,0:T(8,128)(2,1)S(1)}, bf16[16,4096]{1,0:T(8,128)(2,1)S(1)}, u32[]{:S(2)}, u32[]{:S(2)}) %collective-permute-start.5) | collective-permute-done | bytes 131104 | tf_op jit(solution)/shard_map/ppermute | solution.py:24
  54.4 0.0 collective-permute-done.6
  54.4 4.0 %collective-permute-start.9 = (bf16[8,4096]{1,0:T(8,128)(2,1)S(1)}, bf16[8,4096]{1,0:T(8,128)(2,1)S(1)}, u32[]{:S(2)}, u32[]{:S(2)}) collective-permute-start(bf16[8,4096]{1,0:T(8,128)(2,1)S(1)} %add_convert_fusion), channel_id=1, source_target_pairs={{0,8},{1,9},{2,10},{3,11},{4,12},{5,13},{6,14},{7,15},{8,0},{9,1},... | collective-permute-start | bytes 196616 | tf_op jit(solution)/shard_map/ppermute | solution.py:24
  58.4 5.9 %collective-permute-start.10 = (bf16[8,4096]{1,0:T(8,128)(2,1)S(1)}, bf16[8,4096]{1,0:T(8,128)(2,1)S(1)}, u32[]{:S(2)}, u32[]{:S(2)}) collective-permute-start(bf16[8,4096]{1,0:T(8,128)(2,1)S(1)} %add_convert_fusion.1), channel_id=1, source_target_pairs={{0,16},{1,17},{2,18},{3,19},{4,20},{5,21},{6,22},{7,23},{8,24},{9,... | collective-permute-start | bytes 196616 | tf_op jit(solution)/shard_map/ppermute | solution.py:24
  64.3 0.0 collective-permute-done.7
  64.3 0.0 collective-permute-done.8
  64.3 1.6 collective-permute-done.9
  65.9 15.7 %collective-permute-done.10 = bf16[8,4096]{1,0:T(8,128)(2,1)S(1)} collective-permute-done((bf16[8,4096]{1,0:T(8,128)(2,1)S(1)}, bf16[8,4096]{1,0:T(8,128)(2,1)S(1)}, u32[]{:S(2)}, u32[]{:S(2)}) %collective-permute-start.10) | collective-permute-done | bytes 65568 | tf_op jit(solution)/shard_map/ppermute | solution.py:24
  81.6 0.1 reduce-precision_convert_fusion.own
  81.7 2.4 %collective-permute-start.11 = (bf16[8,4096]{1,0:T(8,128)(2,1)S(1)}, bf16[8,4096]{1,0:T(8,128)(2,1)S(1)}, u32[]{:S(2)}, u32[]{:S(2)}) collective-permute-start(bf16[8,4096]{1,0:T(8,128)(2,1)S(1)} %reduce-precision_convert_fusion.own), channel_id=1, source_target_pairs={{0,1},{1,0},{2,3},{3,2},{4,5},{5,4},{6,7},{7,6},{8,9},{9,8},{10,11... | collective-permute-start | bytes 196616 | tf_op jit(solution)/shard_map/ppermute | solution.py:28
  84.7 0.0 copy-done
  84.8 0.2 collective-permute-done.11.twin
  84.9 0.8 cast.1
  85.7 1.9 %collective-permute-start.12 = (bf16[8,4224]{1,0:T(8,128)(2,1)S(1)}, bf16[8,4224]{1,0:T(8,128)(2,1)S(1)}, u32[]{:S(2)}, u32[]{:S(2)}) collective-permute-start(bf16[8,4224]{1,0:T(8,128)(2,1)S(1)} %get-tuple-element.69), channel_id=1, source_target_pairs={{0,32},{1,33},{2,34},{3,35},{4,36},{5,37},{6,38},{7,39},{8,40},{9,... | collective-permute-start | bytes 202760 | tf_op jit(solution)/shard_map/ppermute | solution.py:37
  87.6 2.3 %prefetch.1.weight = bf16[288,8192]{1,0:T(8,128)(2,1)S(1)} custom-call(bf16[288,8192]{1,0:T(8,128)(2,1)} %bitcast.14), custom_call_target="tpu_custom_call" | custom-call | tf_op jit(solution)/shard_map/prefetch/pallas_call | solution.py:136
  90.0 13.9 %collective-permute-done.12.arrived = bf16[8,4224]{1,0:T(8,128)(2,1)S(1)} collective-permute-done((bf16[8,4224]{1,0:T(8,128)(2,1)S(1)}, bf16[8,4224]{1,0:T(8,128)(2,1)S(1)}, u32[]{:S(2)}, u32[]{:S(2)}) %collective-permute-start.12) | collective-permute-done | bytes 67616 | tf_op jit(solution)/shard_map/ppermute | solution.py:37
  104.0 15.6 %collective-permute-start.15 = (bf16[8,4224]{1,0:T(8,128)(2,1)S(1)}, bf16[8,4224]{1,0:T(8,128)(2,1)S(1)}, u32[]{:S(2)}, u32[]{:S(2)}) collective-permute-start(bf16[8,4224]{1,0:T(8,128)(2,1)S(1)} %get-tuple-element.87), channel_id=1, source_target_pairs={{0,16},{1,17},{2,18},{3,19},{4,20},{5,21},{6,22},{7,23},{8,24},{9,... | collective-permute-start | bytes 202760 | tf_op jit(solution)/shard_map/ppermute | solution.py:24
  119.6 1.9 %collective-permute-start.16 = (bf16[8,4224]{1,0:T(8,128)(2,1)S(1)}, bf16[8,4224]{1,0:T(8,128)(2,1)S(1)}, u32[]{:S(2)}, u32[]{:S(2)}) collective-permute-start(bf16[8,4224]{1,0:T(8,128)(2,1)S(1)} %get-tuple-element.87), channel_id=1, source_target_pairs={{0,8},{1,9},{2,10},{3,11},{4,12},{5,13},{6,14},{7,15},{8,0},{9,1},... | collective-permute-start | bytes 202760 | tf_op jit(solution)/shard_map/ppermute | solution.py:24
  121.5 1.9 %collective-permute-start.14 = (bf16[8,4224]{1,0:T(8,128)(2,1)S(1)}, bf16[8,4224]{1,0:T(8,128)(2,1)S(1)}, u32[]{:S(2)}, u32[]{:S(2)}) collective-permute-start(bf16[8,4224]{1,0:T(8,128)(2,1)S(1)} %get-tuple-element.87), channel_id=1, source_target_pairs={{0,4},{1,5},{2,6},{3,7},{4,0},{5,1},{6,2},{7,3},{8,12},{9,13},{10,... | collective-permute-start | bytes 202760 | tf_op jit(solution)/shard_map/ppermute | solution.py:24
  123.5 1.9 %collective-permute-start.13 = (bf16[8,4224]{1,0:T(8,128)(2,1)S(1)}, bf16[8,4224]{1,0:T(8,128)(2,1)S(1)}, u32[]{:S(2)}, u32[]{:S(2)}) collective-permute-start(bf16[8,4224]{1,0:T(8,128)(2,1)S(1)} %get-tuple-element.87), channel_id=1, source_target_pairs={{0,2},{1,3},{2,0},{3,1},{4,6},{5,7},{6,4},{7,5},{8,10},{9,11},{10,... | collective-permute-start | bytes 202760 | tf_op jit(solution)/shard_map/ppermute | solution.py:24
  125.4 0.0 collective-permute-done.15
  125.4 4.6 %collective-permute-done.16 = bf16[8,4224]{1,0:T(8,128)(2,1)S(1)} collective-permute-done((bf16[8,4224]{1,0:T(8,128)(2,1)S(1)}, bf16[8,4224]{1,0:T(8,128)(2,1)S(1)}, u32[]{:S(2)}, u32[]{:S(2)}) %collective-permute-start.16) | collective-permute-done | bytes 67616 | tf_op jit(solution)/shard_map/ppermute | solution.py:24
  130.1 1.9 %collective-permute-start.18 = (bf16[16,4224]{1,0:T(8,128)(2,1)S(1)}, bf16[16,4224]{1,0:T(8,128)(2,1)S(1)}, u32[]{:S(2)}, u32[]{:S(2)}) collective-permute-start(bf16[16,4224]{1,0:T(8,128)(2,1)S(1)} %pad_maximum_fusion.4), channel_id=1, source_target_pairs={{0,4},{1,5},{2,6},{3,7},{4,0},{5,1},{6,2},{7,3},{8,12},{9,13},{10,... | collective-permute-start | bytes 405512 | tf_op jit(solution)/shard_map/ppermute | solution.py:24
  132.0 0.0 collective-permute-done.14
  132.0 1.9 %collective-permute-start.17 = (bf16[24,4224]{1,0:T(8,128)(2,1)S(1)}, bf16[24,4224]{1,0:T(8,128)(2,1)S(1)}, u32[]{:S(2)}, u32[]{:S(2)}) collective-permute-start(bf16[24,4224]{1,0:T(8,128)(2,1)S(1)} %pad_maximum_fusion), channel_id=1, source_target_pairs={{0,2},{1,3},{2,0},{3,1},{4,6},{5,7},{6,4},{7,5},{8,10},{9,11},{10,... | collective-permute-start | bytes 608264 | tf_op jit(solution)/shard_map/ppermute | solution.py:24
  133.9 7.1 %collective-permute-start.19 = (bf16[8,4224]{1,0:T(8,128)(2,1)S(1)}, bf16[8,4224]{1,0:T(8,128)(2,1)S(1)}, u32[]{:S(2)}, u32[]{:S(2)}) collective-permute-start(bf16[8,4224]{1,0:T(8,128)(2,1)S(1)} %collective-permute-done.15), channel_id=1, source_target_pairs={{0,8},{1,9},{2,10},{3,11},{4,12},{5,13},{6,14},{7,15},{8,0},{9,1},... | collective-permute-start | bytes 202760 | tf_op jit(solution)/shard_map/ppermute | solution.py:24
  141.1 0.0 collective-permute-done.13
  141.1 1.9 %collective-permute-done.19 = bf16[8,4224]{1,0:T(8,128)(2,1)S(1)} collective-permute-done((bf16[8,4224]{1,0:T(8,128)(2,1)S(1)}, bf16[8,4224]{1,0:T(8,128)(2,1)S(1)}, u32[]{:S(2)}, u32[]{:S(2)}) %collective-permute-start.19) | collective-permute-done | bytes 67616 | tf_op jit(solution)/shard_map/ppermute | solution.py:24
  143.0 4.2 %collective-permute-start.21 = (bf16[8,4224]{1,0:T(8,128)(2,1)S(1)}, bf16[8,4224]{1,0:T(8,128)(2,1)S(1)}, u32[]{:S(2)}, u32[]{:S(2)}) collective-permute-start(bf16[8,4224]{1,0:T(8,128)(2,1)S(1)} %collective-permute-done.19), channel_id=1, source_target_pairs={{0,4},{1,5},{2,6},{3,7},{4,0},{5,1},{6,2},{7,3},{8,12},{9,13},{10,... | collective-permute-start | bytes 202760 | tf_op jit(solution)/shard_map/ppermute | solution.py:24
  147.3 2.6 %collective-permute-done.21 = bf16[8,4224]{1,0:T(8,128)(2,1)S(1)} collective-permute-done((bf16[8,4224]{1,0:T(8,128)(2,1)S(1)}, bf16[8,4224]{1,0:T(8,128)(2,1)S(1)}, u32[]{:S(2)}, u32[]{:S(2)}) %collective-permute-start.21) | collective-permute-done | bytes 67616 | tf_op jit(solution)/shard_map/ppermute | solution.py:24
  149.9 7.2 %collective-permute-start.22 = (bf16[8,4224]{1,0:T(8,128)(2,1)S(1)}, bf16[8,4224]{1,0:T(8,128)(2,1)S(1)}, u32[]{:S(2)}, u32[]{:S(2)}) collective-permute-start(bf16[8,4224]{1,0:T(8,128)(2,1)S(1)} %collective-permute-done.21), channel_id=1, source_target_pairs={{0,2},{1,3},{2,0},{3,1},{4,6},{5,7},{6,4},{7,5},{8,10},{9,11},{10,... | collective-permute-start | bytes 202760 | tf_op jit(solution)/shard_map/ppermute | solution.py:24
  157.1 0.0 collective-permute-done.18
  157.2 1.9 %collective-permute-start.20 = (bf16[24,4224]{1,0:T(8,128)(2,1)S(1)}, bf16[24,4224]{1,0:T(8,128)(2,1)S(1)}, u32[]{:S(2)}, u32[]{:S(2)}) collective-permute-start(bf16[24,4224]{1,0:T(8,128)(2,1)S(1)} %pad_maximum_fusion.1), channel_id=1, source_target_pairs={{0,2},{1,3},{2,0},{3,1},{4,6},{5,7},{6,4},{7,5},{8,10},{9,11},{10,... | collective-permute-start | bytes 608264 | tf_op jit(solution)/shard_map/ppermute | solution.py:24
  159.1 0.0 collective-permute-done.17
  159.2 4.5 %collective-permute-done.20 = bf16[24,4224]{1,0:T(8,128)(2,1)S(1)} collective-permute-done((bf16[24,4224]{1,0:T(8,128)(2,1)S(1)}, bf16[24,4224]{1,0:T(8,128)(2,1)S(1)}, u32[]{:S(2)}, u32[]{:S(2)}) %collective-permute-start.20) | collective-permute-done | bytes 202784 | tf_op jit(solution)/shard_map/ppermute | solution.py:24
  163.8 0.0 collective-permute-done.22
  163.8 5.7 %collective-permute-start.23 = (bf16[128,4224]{1,0:T(8,128)(2,1)S(1)}, bf16[128,4224]{1,0:T(8,128)(2,1)S(1)}, u32[]{:S(2)}, u32[]{:S(2)}) collective-permute-start(bf16[128,4224]{1,0:T(8,128)(2,1)S(1)} %constant_dynamic-update-slice_fusion.a.twin), channel_id=1, source_target_pairs={{0,1},{1,0},{2,3},{3,2},{4,5},{5,4},{6,7},{7,6},{8,9},{9,8},{10,11... | collective-permute-start | bytes 3244040 | tf_op jit(solution)/shard_map/ppermute | solution.py:28
  169.5 0.7 maximum_select_fusion
  170.2 1.3 first_half.1.start
  171.5 0.3 collective-permute-done.23.a
  171.8 2.1 %second_half.1 = (bf16[288,128]{1,0:T(8,128)(2,1)}, f32[1]{0:T(128)}) custom-call(s32[4]{0:T(128)S(1)} %pad_add_fusion.ids, bf16[288,8192]{1,0:T(8,128)(2,1)S(1)} %prefetch.1.weight, bf16[128,4224]{1,0:T(8,128)(2,1)S(1)} %collective-permute-done.23.a, f32[288,128]{1,0:T(8,128)S(1)} %first_half.1.start, bf16[8,4224]{1,0:T(8,128)(2,1)S(1)} %collective-permute-done.12.arrived, ...), custom_call_target="tpu_custom_call" | custom-call | tf_op jit(solution)/shard_map/second_half/pallas_call | solution.py:193
  (38 shorter events, 0.7 us)
Async XLA Ops:
  3.4 18.8 %collective-permute-start = (bf16[128,4096]{1,0:T(8,128)(2,1)S(1)}, bf16[128,4096]{1,0:T(8,128)(2,1)S(1)}, u32[]{:S(2)}, u32[]{:S(2)}) collective-permute-start(bf16[128,4096]{1,0:T(8,128)(2,1)S(1)} %out_proj.3), channel_id=1, source_target_pairs={{0,1},{1,0},{2,3},{3,2},{4,5},{5,4},{6,7},{7,6},{8,9},{9,8},{10,11... | collective-permute-start | bytes 3145736 | tf_op jit(solution)/shard_map/ppermute | solution.py:28
  22.2 7.4 %collective-permute-start.1 = (bf16[8,4096]{1,0:T(8,128)(2,1)S(1)}, bf16[8,4096]{1,0:T(8,128)(2,1)S(1)}, u32[]{:S(2)}, u32[]{:S(2)}) collective-permute-start(bf16[8,4096]{1,0:T(8,128)(2,1)S(1)} %fusion), channel_id=1, source_target_pairs={{0,2},{1,3},{2,0},{3,1},{4,6},{5,7},{6,4},{7,5},{8,10},{9,11},{10,... | collective-permute-start | bytes 196616 | tf_op jit(solution)/shard_map/ppermute | solution.py:24
  24.3 19.7 %collective-permute-start.4 = (bf16[24,4096]{1,0:T(8,128)(2,1)S(1)}, bf16[24,4096]{1,0:T(8,128)(2,1)S(1)}, u32[]{:S(2)}, u32[]{:S(2)}) collective-permute-start(bf16[24,4096]{1,0:T(8,128)(2,1)S(1)} %pad_maximum_fusion.3), channel_id=1, source_target_pairs={{0,2},{1,3},{2,0},{3,1},{4,6},{5,7},{6,4},{7,5},{8,10},{9,11},{10,... | collective-permute-start | bytes 589832 | tf_op jit(solution)/shard_map/ppermute | solution.py:24
  27.7 10.6 %collective-permute-start.2 = (bf16[24,4096]{1,0:T(8,128)(2,1)S(1)}, bf16[24,4096]{1,0:T(8,128)(2,1)S(1)}, u32[]{:S(2)}, u32[]{:S(2)}) collective-permute-start(bf16[24,4096]{1,0:T(8,128)(2,1)S(1)} %pad_maximum_fusion.2), channel_id=1, source_target_pairs={{0,2},{1,3},{2,0},{3,1},{4,6},{5,7},{6,4},{7,5},{8,10},{9,11},{10,... | collective-permute-start | bytes 589832 | tf_op jit(solution)/shard_map/ppermute | solution.py:24
  29.6 8.6 %collective-permute-start.3 = (bf16[8,4096]{1,0:T(8,128)(2,1)S(1)}, bf16[8,4096]{1,0:T(8,128)(2,1)S(1)}, u32[]{:S(2)}, u32[]{:S(2)}) collective-permute-start(bf16[8,4096]{1,0:T(8,128)(2,1)S(1)} %add_convert_fusion.7), channel_id=1, source_target_pairs={{0,4},{1,5},{2,6},{3,7},{4,0},{5,1},{6,2},{7,3},{8,12},{9,13},{10,... | collective-permute-start | bytes 196616 | tf_op jit(solution)/shard_map/ppermute | solution.py:24
  38.4 16.0 %collective-permute-start.6 = (bf16[8,4096]{1,0:T(8,128)(2,1)S(1)}, bf16[8,4096]{1,0:T(8,128)(2,1)S(1)}, u32[]{:S(2)}, u32[]{:S(2)}) collective-permute-start(bf16[8,4096]{1,0:T(8,128)(2,1)S(1)} %add_convert_fusion.6), channel_id=1, source_target_pairs={{0,8},{1,9},{2,10},{3,11},{4,12},{5,13},{6,14},{7,15},{8,0},{9,1},... | collective-permute-start | bytes 196616 | tf_op jit(solution)/shard_map/ppermute | solution.py:24
  40.3 14.0 %collective-permute-start.5 = (bf16[16,4096]{1,0:T(8,128)(2,1)S(1)}, bf16[16,4096]{1,0:T(8,128)(2,1)S(1)}, u32[]{:S(2)}, u32[]{:S(2)}) collective-permute-start(bf16[16,4096]{1,0:T(8,128)(2,1)S(1)} %pad_maximum_fusion.5), channel_id=1, source_target_pairs={{0,4},{1,5},{2,6},{3,7},{4,0},{5,1},{6,2},{7,3},{8,12},{9,13},{10,... | collective-permute-start | bytes 393224 | tf_op jit(solution)/shard_map/ppermute | solution.py:24
  44.0 40.7 %copy-start = (bf16[8192]{0:T(1024)(128)(2,1)S(1)}, bf16[8192]{0:T(1024)(128)(2,1)}, u32[]{:S(2)}) copy-start(bf16[8192]{0:T(1024)(128)(2,1)} %param.9) | copy-start | bytes 49156
  44.1 20.2 %collective-permute-start.7 = (bf16[8,4096]{1,0:T(8,128)(2,1)S(1)}, bf16[8,4096]{1,0:T(8,128)(2,1)S(1)}, u32[]{:S(2)}, u32[]{:S(2)}) collective-permute-start(bf16[8,4096]{1,0:T(8,128)(2,1)S(1)} %get-tuple-element.64), channel_id=1, source_target_pairs={{0,2},{1,3},{2,0},{3,1},{4,6},{5,7},{6,4},{7,5},{8,10},{9,11},{10,... | collective-permute-start | bytes 196616 | tf_op jit(solution)/shard_map/ppermute | solution.py:24
  46.0 18.3 %collective-permute-start.8 = (bf16[8,4096]{1,0:T(8,128)(2,1)S(1)}, bf16[8,4096]{1,0:T(8,128)(2,1)S(1)}, u32[]{:S(2)}, u32[]{:S(2)}) collective-permute-start(bf16[8,4096]{1,0:T(8,128)(2,1)S(1)} %get-tuple-element.65), channel_id=1, source_target_pairs={{0,4},{1,5},{2,6},{3,7},{4,0},{5,1},{6,2},{7,3},{8,12},{9,13},{10,... | collective-permute-start | bytes 196616 | tf_op jit(solution)/shard_map/ppermute | solution.py:24
  54.4 11.5 %collective-permute-start.9 = (bf16[8,4096]{1,0:T(8,128)(2,1)S(1)}, bf16[8,4096]{1,0:T(8,128)(2,1)S(1)}, u32[]{:S(2)}, u32[]{:S(2)}) collective-permute-start(bf16[8,4096]{1,0:T(8,128)(2,1)S(1)} %add_convert_fusion), channel_id=1, source_target_pairs={{0,8},{1,9},{2,10},{3,11},{4,12},{5,13},{6,14},{7,15},{8,0},{9,1},... | collective-permute-start | bytes 196616 | tf_op jit(solution)/shard_map/ppermute | solution.py:24
  58.4 23.2 %collective-permute-start.10 = (bf16[8,4096]{1,0:T(8,128)(2,1)S(1)}, bf16[8,4096]{1,0:T(8,128)(2,1)S(1)}, u32[]{:S(2)}, u32[]{:S(2)}) collective-permute-start(bf16[8,4096]{1,0:T(8,128)(2,1)S(1)} %add_convert_fusion.1), channel_id=1, source_target_pairs={{0,16},{1,17},{2,18},{3,19},{4,20},{5,21},{6,22},{7,23},{8,24},{9,... | collective-permute-start | bytes 196616 | tf_op jit(solution)/shard_map/ppermute | solution.py:24
  81.7 3.3 %collective-permute-start.11 = (bf16[8,4096]{1,0:T(8,128)(2,1)S(1)}, bf16[8,4096]{1,0:T(8,128)(2,1)S(1)}, u32[]{:S(2)}, u32[]{:S(2)}) collective-permute-start(bf16[8,4096]{1,0:T(8,128)(2,1)S(1)} %reduce-precision_convert_fusion.own), channel_id=1, source_target_pairs={{0,1},{1,0},{2,3},{3,2},{4,5},{5,4},{6,7},{7,6},{8,9},{9,8},{10,11... | collective-permute-start | bytes 196616 | tf_op jit(solution)/shard_map/ppermute | solution.py:28
  85.7 18.2 %collective-permute-start.12 = (bf16[8,4224]{1,0:T(8,128)(2,1)S(1)}, bf16[8,4224]{1,0:T(8,128)(2,1)S(1)}, u32[]{:S(2)}, u32[]{:S(2)}) collective-permute-start(bf16[8,4224]{1,0:T(8,128)(2,1)S(1)} %get-tuple-element.69), channel_id=1, source_target_pairs={{0,32},{1,33},{2,34},{3,35},{4,36},{5,37},{6,38},{7,39},{8,40},{9,... | collective-permute-start | bytes 202760 | tf_op jit(solution)/shard_map/ppermute | solution.py:37
  104.0 21.4 %collective-permute-start.15 = (bf16[8,4224]{1,0:T(8,128)(2,1)S(1)}, bf16[8,4224]{1,0:T(8,128)(2,1)S(1)}, u32[]{:S(2)}, u32[]{:S(2)}) collective-permute-start(bf16[8,4224]{1,0:T(8,128)(2,1)S(1)} %get-tuple-element.87), channel_id=1, source_target_pairs={{0,16},{1,17},{2,18},{3,19},{4,20},{5,21},{6,22},{7,23},{8,24},{9,... | collective-permute-start | bytes 202760 | tf_op jit(solution)/shard_map/ppermute | solution.py:24
  119.6 10.5 %collective-permute-start.16 = (bf16[8,4224]{1,0:T(8,128)(2,1)S(1)}, bf16[8,4224]{1,0:T(8,128)(2,1)S(1)}, u32[]{:S(2)}, u32[]{:S(2)}) collective-permute-start(bf16[8,4224]{1,0:T(8,128)(2,1)S(1)} %get-tuple-element.87), channel_id=1, source_target_pairs={{0,8},{1,9},{2,10},{3,11},{4,12},{5,13},{6,14},{7,15},{8,0},{9,1},... | collective-permute-start | bytes 202760 | tf_op jit(solution)/shard_map/ppermute | solution.py:24
  121.5 10.5 %collective-permute-start.14 = (bf16[8,4224]{1,0:T(8,128)(2,1)S(1)}, bf16[8,4224]{1,0:T(8,128)(2,1)S(1)}, u32[]{:S(2)}, u32[]{:S(2)}) collective-permute-start(bf16[8,4224]{1,0:T(8,128)(2,1)S(1)} %get-tuple-element.87), channel_id=1, source_target_pairs={{0,4},{1,5},{2,6},{3,7},{4,0},{5,1},{6,2},{7,3},{8,12},{9,13},{10,... | collective-permute-start | bytes 202760 | tf_op jit(solution)/shard_map/ppermute | solution.py:24
  123.5 17.6 %collective-permute-start.13 = (bf16[8,4224]{1,0:T(8,128)(2,1)S(1)}, bf16[8,4224]{1,0:T(8,128)(2,1)S(1)}, u32[]{:S(2)}, u32[]{:S(2)}) collective-permute-start(bf16[8,4224]{1,0:T(8,128)(2,1)S(1)} %get-tuple-element.87), channel_id=1, source_target_pairs={{0,2},{1,3},{2,0},{3,1},{4,6},{5,7},{6,4},{7,5},{8,10},{9,11},{10,... | collective-permute-start | bytes 202760 | tf_op jit(solution)/shard_map/ppermute | solution.py:24
  130.1 27.1 %collective-permute-start.18 = (bf16[16,4224]{1,0:T(8,128)(2,1)S(1)}, bf16[16,4224]{1,0:T(8,128)(2,1)S(1)}, u32[]{:S(2)}, u32[]{:S(2)}) collective-permute-start(bf16[16,4224]{1,0:T(8,128)(2,1)S(1)} %pad_maximum_fusion.4), channel_id=1, source_target_pairs={{0,4},{1,5},{2,6},{3,7},{4,0},{5,1},{6,2},{7,3},{8,12},{9,13},{10,... | collective-permute-start | bytes 405512 | tf_op jit(solution)/shard_map/ppermute | solution.py:24
  132.0 27.1 %collective-permute-start.17 = (bf16[24,4224]{1,0:T(8,128)(2,1)S(1)}, bf16[24,4224]{1,0:T(8,128)(2,1)S(1)}, u32[]{:S(2)}, u32[]{:S(2)}) collective-permute-start(bf16[24,4224]{1,0:T(8,128)(2,1)S(1)} %pad_maximum_fusion), channel_id=1, source_target_pairs={{0,2},{1,3},{2,0},{3,1},{4,6},{5,7},{6,4},{7,5},{8,10},{9,11},{10,... | collective-permute-start | bytes 608264 | tf_op jit(solution)/shard_map/ppermute | solution.py:24
  133.9 9.0 %collective-permute-start.19 = (bf16[8,4224]{1,0:T(8,128)(2,1)S(1)}, bf16[8,4224]{1,0:T(8,128)(2,1)S(1)}, u32[]{:S(2)}, u32[]{:S(2)}) collective-permute-start(bf16[8,4224]{1,0:T(8,128)(2,1)S(1)} %collective-permute-done.15), channel_id=1, source_target_pairs={{0,8},{1,9},{2,10},{3,11},{4,12},{5,13},{6,14},{7,15},{8,0},{9,1},... | collective-permute-start | bytes 202760 | tf_op jit(solution)/shard_map/ppermute | solution.py:24
  143.0 6.9 %collective-permute-start.21 = (bf16[8,4224]{1,0:T(8,128)(2,1)S(1)}, bf16[8,4224]{1,0:T(8,128)(2,1)S(1)}, u32[]{:S(2)}, u32[]{:S(2)}) collective-permute-start(bf16[8,4224]{1,0:T(8,128)(2,1)S(1)} %collective-permute-done.19), channel_id=1, source_target_pairs={{0,4},{1,5},{2,6},{3,7},{4,0},{5,1},{6,2},{7,3},{8,12},{9,13},{10,... | collective-permute-start | bytes 202760 | tf_op jit(solution)/shard_map/ppermute | solution.py:24
  149.9 13.9 %collective-permute-start.22 = (bf16[8,4224]{1,0:T(8,128)(2,1)S(1)}, bf16[8,4224]{1,0:T(8,128)(2,1)S(1)}, u32[]{:S(2)}, u32[]{:S(2)}) collective-permute-start(bf16[8,4224]{1,0:T(8,128)(2,1)S(1)} %collective-permute-done.21), channel_id=1, source_target_pairs={{0,2},{1,3},{2,0},{3,1},{4,6},{5,7},{6,4},{7,5},{8,10},{9,11},{10,... | collective-permute-start | bytes 202760 | tf_op jit(solution)/shard_map/ppermute | solution.py:24
  157.2 6.5 %collective-permute-start.20 = (bf16[24,4224]{1,0:T(8,128)(2,1)S(1)}, bf16[24,4224]{1,0:T(8,128)(2,1)S(1)}, u32[]{:S(2)}, u32[]{:S(2)}) collective-permute-start(bf16[24,4224]{1,0:T(8,128)(2,1)S(1)} %pad_maximum_fusion.1), channel_id=1, source_target_pairs={{0,2},{1,3},{2,0},{3,1},{4,6},{5,7},{6,4},{7,5},{8,10},{9,11},{10,... | collective-permute-start | bytes 608264 | tf_op jit(solution)/shard_map/ppermute | solution.py:24
  163.8 8.0 %collective-permute-start.23 = (bf16[128,4224]{1,0:T(8,128)(2,1)S(1)}, bf16[128,4224]{1,0:T(8,128)(2,1)S(1)}, u32[]{:S(2)}, u32[]{:S(2)}) collective-permute-start(bf16[128,4224]{1,0:T(8,128)(2,1)S(1)} %constant_dynamic-update-slice_fusion.a.twin), channel_id=1, source_target_pairs={{0,1},{1,0},{2,3},{3,2},{4,5},{5,4},{6,7},{7,6},{8,9},{9,8},{10,11... | collective-permute-start | bytes 3244040 | tf_op jit(solution)/shard_map/ppermute | solution.py:28

commit v2 on v1

--- a/solution.py
+++ b/solution.py
@@ -219,10 +219,6 @@
     return cat(*[b.astype(bf16) for b in blocks])
 
 
-def unpacked(x):
-    return [g.astype(f32) for g in split(x)]
-
-
 def reduce_rounds(kept, incoming):
     def block(o):
         rows = slice(o * ROWS, (o + 1) * ROWS)
@@ -232,25 +228,26 @@
     a15 = across(out15, 1)
     out13, kept, incoming = apart(packed(block(13), block(11), block(7)), kept, incoming)
     a13 = across(out13, 1)
+    out14, kept, incoming = apart(packed(block(14) + a15.astype(f32)), kept, incoming)
+    a14 = across(out14, 2)
+    b13, b11, b7 = split(a13)
+    out12, b11, b7, kept, incoming = apart(
+        packed(block(12) + b13.astype(f32) + a14.astype(f32)), b11, b7, kept, incoming
+    )
+    a12 = across(out12, 4)
+    out10, kept, incoming = apart(packed(block(10) + b11.astype(f32), block(6) + b7.astype(f32)), kept, incoming)
+    a10 = across(out10, 2)
     out9, kept, incoming = apart(packed(block(9), block(5), block(3)), kept, incoming)
     a9 = across(out9, 1)
-    out14, kept, incoming = apart(packed(block(14) + a15.astype(f32)), kept, incoming)
-    a14 = across(out14, 2)
-    b13, b11, b7 = unpacked(a13)
-    out12, b11, b7, kept, incoming = apart(packed(block(12) + b13 + a14.astype(f32)), b11, b7, kept, incoming)
-    a12 = across(out12, 4)
-    out10, kept, incoming = apart(packed(block(10) + b11, block(6) + b7), kept, incoming)
-    a10 = across(out10, 2)
-    c9, c5, c3 = unpacked(a9)
-    out2, out1, c9, c5, kept, incoming = apart(
-        packed(block(2) + c3), packed(block(1)), c9, c5, kept, incoming
+    c9, c5, c3 = split(a9)
+    c10, c6 = split(a10)
+    out8, c5, c3, c6, kept, incoming = apart(
+        packed(block(8) + c9.astype(f32) + c10.astype(f32) + a12.astype(f32)), c5, c3, c6, kept, incoming
     )
-    a2 = across(out2, 2)
-    a1 = across(out1, 1)
-    c10, c6 = unpacked(a10)
-    out8, c5, c6, kept, incoming = apart(packed(block(8) + c9 + c10 + a12.astype(f32)), c5, c6, kept, incoming)
     a8 = across(out8, 8)
-    a4 = across(packed(block(4) + c5 + c6), 4)
+    a4 = across(packed(block(4) + c5.astype(f32) + c6.astype(f32)), 4)
+    a2 = across(packed(block(2) + c3.astype(f32)), 2)
+    a1 = across(packed(block(1)), 1)
     return block(0) + a1.astype(f32) + a2.astype(f32) + a4.astype(f32) + a8.astype(f32)
 
 

time: 175 us -> 178 us (1.017)
  the two profiles are of different devices: /device:TPU:1 before, /device:TPU:6 now
where the time goes in v2:
time: 178 us; the launch traced here: 175 us
  starting transfers between devices  113 us (63%)
  waiting for transfers between devices  46 us (26%)
  Pallas kernels  11.9 us (7%)
  between operations  1.83 us (1%)
    ppermute x20, starting transfers between devices, across(): return lax.ppermute(x, 'tp', [(i, i ^ 2 * d) for i in range(TP)])  104 us
    ppermute x20, waiting for transfers between devices, across(): return lax.ppermute(x, 'tp', [(i, i ^ 2 * d) for i in range(TP)])  32.6 us
    ppermute x1, waiting for transfers between devices, next_section(): return lax.ppermute(x, ('section', 'tp'), pairs)  12.2 us
    ppermute x3, starting transfers between devices, other_core(): return lax.ppermute(x, 'tp', [(i, i ^ 1) for i in range(TP)])  5.76 us
    pallas_call x2, Pallas kernels, out_proj(): pl.pallas_call(out_proj_body, out_shape=jax.ShapeDtypeStruct((TOK, HALF),...  5.4 us
  transfers between devices with their start and end apart: 24, of which 11 were waited for; matrix products, arithmetic and copies ran while one was open for 1% of the time, Pallas kernels for 4%

profile of v2, /device:TPU:6, one launch (start us, length us, event | category | flops | bytes accessed | tf_op | source)
XLA Modules:
  0.0 174.6 jit_solution(15828697934103486183)
XLA Ops:
  0.7 0.1 pad_add_fusion.ids
  0.7 2.7 %out_proj.3 = bf16[128,4096]{1,0:T(8,128)(2,1)S(1)} custom-call(s32[4]{0:T(128)S(1)} %pad_add_fusion.ids, bf16[128,256]{1,0:T(8,128)(2,1)} %bitcast.15, bf16[256,8192]{1,0:T(8,128)(2,1)} %weight.3, bf16[4,8192]{1,0:T(4,128)(2,1)} %bitcast.17), custom_call_target="tpu_custom_call" | custom-call | tf_op jit(solution)/shard_map/out_proj/pallas_call | solution.py:67
  3.4 1.9 %collective-permute-start = (bf16[128,4096]{1,0:T(8,128)(2,1)S(1)}, bf16[128,4096]{1,0:T(8,128)(2,1)S(1)}, u32[]{:S(2)}, u32[]{:S(2)}) collective-permute-start(bf16[128,4096]{1,0:T(8,128)(2,1)S(1)} %out_proj.3), channel_id=1, source_target_pairs={{0,1},{1,0},{2,3},{3,2},{4,5},{5,4},{6,7},{7,6},{8,9},{9,8},{10,11... | collective-permute-start | bytes 3145736 | tf_op jit(solution)/shard_map/ppermute | solution.py:28
  5.3 2.7 %out_proj.2 = f32[128,4096]{1,0:T(8,128)S(1)} custom-call(s32[4]{0:T(128)S(1)} %pad_add_fusion.ids, bf16[128,256]{1,0:T(8,128)(2,1)} %bitcast.16, bf16[256,8192]{1,0:T(8,128)(2,1)} %weight.3, bf16[4,8192]{1,0:T(4,128)(2,1)} %bitcast.18), custom_call_target="tpu_custom_call" | custom-call | tf_op jit(solution)/shard_map/out_proj/pallas_call | solution.py:67
  8.1 0.0 collective-permute-done
  8.1 3.8 %collective-permute-start.1 = (bf16[8,4096]{1,0:T(8,128)(2,1)S(1)}, bf16[8,4096]{1,0:T(8,128)(2,1)S(1)}, u32[]{:S(2)}, u32[]{:S(2)}) collective-permute-start(bf16[8,4096]{1,0:T(8,128)(2,1)S(1)} %fusion), channel_id=1, source_target_pairs={{0,2},{1,3},{2,0},{3,1},{4,6},{5,7},{6,4},{7,5},{8,10},{9,11},{10,... | collective-permute-start | bytes 196616 | tf_op jit(solution)/shard_map/ppermute | solution.py:24
  12.0 2.0 %collective-permute-start.2 = (bf16[24,4096]{1,0:T(8,128)(2,1)S(1)}, bf16[24,4096]{1,0:T(8,128)(2,1)S(1)}, u32[]{:S(2)}, u32[]{:S(2)}) collective-permute-start(bf16[24,4096]{1,0:T(8,128)(2,1)S(1)} %pad_maximum_fusion.2), channel_id=1, source_target_pairs={{0,2},{1,3},{2,0},{3,1},{4,6},{5,7},{6,4},{7,5},{8,10},{9,11},{10,... | collective-permute-start | bytes 589832 | tf_op jit(solution)/shard_map/ppermute | solution.py:24
  14.0 0.7 collective-permute-done.1
  14.7 5.2 %collective-permute-start.3 = (bf16[8,4096]{1,0:T(8,128)(2,1)S(1)}, bf16[8,4096]{1,0:T(8,128)(2,1)S(1)}, u32[]{:S(2)}, u32[]{:S(2)}) collective-permute-start(bf16[8,4096]{1,0:T(8,128)(2,1)S(1)} %add_convert_fusion.10), channel_id=1, source_target_pairs={{0,4},{1,5},{2,6},{3,7},{4,0},{5,1},{6,2},{7,3},{8,12},{9,13},{10,... | collective-permute-start | bytes 196616 | tf_op jit(solution)/shard_map/ppermute | solution.py:24
  19.9 2.4 %collective-permute-done.2 = bf16[24,4096]{1,0:T(8,128)(2,1)S(1)} collective-permute-done((bf16[24,4096]{1,0:T(8,128)(2,1)S(1)}, bf16[24,4096]{1,0:T(8,128)(2,1)S(1)}, u32[]{:S(2)}, u32[]{:S(2)}) %collective-permute-start.2) | collective-permute-done | bytes 196640 | tf_op jit(solution)/shard_map/ppermute | solution.py:24
  22.4 0.0 collective-permute-done.3
  22.6 5.1 %collective-permute-start.4 = (bf16[24,4096]{1,0:T(8,128)(2,1)S(1)}, bf16[24,4096]{1,0:T(8,128)(2,1)S(1)}, u32[]{:S(2)}, u32[]{:S(2)}) collective-permute-start(bf16[24,4096]{1,0:T(8,128)(2,1)S(1)} %pad_maximum_fusion.3), channel_id=1, source_target_pairs={{0,2},{1,3},{2,0},{3,1},{4,6},{5,7},{6,4},{7,5},{8,10},{9,11},{10,... | collective-permute-start | bytes 589832 | tf_op jit(solution)/shard_map/ppermute | solution.py:24
  27.7 3.8 %collective-permute-start.5 = (bf16[16,4096]{1,0:T(8,128)(2,1)S(1)}, bf16[16,4096]{1,0:T(8,128)(2,1)S(1)}, u32[]{:S(2)}, u32[]{:S(2)}) collective-permute-start(bf16[16,4096]{1,0:T(8,128)(2,1)S(1)} %pad_maximum_fusion.5), channel_id=1, source_target_pairs={{0,4},{1,5},{2,6},{3,7},{4,0},{5,1},{6,2},{7,3},{8,12},{9,13},{10,... | collective-permute-start | bytes 393224 | tf_op jit(solution)/shard_map/ppermute | solution.py:24
  31.5 9.1 %collective-permute-start.6 = (bf16[8,4096]{1,0:T(8,128)(2,1)S(1)}, bf16[8,4096]{1,0:T(8,128)(2,1)S(1)}, u32[]{:S(2)}, u32[]{:S(2)}) collective-permute-start(bf16[8,4096]{1,0:T(8,128)(2,1)S(1)} %add_convert_fusion.9), channel_id=1, source_target_pairs={{0,8},{1,9},{2,10},{3,11},{4,12},{5,13},{6,14},{7,15},{8,0},{9,1},... | collective-permute-start | bytes 196616 | tf_op jit(solution)/shard_map/ppermute | solution.py:24
  40.6 0.0 collective-permute-done.5
  40.6 0.0 copy-start
  40.6 0.0 collective-permute-done.4
  40.7 4.5 %collective-permute-done.6 = bf16[8,4096]{1,0:T(8,128)(2,1)S(1)} collective-permute-done((bf16[8,4096]{1,0:T(8,128)(2,1)S(1)}, bf16[8,4096]{1,0:T(8,128)(2,1)S(1)}, u32[]{:S(2)}, u32[]{:S(2)}) %collective-permute-start.6) | collective-permute-done | bytes 65568 | tf_op jit(solution)/shard_map/ppermute | solution.py:24
  45.2 0.1 add_convert_fusion.2
  45.3 1.9 %collective-permute-start.7 = (bf16[8,4096]{1,0:T(8,128)(2,1)S(1)}, bf16[8,4096]{1,0:T(8,128)(2,1)S(1)}, u32[]{:S(2)}, u32[]{:S(2)}) collective-permute-start(bf16[8,4096]{1,0:T(8,128)(2,1)S(1)} %get-tuple-element.63), channel_id=1, source_target_pairs={{0,2},{1,3},{2,0},{3,1},{4,6},{5,7},{6,4},{7,5},{8,10},{9,11},{10,... | collective-permute-start | bytes 196616 | tf_op jit(solution)/shard_map/ppermute | solution.py:24
  47.2 5.9 %collective-permute-start.9 = (bf16[8,4096]{1,0:T(8,128)(2,1)S(1)}, bf16[8,4096]{1,0:T(8,128)(2,1)S(1)}, u32[]{:S(2)}, u32[]{:S(2)}) collective-permute-start(bf16[8,4096]{1,0:T(8,128)(2,1)S(1)} %get-tuple-element.64), channel_id=1, source_target_pairs={{0,8},{1,9},{2,10},{3,11},{4,12},{5,13},{6,14},{7,15},{8,0},{9,1},... | collective-permute-start | bytes 196616 | tf_op jit(solution)/shard_map/ppermute | solution.py:24
  53.1 5.8 %collective-permute-start.8 = (bf16[8,4096]{1,0:T(8,128)(2,1)S(1)}, bf16[8,4096]{1,0:T(8,128)(2,1)S(1)}, u32[]{:S(2)}, u32[]{:S(2)}) collective-permute-start(bf16[8,4096]{1,0:T(8,128)(2,1)S(1)} %get-tuple-element.65), channel_id=1, source_target_pairs={{0,4},{1,5},{2,6},{3,7},{4,0},{5,1},{6,2},{7,3},{8,12},{9,13},{10,... | collective-permute-start | bytes 196616 | tf_op jit(solution)/shard_map/ppermute | solution.py:24
  59.0 15.7 %collective-permute-start.10 = (bf16[8,4096]{1,0:T(8,128)(2,1)S(1)}, bf16[8,4096]{1,0:T(8,128)(2,1)S(1)}, u32[]{:S(2)}, u32[]{:S(2)}) collective-permute-start(bf16[8,4096]{1,0:T(8,128)(2,1)S(1)} %add_convert_fusion.3), channel_id=1, source_target_pairs={{0,16},{1,17},{2,18},{3,19},{4,20},{5,21},{6,22},{7,23},{8,24},{9,... | collective-permute-start | bytes 196616 | tf_op jit(solution)/shard_map/ppermute | solution.py:24
  74.7 0.0 collective-permute-done.7
  74.7 0.0 collective-permute-done.9
  74.7 0.0 collective-permute-done.8
  74.7 7.2 %collective-permute-done.10 = bf16[8,4096]{1,0:T(8,128)(2,1)S(1)} collective-permute-done((bf16[8,4096]{1,0:T(8,128)(2,1)S(1)}, bf16[8,4096]{1,0:T(8,128)(2,1)S(1)}, u32[]{:S(2)}, u32[]{:S(2)}) %collective-permute-start.10) | collective-permute-done | bytes 65568 | tf_op jit(solution)/shard_map/ppermute | solution.py:24
  82.0 0.1 reduce-precision_convert_fusion.own
  82.0 1.9 %collective-permute-start.11 = (bf16[8,4096]{1,0:T(8,128)(2,1)S(1)}, bf16[8,4096]{1,0:T(8,128)(2,1)S(1)}, u32[]{:S(2)}, u32[]{:S(2)}) collective-permute-start(bf16[8,4096]{1,0:T(8,128)(2,1)S(1)} %reduce-precision_convert_fusion.own), channel_id=1, source_target_pairs={{0,1},{1,0},{2,3},{3,2},{4,5},{5,4},{6,7},{7,6},{8,9},{9,8},{10,11... | collective-permute-start | bytes 196616 | tf_op jit(solution)/shard_map/ppermute | solution.py:28
  84.6 0.0 copy-done
  84.6 0.5 collective-permute-done.11.twin
  85.2 0.8 cast.1
  85.9 3.5 %collective-permute-start.12 = (bf16[8,4224]{1,0:T(8,128)(2,1)S(1)}, bf16[8,4224]{1,0:T(8,128)(2,1)S(1)}, u32[]{:S(2)}, u32[]{:S(2)}) collective-permute-start(bf16[8,4224]{1,0:T(8,128)(2,1)S(1)} %get-tuple-element.59), channel_id=1, source_target_pairs={{0,32},{1,33},{2,34},{3,35},{4,36},{5,37},{6,38},{7,39},{8,40},{9,... | collective-permute-start | bytes 202760 | tf_op jit(solution)/shard_map/ppermute | solution.py:37
  89.4 2.3 %prefetch.1.weight = bf16[288,8192]{1,0:T(8,128)(2,1)S(1)} custom-call(bf16[288,8192]{1,0:T(8,128)(2,1)} %bitcast.14), custom_call_target="tpu_custom_call" | custom-call | tf_op jit(solution)/shard_map/prefetch/pallas_call | solution.py:136
  91.8 12.2 %collective-permute-done.12.arrived = bf16[8,4224]{1,0:T(8,128)(2,1)S(1)} collective-permute-done((bf16[8,4224]{1,0:T(8,128)(2,1)S(1)}, bf16[8,4224]{1,0:T(8,128)(2,1)S(1)}, u32[]{:S(2)}, u32[]{:S(2)}) %collective-permute-start.12) | collective-permute-done | bytes 67616 | tf_op jit(solution)/shard_map/ppermute | solution.py:37
  104.0 17.2 %collective-permute-start.15 = (bf16[8,4224]{1,0:T(8,128)(2,1)S(1)}, bf16[8,4224]{1,0:T(8,128)(2,1)S(1)}, u32[]{:S(2)}, u32[]{:S(2)}) collective-permute-start(bf16[8,4224]{1,0:T(8,128)(2,1)S(1)} %get-tuple-element.78), channel_id=1, source_target_pairs={{0,16},{1,17},{2,18},{3,19},{4,20},{5,21},{6,22},{7,23},{8,24},{9,... | collective-permute-start | bytes 202760 | tf_op jit(solution)/shard_map/ppermute | solution.py:24
  121.2 1.9 %collective-permute-start.16 = (bf16[8,4224]{1,0:T(8,128)(2,1)S(1)}, bf16[8,4224]{1,0:T(8,128)(2,1)S(1)}, u32[]{:S(2)}, u32[]{:S(2)}) collective-permute-start(bf16[8,4224]{1,0:T(8,128)(2,1)S(1)} %get-tuple-element.78), channel_id=1, source_target_pairs={{0,8},{1,9},{2,10},{3,11},{4,12},{5,13},{6,14},{7,15},{8,0},{9,1},... | collective-permute-start | bytes 202760 | tf_op jit(solution)/shard_map/ppermute | solution.py:24
  123.2 1.9 %collective-permute-start.14 = (bf16[8,4224]{1,0:T(8,128)(2,1)S(1)}, bf16[8,4224]{1,0:T(8,128)(2,1)S(1)}, u32[]{:S(2)}, u32[]{:S(2)}) collective-permute-start(bf16[8,4224]{1,0:T(8,128)(2,1)S(1)} %get-tuple-element.78), channel_id=1, source_target_pairs={{0,4},{1,5},{2,6},{3,7},{4,0},{5,1},{6,2},{7,3},{8,12},{9,13},{10,... | collective-permute-start | bytes 202760 | tf_op jit(solution)/shard_map/ppermute | solution.py:24
  125.1 3.2 %collective-permute-start.13 = (bf16[8,4224]{1,0:T(8,128)(2,1)S(1)}, bf16[8,4224]{1,0:T(8,128)(2,1)S(1)}, u32[]{:S(2)}, u32[]{:S(2)}) collective-permute-start(bf16[8,4224]{1,0:T(8,128)(2,1)S(1)} %get-tuple-element.78), channel_id=1, source_target_pairs={{0,2},{1,3},{2,0},{3,1},{4,6},{5,7},{6,4},{7,5},{8,10},{9,11},{10,... | collective-permute-start | bytes 202760 | tf_op jit(solution)/shard_map/ppermute | solution.py:24
  128.3 0.0 collective-permute-done.15
  128.3 3.0 %collective-permute-done.16 = bf16[8,4224]{1,0:T(8,128)(2,1)S(1)} collective-permute-done((bf16[8,4224]{1,0:T(8,128)(2,1)S(1)}, bf16[8,4224]{1,0:T(8,128)(2,1)S(1)}, u32[]{:S(2)}, u32[]{:S(2)}) %collective-permute-start.16) | collective-permute-done | bytes 67616 | tf_op jit(solution)/shard_map/ppermute | solution.py:24
  131.3 1.9 %collective-permute-start.18 = (bf16[16,4224]{1,0:T(8,128)(2,1)S(1)}, bf16[16,4224]{1,0:T(8,128)(2,1)S(1)}, u32[]{:S(2)}, u32[]{:S(2)}) collective-permute-start(bf16[16,4224]{1,0:T(8,128)(2,1)S(1)} %pad_maximum_fusion.4), channel_id=1, source_target_pairs={{0,4},{1,5},{2,6},{3,7},{4,0},{5,1},{6,2},{7,3},{8,12},{9,13},{10,... | collective-permute-start | bytes 405512 | tf_op jit(solution)/shard_map/ppermute | solution.py:24
  133.3 0.0 collective-permute-done.14
  133.3 2.6 %collective-permute-start.17 = (bf16[24,4224]{1,0:T(8,128)(2,1)S(1)}, bf16[24,4224]{1,0:T(8,128)(2,1)S(1)}, u32[]{:S(2)}, u32[]{:S(2)}) collective-permute-start(bf16[24,4224]{1,0:T(8,128)(2,1)S(1)} %pad_maximum_fusion), channel_id=1, source_target_pairs={{0,2},{1,3},{2,0},{3,1},{4,6},{5,7},{6,4},{7,5},{8,10},{9,11},{10,... | collective-permute-start | bytes 608264 | tf_op jit(solution)/shard_map/ppermute | solution.py:24
  135.9 7.8 %collective-permute-start.19 = (bf16[8,4224]{1,0:T(8,128)(2,1)S(1)}, bf16[8,4224]{1,0:T(8,128)(2,1)S(1)}, u32[]{:S(2)}, u32[]{:S(2)}) collective-permute-start(bf16[8,4224]{1,0:T(8,128)(2,1)S(1)} %collective-permute-done.15), channel_id=1, source_target_pairs={{0,8},{1,9},{2,10},{3,11},{4,12},{5,13},{6,14},{7,15},{8,0},{9,1},... | collective-permute-start | bytes 202760 | tf_op jit(solution)/shard_map/ppermute | solution.py:24
  143.7 0.0 collective-permute-done.13
  143.8 4.2 %collective-permute-done.19 = bf16[8,4224]{1,0:T(8,128)(2,1)S(1)} collective-permute-done((bf16[8,4224]{1,0:T(8,128)(2,1)S(1)}, bf16[8,4224]{1,0:T(8,128)(2,1)S(1)}, u32[]{:S(2)}, u32[]{:S(2)}) %collective-permute-start.19) | collective-permute-done | bytes 67616 | tf_op jit(solution)/shard_map/ppermute | solution.py:24
  148.0 2.2 %collective-permute-start.21 = (bf16[8,4224]{1,0:T(8,128)(2,1)S(1)}, bf16[8,4224]{1,0:T(8,128)(2,1)S(1)}, u32[]{:S(2)}, u32[]{:S(2)}) collective-permute-start(bf16[8,4224]{1,0:T(8,128)(2,1)S(1)} %collective-permute-done.19), channel_id=1, source_target_pairs={{0,4},{1,5},{2,6},{3,7},{4,0},{5,1},{6,2},{7,3},{8,12},{9,13},{10,... | collective-permute-start | bytes 202760 | tf_op jit(solution)/shard_map/ppermute | solution.py:24
  150.2 4.9 %collective-permute-done.21 = bf16[8,4224]{1,0:T(8,128)(2,1)S(1)} collective-permute-done((bf16[8,4224]{1,0:T(8,128)(2,1)S(1)}, bf16[8,4224]{1,0:T(8,128)(2,1)S(1)}, u32[]{:S(2)}, u32[]{:S(2)}) %collective-permute-start.21) | collective-permute-done | bytes 67616 | tf_op jit(solution)/shard_map/ppermute | solution.py:24
  155.1 5.0 %collective-permute-start.22 = (bf16[8,4224]{1,0:T(8,128)(2,1)S(1)}, bf16[8,4224]{1,0:T(8,128)(2,1)S(1)}, u32[]{:S(2)}, u32[]{:S(2)}) collective-permute-start(bf16[8,4224]{1,0:T(8,128)(2,1)S(1)} %collective-permute-done.21), channel_id=1, source_target_pairs={{0,2},{1,3},{2,0},{3,1},{4,6},{5,7},{6,4},{7,5},{8,10},{9,11},{10,... | collective-permute-start | bytes 202760 | tf_op jit(solution)/shard_map/ppermute | solution.py:24
  160.0 0.0 collective-permute-done.18
  160.1 1.9 %collective-permute-start.20 = (bf16[24,4224]{1,0:T(8,128)(2,1)S(1)}, bf16[24,4224]{1,0:T(8,128)(2,1)S(1)}, u32[]{:S(2)}, u32[]{:S(2)}) collective-permute-start(bf16[24,4224]{1,0:T(8,128)(2,1)S(1)} %pad_maximum_fusion.1), channel_id=1, source_target_pairs={{0,2},{1,3},{2,0},{3,1},{4,6},{5,7},{6,4},{7,5},{8,10},{9,11},{10,... | collective-permute-start | bytes 608264 | tf_op jit(solution)/shard_map/ppermute | solution.py:24
  162.0 0.0 collective-permute-done.17
  162.1 5.6 %collective-permute-done.20 = bf16[24,4224]{1,0:T(8,128)(2,1)S(1)} collective-permute-done((bf16[24,4224]{1,0:T(8,128)(2,1)S(1)}, bf16[24,4224]{1,0:T(8,128)(2,1)S(1)}, u32[]{:S(2)}, u32[]{:S(2)}) %collective-permute-start.20) | collective-permute-done | bytes 202784 | tf_op jit(solution)/shard_map/ppermute | solution.py:24
  167.8 0.0 collective-permute-done.22
  167.9 1.9 %collective-permute-start.23 = (bf16[128,4224]{1,0:T(8,128)(2,1)S(1)}, bf16[128,4224]{1,0:T(8,128)(2,1)S(1)}, u32[]{:S(2)}, u32[]{:S(2)}) collective-permute-start(bf16[128,4224]{1,0:T(8,128)(2,1)S(1)} %constant_dynamic-update-slice_fusion.a.twin), channel_id=1, source_target_pairs={{0,1},{1,0},{2,3},{3,2},{4,5},{5,4},{6,7},{7,6},{8,9},{9,8},{10,11... | collective-permute-start | bytes 3244040 | tf_op jit(solution)/shard_map/ppermute | solution.py:28
  169.8 0.7 maximum_select_fusion
  170.5 1.3 first_half.1.start
  171.8 0.6 collective-permute-done.23.a
  172.5 2.1 %second_half.1 = (bf16[288,128]{1,0:T(8,128)(2,1)}, f32[1]{0:T(128)}) custom-call(s32[4]{0:T(128)S(1)} %pad_add_fusion.ids, bf16[288,8192]{1,0:T(8,128)(2,1)S(1)} %prefetch.1.weight, bf16[128,4224]{1,0:T(8,128)(2,1)S(1)} %collective-permute-done.23.a, f32[288,128]{1,0:T(8,128)S(1)} %first_half.1.start, bf16[8,4224]{1,0:T(8,128)(2,1)S(1)} %collective-permute-done.12.arrived, ...), custom_call_target="tpu_custom_call" | custom-call | tf_op jit(solution)/shard_map/second_half/pallas_call | solution.py:193
  (36 shorter events, 0.7 us)
Async XLA Ops:
  3.4 4.7 %collective-permute-start = (bf16[128,4096]{1,0:T(8,128)(2,1)S(1)}, bf16[128,4096]{1,0:T(8,128)(2,1)S(1)}, u32[]{:S(2)}, u32[]{:S(2)}) collective-permute-start(bf16[128,4096]{1,0:T(8,128)(2,1)S(1)} %out_proj.3), channel_id=1, source_target_pairs={{0,1},{1,0},{2,3},{3,2},{4,5},{5,4},{6,7},{7,6},{8,9},{9,8},{10,11... | collective-permute-start | bytes 3145736 | tf_op jit(solution)/shard_map/ppermute | solution.py:28
  8.1 6.6 %collective-permute-start.1 = (bf16[8,4096]{1,0:T(8,128)(2,1)S(1)}, bf16[8,4096]{1,0:T(8,128)(2,1)S(1)}, u32[]{:S(2)}, u32[]{:S(2)}) collective-permute-start(bf16[8,4096]{1,0:T(8,128)(2,1)S(1)} %fusion), channel_id=1, source_target_pairs={{0,2},{1,3},{2,0},{3,1},{4,6},{5,7},{6,4},{7,5},{8,10},{9,11},{10,... | collective-permute-start | bytes 196616 | tf_op jit(solution)/shard_map/ppermute | solution.py:24
  12.0 10.3 %collective-permute-start.2 = (bf16[24,4096]{1,0:T(8,128)(2,1)S(1)}, bf16[24,4096]{1,0:T(8,128)(2,1)S(1)}, u32[]{:S(2)}, u32[]{:S(2)}) collective-permute-start(bf16[24,4096]{1,0:T(8,128)(2,1)S(1)} %pad_maximum_fusion.2), channel_id=1, source_target_pairs={{0,2},{1,3},{2,0},{3,1},{4,6},{5,7},{6,4},{7,5},{8,10},{9,11},{10,... | collective-permute-start | bytes 589832 | tf_op jit(solution)/shard_map/ppermute | solution.py:24
  14.7 7.6 %collective-permute-start.3 = (bf16[8,4096]{1,0:T(8,128)(2,1)S(1)}, bf16[8,4096]{1,0:T(8,128)(2,1)S(1)}, u32[]{:S(2)}, u32[]{:S(2)}) collective-permute-start(bf16[8,4096]{1,0:T(8,128)(2,1)S(1)} %add_convert_fusion.10), channel_id=1, source_target_pairs={{0,4},{1,5},{2,6},{3,7},{4,0},{5,1},{6,2},{7,3},{8,12},{9,13},{10,... | collective-permute-start | bytes 196616 | tf_op jit(solution)/shard_map/ppermute | solution.py:24
  22.6 18.1 %collective-permute-start.4 = (bf16[24,4096]{1,0:T(8,128)(2,1)S(1)}, bf16[24,4096]{1,0:T(8,128)(2,1)S(1)}, u32[]{:S(2)}, u32[]{:S(2)}) collective-permute-start(bf16[24,4096]{1,0:T(8,128)(2,1)S(1)} %pad_maximum_fusion.3), channel_id=1, source_target_pairs={{0,2},{1,3},{2,0},{3,1},{4,6},{5,7},{6,4},{7,5},{8,10},{9,11},{10,... | collective-permute-start | bytes 589832 | tf_op jit(solution)/shard_map/ppermute | solution.py:24
  27.7 12.9 %collective-permute-start.5 = (bf16[16,4096]{1,0:T(8,128)(2,1)S(1)}, bf16[16,4096]{1,0:T(8,128)(2,1)S(1)}, u32[]{:S(2)}, u32[]{:S(2)}) collective-permute-start(bf16[16,4096]{1,0:T(8,128)(2,1)S(1)} %pad_maximum_fusion.5), channel_id=1, source_target_pairs={{0,4},{1,5},{2,6},{3,7},{4,0},{5,1},{6,2},{7,3},{8,12},{9,13},{10,... | collective-permute-start | bytes 393224 | tf_op jit(solution)/shard_map/ppermute | solution.py:24
  31.5 13.7 %collective-permute-start.6 = (bf16[8,4096]{1,0:T(8,128)(2,1)S(1)}, bf16[8,4096]{1,0:T(8,128)(2,1)S(1)}, u32[]{:S(2)}, u32[]{:S(2)}) collective-permute-start(bf16[8,4096]{1,0:T(8,128)(2,1)S(1)} %add_convert_fusion.9), channel_id=1, source_target_pairs={{0,8},{1,9},{2,10},{3,11},{4,12},{5,13},{6,14},{7,15},{8,0},{9,1},... | collective-permute-start | bytes 196616 | tf_op jit(solution)/shard_map/ppermute | solution.py:24
  40.6 44.0 %copy-start = (bf16[8192]{0:T(1024)(128)(2,1)S(1)}, bf16[8192]{0:T(1024)(128)(2,1)}, u32[]{:S(2)}) copy-start(bf16[8192]{0:T(1024)(128)(2,1)} %param.9) | copy-start | bytes 49156
  45.3 29.4 %collective-permute-start.7 = (bf16[8,4096]{1,0:T(8,128)(2,1)S(1)}, bf16[8,4096]{1,0:T(8,128)(2,1)S(1)}, u32[]{:S(2)}, u32[]{:S(2)}) collective-permute-start(bf16[8,4096]{1,0:T(8,128)(2,1)S(1)} %get-tuple-element.63), channel_id=1, source_target_pairs={{0,2},{1,3},{2,0},{3,1},{4,6},{5,7},{6,4},{7,5},{8,10},{9,11},{10,... | collective-permute-start | bytes 196616 | tf_op jit(solution)/shard_map/ppermute | solution.py:24
  47.2 27.5 %collective-permute-start.9 = (bf16[8,4096]{1,0:T(8,128)(2,1)S(1)}, bf16[8,4096]{1,0:T(8,128)(2,1)S(1)}, u32[]{:S(2)}, u32[]{:S(2)}) collective-permute-start(bf16[8,4096]{1,0:T(8,128)(2,1)S(1)} %get-tuple-element.64), channel_id=1, source_target_pairs={{0,8},{1,9},{2,10},{3,11},{4,12},{5,13},{6,14},{7,15},{8,0},{9,1},... | collective-permute-start | bytes 196616 | tf_op jit(solution)/shard_map/ppermute | solution.py:24
  53.1 21.6 %collective-permute-start.8 = (bf16[8,4096]{1,0:T(8,128)(2,1)S(1)}, bf16[8,4096]{1,0:T(8,128)(2,1)S(1)}, u32[]{:S(2)}, u32[]{:S(2)}) collective-permute-start(bf16[8,4096]{1,0:T(8,128)(2,1)S(1)} %get-tuple-element.65), channel_id=1, source_target_pairs={{0,4},{1,5},{2,6},{3,7},{4,0},{5,1},{6,2},{7,3},{8,12},{9,13},{10,... | collective-permute-start | bytes 196616 | tf_op jit(solution)/shard_map/ppermute | solution.py:24
  59.0 23.0 %collective-permute-start.10 = (bf16[8,4096]{1,0:T(8,128)(2,1)S(1)}, bf16[8,4096]{1,0:T(8,128)(2,1)S(1)}, u32[]{:S(2)}, u32[]{:S(2)}) collective-permute-start(bf16[8,4096]{1,0:T(8,128)(2,1)S(1)} %add_convert_fusion.3), channel_id=1, source_target_pairs={{0,16},{1,17},{2,18},{3,19},{4,20},{5,21},{6,22},{7,23},{8,24},{9,... | collective-permute-start | bytes 196616 | tf_op jit(solution)/shard_map/ppermute | solution.py:24
  82.0 3.1 %collective-permute-start.11 = (bf16[8,4096]{1,0:T(8,128)(2,1)S(1)}, bf16[8,4096]{1,0:T(8,128)(2,1)S(1)}, u32[]{:S(2)}, u32[]{:S(2)}) collective-permute-start(bf16[8,4096]{1,0:T(8,128)(2,1)S(1)} %reduce-precision_convert_fusion.own), channel_id=1, source_target_pairs={{0,1},{1,0},{2,3},{3,2},{4,5},{5,4},{6,7},{7,6},{8,9},{9,8},{10,11... | collective-permute-start | bytes 196616 | tf_op jit(solution)/shard_map/ppermute | solution.py:28
  85.9 18.0 %collective-permute-start.12 = (bf16[8,4224]{1,0:T(8,128)(2,1)S(1)}, bf16[8,4224]{1,0:T(8,128)(2,1)S(1)}, u32[]{:S(2)}, u32[]{:S(2)}) collective-permute-start(bf16[8,4224]{1,0:T(8,128)(2,1)S(1)} %get-tuple-element.59), channel_id=1, source_target_pairs={{0,32},{1,33},{2,34},{3,35},{4,36},{5,37},{6,38},{7,39},{8,40},{9,... | collective-permute-start | bytes 202760 | tf_op jit(solution)/shard_map/ppermute | solution.py:37
  104.0 24.3 %collective-permute-start.15 = (bf16[8,4224]{1,0:T(8,128)(2,1)S(1)}, bf16[8,4224]{1,0:T(8,128)(2,1)S(1)}, u32[]{:S(2)}, u32[]{:S(2)}) collective-permute-start(bf16[8,4224]{1,0:T(8,128)(2,1)S(1)} %get-tuple-element.78), channel_id=1, source_target_pairs={{0,16},{1,17},{2,18},{3,19},{4,20},{5,21},{6,22},{7,23},{8,24},{9,... | collective-permute-start | bytes 202760 | tf_op jit(solution)/shard_map/ppermute | solution.py:24
  121.2 10.1 %collective-permute-start.16 = (bf16[8,4224]{1,0:T(8,128)(2,1)S(1)}, bf16[8,4224]{1,0:T(8,128)(2,1)S(1)}, u32[]{:S(2)}, u32[]{:S(2)}) collective-permute-start(bf16[8,4224]{1,0:T(8,128)(2,1)S(1)} %get-tuple-element.78), channel_id=1, source_target_pairs={{0,8},{1,9},{2,10},{3,11},{4,12},{5,13},{6,14},{7,15},{8,0},{9,1},... | collective-permute-start | bytes 202760 | tf_op jit(solution)/shard_map/ppermute | solution.py:24
  123.2 10.1 %collective-permute-start.14 = (bf16[8,4224]{1,0:T(8,128)(2,1)S(1)}, bf16[8,4224]{1,0:T(8,128)(2,1)S(1)}, u32[]{:S(2)}, u32[]{:S(2)}) collective-permute-start(bf16[8,4224]{1,0:T(8,128)(2,1)S(1)} %get-tuple-element.78), channel_id=1, source_target_pairs={{0,4},{1,5},{2,6},{3,7},{4,0},{5,1},{6,2},{7,3},{8,12},{9,13},{10,... | collective-permute-start | bytes 202760 | tf_op jit(solution)/shard_map/ppermute | solution.py:24
  125.1 18.6 %collective-permute-start.13 = (bf16[8,4224]{1,0:T(8,128)(2,1)S(1)}, bf16[8,4224]{1,0:T(8,128)(2,1)S(1)}, u32[]{:S(2)}, u32[]{:S(2)}) collective-permute-start(bf16[8,4224]{1,0:T(8,128)(2,1)S(1)} %get-tuple-element.78), channel_id=1, source_target_pairs={{0,2},{1,3},{2,0},{3,1},{4,6},{5,7},{6,4},{7,5},{8,10},{9,11},{10,... | collective-permute-start | bytes 202760 | tf_op jit(solution)/shard_map/ppermute | solution.py:24
  131.3 28.7 %collective-permute-start.18 = (bf16[16,4224]{1,0:T(8,128)(2,1)S(1)}, bf16[16,4224]{1,0:T(8,128)(2,1)S(1)}, u32[]{:S(2)}, u32[]{:S(2)}) collective-permute-start(bf16[16,4224]{1,0:T(8,128)(2,1)S(1)} %pad_maximum_fusion.4), channel_id=1, source_target_pairs={{0,4},{1,5},{2,6},{3,7},{4,0},{5,1},{6,2},{7,3},{8,12},{9,13},{10,... | collective-permute-start | bytes 405512 | tf_op jit(solution)/shard_map/ppermute | solution.py:24
  133.3 28.7 %collective-permute-start.17 = (bf16[24,4224]{1,0:T(8,128)(2,1)S(1)}, bf16[24,4224]{1,0:T(8,128)(2,1)S(1)}, u32[]{:S(2)}, u32[]{:S(2)}) collective-permute-start(bf16[24,4224]{1,0:T(8,128)(2,1)S(1)} %pad_maximum_fusion), channel_id=1, source_target_pairs={{0,2},{1,3},{2,0},{3,1},{4,6},{5,7},{6,4},{7,5},{8,10},{9,11},{10,... | collective-permute-start | bytes 608264 | tf_op jit(solution)/shard_map/ppermute | solution.py:24
  135.9 12.1 %collective-permute-start.19 = (bf16[8,4224]{1,0:T(8,128)(2,1)S(1)}, bf16[8,4224]{1,0:T(8,128)(2,1)S(1)}, u32[]{:S(2)}, u32[]{:S(2)}) collective-permute-start(bf16[8,4224]{1,0:T(8,128)(2,1)S(1)} %collective-permute-done.15), channel_id=1, source_target_pairs={{0,8},{1,9},{2,10},{3,11},{4,12},{5,13},{6,14},{7,15},{8,0},{9,1},... | collective-permute-start | bytes 202760 | tf_op jit(solution)/shard_map/ppermute | solution.py:24
  148.0 7.1 %collective-permute-start.21 = (bf16[8,4224]{1,0:T(8,128)(2,1)S(1)}, bf16[8,4224]{1,0:T(8,128)(2,1)S(1)}, u32[]{:S(2)}, u32[]{:S(2)}) collective-permute-start(bf16[8,4224]{1,0:T(8,128)(2,1)S(1)} %collective-permute-done.19), channel_id=1, source_target_pairs={{0,4},{1,5},{2,6},{3,7},{4,0},{5,1},{6,2},{7,3},{8,12},{9,13},{10,... | collective-permute-start | bytes 202760 | tf_op jit(solution)/shard_map/ppermute | solution.py:24
  155.1 12.8 %collective-permute-start.22 = (bf16[8,4224]{1,0:T(8,128)(2,1)S(1)}, bf16[8,4224]{1,0:T(8,128)(2,1)S(1)}, u32[]{:S(2)}, u32[]{:S(2)}) collective-permute-start(bf16[8,4224]{1,0:T(8,128)(2,1)S(1)} %collective-permute-done.21), channel_id=1, source_target_pairs={{0,2},{1,3},{2,0},{3,1},{4,6},{5,7},{6,4},{7,5},{8,10},{9,11},{10,... | collective-permute-start | bytes 202760 | tf_op jit(solution)/shard_map/ppermute | solution.py:24
  160.1 7.6 %collective-permute-start.20 = (bf16[24,4224]{1,0:T(8,128)(2,1)S(1)}, bf16[24,4224]{1,0:T(8,128)(2,1)S(1)}, u32[]{:S(2)}, u32[]{:S(2)}) collective-permute-start(bf16[24,4224]{1,0:T(8,128)(2,1)S(1)} %pad_maximum_fusion.1), channel_id=1, source_target_pairs={{0,2},{1,3},{2,0},{3,1},{4,6},{5,7},{6,4},{7,5},{8,10},{9,11},{10,... | collective-permute-start | bytes 608264 | tf_op jit(solution)/shard_map/ppermute | solution.py:24
  167.9 4.6 %collective-permute-start.23 = (bf16[128,4224]{1,0:T(8,128)(2,1)S(1)}, bf16[128,4224]{1,0:T(8,128)(2,1)S(1)}, u32[]{:S(2)}, u32[]{:S(2)}) collective-permute-start(bf16[128,4224]{1,0:T(8,128)(2,1)S(1)} %constant_dynamic-update-slice_fusion.a.twin), channel_id=1, source_target_pairs={{0,1},{1,0},{2,3},{3,2},{4,5},{5,4},{6,7},{7,6},{8,9},{9,8},{10,11... | collective-permute-start | bytes 3244040 | tf_op jit(solution)/shard_map/ppermute | solution.py:28

commit v3 on v2

--- a/solution.py
+++ b/solution.py
@@ -228,26 +228,29 @@
     a15 = across(out15, 1)
     out13, kept, incoming = apart(packed(block(13), block(11), block(7)), kept, incoming)
     a13 = across(out13, 1)
+    out9, kept, incoming = apart(packed(block(9), block(5), block(3)), kept, incoming)
+    a9 = across(out9, 1)
     out14, kept, incoming = apart(packed(block(14) + a15.astype(f32)), kept, incoming)
     a14 = across(out14, 2)
     b13, b11, b7 = split(a13)
-    out12, b11, b7, kept, incoming = apart(
-        packed(block(12) + b13.astype(f32) + a14.astype(f32)), b11, b7, kept, incoming
-    )
+    out10, b13, kept, incoming = apart(
+        packed(block(10) + b11.astype(f32), block(6) + b7.astype(f32)), b13, kept, incoming
+    )
+    a10 = across(out10, 2)
+    out12, kept, incoming = apart(packed(block(12) + b13.astype(f32) + a14.astype(f32)), kept, incoming)
     a12 = across(out12, 4)
-    out10, kept, incoming = apart(packed(block(10) + b11.astype(f32), block(6) + b7.astype(f32)), kept, incoming)
-    a10 = across(out10, 2)
-    out9, kept, incoming = apart(packed(block(9), block(5), block(3)), kept, incoming)
-    a9 = across(out9, 1)
     c9, c5, c3 = split(a9)
+    out1, out2, c9, c5, kept, incoming = apart(
+        packed(block(1)), packed(block(2) + c3.astype(f32)), c9, c5, kept, incoming
+    )
+    a1 = across(out1, 1)
+    a2 = across(out2, 2)
     c10, c6 = split(a10)
-    out8, c5, c3, c6, kept, incoming = apart(
-        packed(block(8) + c9.astype(f32) + c10.astype(f32) + a12.astype(f32)), c5, c3, c6, kept, incoming
-    )
-    a8 = across(out8, 8)
-    a4 = across(packed(block(4) + c5.astype(f32) + c6.astype(f32)), 4)
-    a2 = across(packed(block(2) + c3.astype(f32)), 2)
-    a1 = across(packed(block(1)), 1)
+    out4, c9, c10, kept, incoming = apart(
+        packed(block(4) + c5.astype(f32) + c6.astype(f32)), c9, c10, kept, incoming
+    )
+    a4 = across(out4, 4)
+    a8 = across(packed(block(8) + c9.astype(f32) + c10.astype(f32) + a12.astype(f32)), 8)
     return block(0) + a1.astype(f32) + a2.astype(f32) + a4.astype(f32) + a8.astype(f32)
 
 

time: 178 us -> 177 us (level)
  the two profiles are of different devices: /device:TPU:6 before, /device:TPU:1 now
where the time goes in v3:
time: 177 us; the launch traced here: 176 us
  starting transfers between devices  113 us (64%)
  waiting for transfers between devices  47.5 us (27%)
  Pallas kernels  11.9 us (7%)
  between operations  1.84 us (1%)
    ppermute x20, starting transfers between devices, across(): return lax.ppermute(x, 'tp', [(i, i ^ 2 * d) for i in range(TP)])  78.7 us
    ppermute x20, waiting for transfers between devices, across(): return lax.ppermute(x, 'tp', [(i, i ^ 2 * d) for i in range(TP)])  33.1 us
    ppermute x3, starting transfers between devices, other_core(): return lax.ppermute(x, 'tp', [(i, i ^ 1) for i in range(TP)])  32.4 us
    ppermute x1, waiting for transfers between devices, next_section(): return lax.ppermute(x, ('section', 'tp'), pairs)  13.9 us
    pallas_call x2, Pallas kernels, out_proj(): pl.pallas_call(out_proj_body, out_shape=jax.ShapeDtypeStruct((TOK, HALF),...  5.4 us
  transfers between devices with their start and end apart: 24, of which 11 were waited for; matrix products, arithmetic and copies ran while one was open for 1% of the time, Pallas kernels for 4%

profile of v3, /device:TPU:1, one launch (start us, length us, event | category | flops | bytes accessed | tf_op | source)
XLA Modules:
  0.0 175.8 jit_solution(4453588757546471789)
XLA Ops:
  0.7 0.1 pad_add_fusion.ids
  0.7 2.7 %out_proj.3 = bf16[128,4096]{1,0:T(8,128)(2,1)S(1)} custom-call(s32[4]{0:T(128)S(1)} %pad_add_fusion.ids, bf16[128,256]{1,0:T(8,128)(2,1)} %bitcast.15, bf16[256,8192]{1,0:T(8,128)(2,1)} %weight.3, bf16[4,8192]{1,0:T(4,128)(2,1)} %bitcast.17), custom_call_target="tpu_custom_call" | custom-call | tf_op jit(solution)/shard_map/out_proj/pallas_call | solution.py:67
  3.4 16.0 %collective-permute-start = (bf16[128,4096]{1,0:T(8,128)(2,1)S(1)}, bf16[128,4096]{1,0:T(8,128)(2,1)S(1)}, u32[]{:S(2)}, u32[]{:S(2)}) collective-permute-start(bf16[128,4096]{1,0:T(8,128)(2,1)S(1)} %out_proj.3), channel_id=1, source_target_pairs={{0,1},{1,0},{2,3},{3,2},{4,5},{5,4},{6,7},{7,6},{8,9},{9,8},{10,11... | collective-permute-start | bytes 3145736 | tf_op jit(solution)/shard_map/ppermute | solution.py:28
  19.4 2.7 %out_proj.2 = f32[128,4096]{1,0:T(8,128)S(1)} custom-call(s32[4]{0:T(128)S(1)} %pad_add_fusion.ids, bf16[128,256]{1,0:T(8,128)(2,1)} %bitcast.16, bf16[256,8192]{1,0:T(8,128)(2,1)} %weight.3, bf16[4,8192]{1,0:T(4,128)(2,1)} %bitcast.18), custom_call_target="tpu_custom_call" | custom-call | tf_op jit(solution)/shard_map/out_proj/pallas_call | solution.py:67
  22.2 0.0 collective-permute-done
  22.2 1.9 %collective-permute-start.1 = (bf16[8,4096]{1,0:T(8,128)(2,1)S(1)}, bf16[8,4096]{1,0:T(8,128)(2,1)S(1)}, u32[]{:S(2)}, u32[]{:S(2)}) collective-permute-start(bf16[8,4096]{1,0:T(8,128)(2,1)S(1)} %fusion), channel_id=1, source_target_pairs={{0,2},{1,3},{2,0},{3,1},{4,6},{5,7},{6,4},{7,5},{8,10},{9,11},{10,... | collective-permute-start | bytes 196616 | tf_op jit(solution)/shard_map/ppermute | solution.py:24
  24.3 3.4 %collective-permute-start.4 = (bf16[24,4096]{1,0:T(8,128)(2,1)S(1)}, bf16[24,4096]{1,0:T(8,128)(2,1)S(1)}, u32[]{:S(2)}, u32[]{:S(2)}) collective-permute-start(bf16[24,4096]{1,0:T(8,128)(2,1)S(1)} %pad_maximum_fusion.3), channel_id=1, source_target_pairs={{0,2},{1,3},{2,0},{3,1},{4,6},{5,7},{6,4},{7,5},{8,10},{9,11},{10,... | collective-permute-start | bytes 589832 | tf_op jit(solution)/shard_map/ppermute | solution.py:24
  27.7 1.9 %collective-permute-start.2 = (bf16[24,4096]{1,0:T(8,128)(2,1)S(1)}, bf16[24,4096]{1,0:T(8,128)(2,1)S(1)}, u32[]{:S(2)}, u32[]{:S(2)}) collective-permute-start(bf16[24,4096]{1,0:T(8,128)(2,1)S(1)} %pad_maximum_fusion.2), channel_id=1, source_target_pairs={{0,2},{1,3},{2,0},{3,1},{4,6},{5,7},{6,4},{7,5},{8,10},{9,11},{10,... | collective-permute-start | bytes 589832 | tf_op jit(solution)/shard_map/ppermute | solution.py:24
  29.6 0.0 collective-permute-done.1
  29.6 1.9 %collective-permute-start.3 = (bf16[8,4096]{1,0:T(8,128)(2,1)S(1)}, bf16[8,4096]{1,0:T(8,128)(2,1)S(1)}, u32[]{:S(2)}, u32[]{:S(2)}) collective-permute-start(bf16[8,4096]{1,0:T(8,128)(2,1)S(1)} %add_convert_fusion.7), channel_id=1, source_target_pairs={{0,4},{1,5},{2,6},{3,7},{4,0},{5,1},{6,2},{7,3},{8,12},{9,13},{10,... | collective-permute-start | bytes 196616 | tf_op jit(solution)/shard_map/ppermute | solution.py:24
  31.6 6.7 %collective-permute-done.2 = bf16[24,4096]{1,0:T(8,128)(2,1)S(1)} collective-permute-done((bf16[24,4096]{1,0:T(8,128)(2,1)S(1)}, bf16[24,4096]{1,0:T(8,128)(2,1)S(1)}, u32[]{:S(2)}, u32[]{:S(2)}) %collective-permute-start.2) | collective-permute-done | bytes 196640 | tf_op jit(solution)/shard_map/ppermute | solution.py:24
  38.3 0.0 collective-permute-done.3
  38.4 0.0 copy-start
  38.4 3.6 %collective-permute-start.5 = (bf16[16,4096]{1,0:T(8,128)(2,1)S(1)}, bf16[16,4096]{1,0:T(8,128)(2,1)S(1)}, u32[]{:S(2)}, u32[]{:S(2)}) collective-permute-start(bf16[16,4096]{1,0:T(8,128)(2,1)S(1)} %pad_maximum_fusion.5), channel_id=1, source_target_pairs={{0,4},{1,5},{2,6},{3,7},{4,0},{5,1},{6,2},{7,3},{8,12},{9,13},{10,... | collective-permute-start | bytes 393224 | tf_op jit(solution)/shard_map/ppermute | solution.py:24
  42.0 0.0 collective-permute-done.4
  42.1 1.9 %collective-permute-start.6 = (bf16[8,4096]{1,0:T(8,128)(2,1)S(1)}, bf16[8,4096]{1,0:T(8,128)(2,1)S(1)}, u32[]{:S(2)}, u32[]{:S(2)}) collective-permute-start(bf16[8,4096]{1,0:T(8,128)(2,1)S(1)} %get-tuple-element.61), channel_id=1, source_target_pairs={{0,2},{1,3},{2,0},{3,1},{4,6},{5,7},{6,4},{7,5},{8,10},{9,11},{10,... | collective-permute-start | bytes 196616 | tf_op jit(solution)/shard_map/ppermute | solution.py:24
  44.0 2.6 %collective-permute-start.7 = (bf16[8,4096]{1,0:T(8,128)(2,1)S(1)}, bf16[8,4096]{1,0:T(8,128)(2,1)S(1)}, u32[]{:S(2)}, u32[]{:S(2)}) collective-permute-start(bf16[8,4096]{1,0:T(8,128)(2,1)S(1)} %get-tuple-element.62), channel_id=1, source_target_pairs={{0,4},{1,5},{2,6},{3,7},{4,0},{5,1},{6,2},{7,3},{8,12},{9,13},{10,... | collective-permute-start | bytes 196616 | tf_op jit(solution)/shard_map/ppermute | solution.py:24
  46.6 1.9 %collective-permute-start.9 = (bf16[8,4096]{1,0:T(8,128)(2,1)S(1)}, bf16[8,4096]{1,0:T(8,128)(2,1)S(1)}, u32[]{:S(2)}, u32[]{:S(2)}) collective-permute-start(bf16[8,4096]{1,0:T(8,128)(2,1)S(1)} %add_convert_fusion.4), channel_id=1, source_target_pairs={{0,8},{1,9},{2,10},{3,11},{4,12},{5,13},{6,14},{7,15},{8,0},{9,1},... | collective-permute-start | bytes 196616 | tf_op jit(solution)/shard_map/ppermute | solution.py:24
  48.5 0.1 collective-permute-done.5
  48.7 6.9 %collective-permute-done.9 = bf16[8,4096]{1,0:T(8,128)(2,1)S(1)} collective-permute-done((bf16[8,4096]{1,0:T(8,128)(2,1)S(1)}, bf16[8,4096]{1,0:T(8,128)(2,1)S(1)}, u32[]{:S(2)}, u32[]{:S(2)}) %collective-permute-start.9) | collective-permute-done | bytes 65568 | tf_op jit(solution)/shard_map/ppermute | solution.py:24
  55.6 9.9 %collective-permute-start.10 = (bf16[8,4096]{1,0:T(8,128)(2,1)S(1)}, bf16[8,4096]{1,0:T(8,128)(2,1)S(1)}, u32[]{:S(2)}, u32[]{:S(2)}) collective-permute-start(bf16[8,4096]{1,0:T(8,128)(2,1)S(1)} %add_convert_fusion), channel_id=1, source_target_pairs={{0,16},{1,17},{2,18},{3,19},{4,20},{5,21},{6,22},{7,23},{8,24},{9,... | collective-permute-start | bytes 196616 | tf_op jit(solution)/shard_map/ppermute | solution.py:24
  65.5 5.7 %collective-permute-start.8 = (bf16[8,4096]{1,0:T(8,128)(2,1)S(1)}, bf16[8,4096]{1,0:T(8,128)(2,1)S(1)}, u32[]{:S(2)}, u32[]{:S(2)}) collective-permute-start(bf16[8,4096]{1,0:T(8,128)(2,1)S(1)} %add_convert_fusion.1), channel_id=1, source_target_pairs={{0,8},{1,9},{2,10},{3,11},{4,12},{5,13},{6,14},{7,15},{8,0},{9,1},... | collective-permute-start | bytes 196616 | tf_op jit(solution)/shard_map/ppermute | solution.py:24
  71.2 0.0 collective-permute-done.6
  71.2 0.0 collective-permute-done.7
  71.2 0.0 collective-permute-done.10
  71.2 3.6 %collective-permute-done.8 = bf16[8,4096]{1,0:T(8,128)(2,1)S(1)} collective-permute-done((bf16[8,4096]{1,0:T(8,128)(2,1)S(1)}, bf16[8,4096]{1,0:T(8,128)(2,1)S(1)}, u32[]{:S(2)}, u32[]{:S(2)}) %collective-permute-start.8) | collective-permute-done | bytes 65568 | tf_op jit(solution)/shard_map/ppermute | solution.py:24
  74.8 0.1 reduce-precision_convert_fusion.own
  74.9 10.4 %collective-permute-start.11 = (bf16[8,4096]{1,0:T(8,128)(2,1)S(1)}, bf16[8,4096]{1,0:T(8,128)(2,1)S(1)}, u32[]{:S(2)}, u32[]{:S(2)}) collective-permute-start(bf16[8,4096]{1,0:T(8,128)(2,1)S(1)} %reduce-precision_convert_fusion.own), channel_id=1, source_target_pairs={{0,1},{1,0},{2,3},{3,2},{4,5},{5,4},{6,7},{7,6},{8,9},{9,8},{10,11... | collective-permute-start | bytes 196616 | tf_op jit(solution)/shard_map/ppermute | solution.py:28
  86.0 0.0 copy-done
  86.0 0.2 collective-permute-done.11.twin
  86.2 0.8 cast.1
  87.0 1.9 %collective-permute-start.12 = (bf16[8,4224]{1,0:T(8,128)(2,1)S(1)}, bf16[8,4224]{1,0:T(8,128)(2,1)S(1)}, u32[]{:S(2)}, u32[]{:S(2)}) collective-permute-start(bf16[8,4224]{1,0:T(8,128)(2,1)S(1)} %get-tuple-element.67), channel_id=1, source_target_pairs={{0,32},{1,33},{2,34},{3,35},{4,36},{5,37},{6,38},{7,39},{8,40},{9,... | collective-permute-start | bytes 202760 | tf_op jit(solution)/shard_map/ppermute | solution.py:37
  88.9 2.3 %prefetch.1.weight = bf16[288,8192]{1,0:T(8,128)(2,1)S(1)} custom-call(bf16[288,8192]{1,0:T(8,128)(2,1)} %bitcast.14), custom_call_target="tpu_custom_call" | custom-call | tf_op jit(solution)/shard_map/prefetch/pallas_call | solution.py:136
  91.2 13.9 %collective-permute-done.12.arrived = bf16[8,4224]{1,0:T(8,128)(2,1)S(1)} collective-permute-done((bf16[8,4224]{1,0:T(8,128)(2,1)S(1)}, bf16[8,4224]{1,0:T(8,128)(2,1)S(1)}, u32[]{:S(2)}, u32[]{:S(2)}) %collective-permute-start.12) | collective-permute-done | bytes 67616 | tf_op jit(solution)/shard_map/ppermute | solution.py:37
  105.2 16.1 %collective-permute-start.15 = (bf16[8,4224]{1,0:T(8,128)(2,1)S(1)}, bf16[8,4224]{1,0:T(8,128)(2,1)S(1)}, u32[]{:S(2)}, u32[]{:S(2)}) collective-permute-start(bf16[8,4224]{1,0:T(8,128)(2,1)S(1)} %get-tuple-element.83), channel_id=1, source_target_pairs={{0,16},{1,17},{2,18},{3,19},{4,20},{5,21},{6,22},{7,23},{8,24},{9,... | collective-permute-start | bytes 202760 | tf_op jit(solution)/shard_map/ppermute | solution.py:24
  121.4 1.9 %collective-permute-start.16 = (bf16[8,4224]{1,0:T(8,128)(2,1)S(1)}, bf16[8,4224]{1,0:T(8,128)(2,1)S(1)}, u32[]{:S(2)}, u32[]{:S(2)}) collective-permute-start(bf16[8,4224]{1,0:T(8,128)(2,1)S(1)} %get-tuple-element.83), channel_id=1, source_target_pairs={{0,8},{1,9},{2,10},{3,11},{4,12},{5,13},{6,14},{7,15},{8,0},{9,1},... | collective-permute-start | bytes 202760 | tf_op jit(solution)/shard_map/ppermute | solution.py:24
  123.3 1.9 %collective-permute-start.14 = (bf16[8,4224]{1,0:T(8,128)(2,1)S(1)}, bf16[8,4224]{1,0:T(8,128)(2,1)S(1)}, u32[]{:S(2)}, u32[]{:S(2)}) collective-permute-start(bf16[8,4224]{1,0:T(8,128)(2,1)S(1)} %get-tuple-element.83), channel_id=1, source_target_pairs={{0,4},{1,5},{2,6},{3,7},{4,0},{5,1},{6,2},{7,3},{8,12},{9,13},{10,... | collective-permute-start | bytes 202760 | tf_op jit(solution)/shard_map/ppermute | solution.py:24
  125.3 1.9 %collective-permute-start.13 = (bf16[8,4224]{1,0:T(8,128)(2,1)S(1)}, bf16[8,4224]{1,0:T(8,128)(2,1)S(1)}, u32[]{:S(2)}, u32[]{:S(2)}) collective-permute-start(bf16[8,4224]{1,0:T(8,128)(2,1)S(1)} %get-tuple-element.83), channel_id=1, source_target_pairs={{0,2},{1,3},{2,0},{3,1},{4,6},{5,7},{6,4},{7,5},{8,10},{9,11},{10,... | collective-permute-start | bytes 202760 | tf_op jit(solution)/shard_map/ppermute | solution.py:24
  127.2 0.0 collective-permute-done.15
  127.2 5.8 %collective-permute-done.16 = bf16[8,4224]{1,0:T(8,128)(2,1)S(1)} collective-permute-done((bf16[8,4224]{1,0:T(8,128)(2,1)S(1)}, bf16[8,4224]{1,0:T(8,128)(2,1)S(1)}, u32[]{:S(2)}, u32[]{:S(2)}) %collective-permute-start.16) | collective-permute-done | bytes 67616 | tf_op jit(solution)/shard_map/ppermute | solution.py:24
  133.0 1.9 %collective-permute-start.18 = (bf16[16,4224]{1,0:T(8,128)(2,1)S(1)}, bf16[16,4224]{1,0:T(8,128)(2,1)S(1)}, u32[]{:S(2)}, u32[]{:S(2)}) collective-permute-start(bf16[16,4224]{1,0:T(8,128)(2,1)S(1)} %pad_maximum_fusion.4), channel_id=1, source_target_pairs={{0,4},{1,5},{2,6},{3,7},{4,0},{5,1},{6,2},{7,3},{8,12},{9,13},{10,... | collective-permute-start | bytes 405512 | tf_op jit(solution)/shard_map/ppermute | solution.py:24
  135.0 0.0 collective-permute-done.14
  135.0 1.9 %collective-permute-start.17 = (bf16[24,4224]{1,0:T(8,128)(2,1)S(1)}, bf16[24,4224]{1,0:T(8,128)(2,1)S(1)}, u32[]{:S(2)}, u32[]{:S(2)}) collective-permute-start(bf16[24,4224]{1,0:T(8,128)(2,1)S(1)} %pad_maximum_fusion), channel_id=1, source_target_pairs={{0,2},{1,3},{2,0},{3,1},{4,6},{5,7},{6,4},{7,5},{8,10},{9,11},{10,... | collective-permute-start | bytes 608264 | tf_op jit(solution)/shard_map/ppermute | solution.py:24
  136.9 6.1 %collective-permute-start.19 = (bf16[8,4224]{1,0:T(8,128)(2,1)S(1)}, bf16[8,4224]{1,0:T(8,128)(2,1)S(1)}, u32[]{:S(2)}, u32[]{:S(2)}) collective-permute-start(bf16[8,4224]{1,0:T(8,128)(2,1)S(1)} %collective-permute-done.15), channel_id=1, source_target_pairs={{0,8},{1,9},{2,10},{3,11},{4,12},{5,13},{6,14},{7,15},{8,0},{9,1},... | collective-permute-start | bytes 202760 | tf_op jit(solution)/shard_map/ppermute | solution.py:24
  143.0 0.0 collective-permute-done.13
  143.0 3.0 %collective-permute-done.19 = bf16[8,4224]{1,0:T(8,128)(2,1)S(1)} collective-permute-done((bf16[8,4224]{1,0:T(8,128)(2,1)S(1)}, bf16[8,4224]{1,0:T(8,128)(2,1)S(1)}, u32[]{:S(2)}, u32[]{:S(2)}) %collective-permute-start.19) | collective-permute-done | bytes 67616 | tf_op jit(solution)/shard_map/ppermute | solution.py:24
  146.0 4.3 %collective-permute-start.21 = (bf16[8,4224]{1,0:T(8,128)(2,1)S(1)}, bf16[8,4224]{1,0:T(8,128)(2,1)S(1)}, u32[]{:S(2)}, u32[]{:S(2)}) collective-permute-start(bf16[8,4224]{1,0:T(8,128)(2,1)S(1)} %collective-permute-done.19), channel_id=1, source_target_pairs={{0,4},{1,5},{2,6},{3,7},{4,0},{5,1},{6,2},{7,3},{8,12},{9,13},{10,... | collective-permute-start | bytes 202760 | tf_op jit(solution)/shard_map/ppermute | solution.py:24
  150.3 1.8 %collective-permute-done.21 = bf16[8,4224]{1,0:T(8,128)(2,1)S(1)} collective-permute-done((bf16[8,4224]{1,0:T(8,128)(2,1)S(1)}, bf16[8,4224]{1,0:T(8,128)(2,1)S(1)}, u32[]{:S(2)}, u32[]{:S(2)}) %collective-permute-start.21) | collective-permute-done | bytes 67616 | tf_op jit(solution)/shard_map/ppermute | solution.py:24
  152.1 5.9 %collective-permute-start.22 = (bf16[8,4224]{1,0:T(8,128)(2,1)S(1)}, bf16[8,4224]{1,0:T(8,128)(2,1)S(1)}, u32[]{:S(2)}, u32[]{:S(2)}) collective-permute-start(bf16[8,4224]{1,0:T(8,128)(2,1)S(1)} %collective-permute-done.21), channel_id=1, source_target_pairs={{0,2},{1,3},{2,0},{3,1},{4,6},{5,7},{6,4},{7,5},{8,10},{9,11},{10,... | collective-permute-start | bytes 202760 | tf_op jit(solution)/shard_map/ppermute | solution.py:24
  158.1 0.0 collective-permute-done.18
  158.1 1.9 %collective-permute-start.20 = (bf16[24,4224]{1,0:T(8,128)(2,1)S(1)}, bf16[24,4224]{1,0:T(8,128)(2,1)S(1)}, u32[]{:S(2)}, u32[]{:S(2)}) collective-permute-start(bf16[24,4224]{1,0:T(8,128)(2,1)S(1)} %pad_maximum_fusion.1), channel_id=1, source_target_pairs={{0,2},{1,3},{2,0},{3,1},{4,6},{5,7},{6,4},{7,5},{8,10},{9,11},{10,... | collective-permute-start | bytes 608264 | tf_op jit(solution)/shard_map/ppermute | solution.py:24
  160.0 0.0 collective-permute-done.17
  160.1 5.2 %collective-permute-done.20 = bf16[24,4224]{1,0:T(8,128)(2,1)S(1)} collective-permute-done((bf16[24,4224]{1,0:T(8,128)(2,1)S(1)}, bf16[24,4224]{1,0:T(8,128)(2,1)S(1)}, u32[]{:S(2)}, u32[]{:S(2)}) %collective-permute-start.20) | collective-permute-done | bytes 202784 | tf_op jit(solution)/shard_map/ppermute | solution.py:24
  165.4 0.0 collective-permute-done.22
  165.5 5.9 %collective-permute-start.23 = (bf16[128,4224]{1,0:T(8,128)(2,1)S(1)}, bf16[128,4224]{1,0:T(8,128)(2,1)S(1)}, u32[]{:S(2)}, u32[]{:S(2)}) collective-permute-start(bf16[128,4224]{1,0:T(8,128)(2,1)S(1)} %constant_dynamic-update-slice_fusion.a.twin), channel_id=1, source_target_pairs={{0,1},{1,0},{2,3},{3,2},{4,5},{5,4},{6,7},{7,6},{8,9},{9,8},{10,11... | collective-permute-start | bytes 3244040 | tf_op jit(solution)/shard_map/ppermute | solution.py:28
  171.4 0.7 maximum_select_fusion
  172.1 1.3 first_half.1.start
  173.4 0.3 collective-permute-done.23.a
  173.7 2.1 %second_half.1 = (bf16[288,128]{1,0:T(8,128)(2,1)}, f32[1]{0:T(128)}) custom-call(s32[4]{0:T(128)S(1)} %pad_add_fusion.ids, bf16[288,8192]{1,0:T(8,128)(2,1)S(1)} %prefetch.1.weight, bf16[128,4224]{1,0:T(8,128)(2,1)S(1)} %collective-permute-done.23.a, f32[288,128]{1,0:T(8,128)S(1)} %first_half.1.start, bf16[8,4224]{1,0:T(8,128)(2,1)S(1)} %collective-permute-done.12.arrived, ...), custom_call_target="tpu_custom_call" | custom-call | tf_op jit(solution)/shard_map/second_half/pallas_call | solution.py:193
  (38 shorter events, 0.7 us)
Async XLA Ops:
  3.4 18.8 %collective-permute-start = (bf16[128,4096]{1,0:T(8,128)(2,1)S(1)}, bf16[128,4096]{1,0:T(8,128)(2,1)S(1)}, u32[]{:S(2)}, u32[]{:S(2)}) collective-permute-start(bf16[128,4096]{1,0:T(8,128)(2,1)S(1)} %out_proj.3), channel_id=1, source_target_pairs={{0,1},{1,0},{2,3},{3,2},{4,5},{5,4},{6,7},{7,6},{8,9},{9,8},{10,11... | collective-permute-start | bytes 3145736 | tf_op jit(solution)/shard_map/ppermute | solution.py:28
  22.2 7.4 %collective-permute-start.1 = (bf16[8,4096]{1,0:T(8,128)(2,1)S(1)}, bf16[8,4096]{1,0:T(8,128)(2,1)S(1)}, u32[]{:S(2)}, u32[]{:S(2)}) collective-permute-start(bf16[8,4096]{1,0:T(8,128)(2,1)S(1)} %fusion), channel_id=1, source_target_pairs={{0,2},{1,3},{2,0},{3,1},{4,6},{5,7},{6,4},{7,5},{8,10},{9,11},{10,... | collective-permute-start | bytes 196616 | tf_op jit(solution)/shard_map/ppermute | solution.py:24
  24.3 17.7 %collective-permute-start.4 = (bf16[24,4096]{1,0:T(8,128)(2,1)S(1)}, bf16[24,4096]{1,0:T(8,128)(2,1)S(1)}, u32[]{:S(2)}, u32[]{:S(2)}) collective-permute-start(bf16[24,4096]{1,0:T(8,128)(2,1)S(1)} %pad_maximum_fusion.3), channel_id=1, source_target_pairs={{0,2},{1,3},{2,0},{3,1},{4,6},{5,7},{6,4},{7,5},{8,10},{9,11},{10,... | collective-permute-start | bytes 589832 | tf_op jit(solution)/shard_map/ppermute | solution.py:24
  27.7 10.6 %collective-permute-start.2 = (bf16[24,4096]{1,0:T(8,128)(2,1)S(1)}, bf16[24,4096]{1,0:T(8,128)(2,1)S(1)}, u32[]{:S(2)}, u32[]{:S(2)}) collective-permute-start(bf16[24,4096]{1,0:T(8,128)(2,1)S(1)} %pad_maximum_fusion.2), channel_id=1, source_target_pairs={{0,2},{1,3},{2,0},{3,1},{4,6},{5,7},{6,4},{7,5},{8,10},{9,11},{10,... | collective-permute-start | bytes 589832 | tf_op jit(solution)/shard_map/ppermute | solution.py:24
  29.6 8.7 %collective-permute-start.3 = (bf16[8,4096]{1,0:T(8,128)(2,1)S(1)}, bf16[8,4096]{1,0:T(8,128)(2,1)S(1)}, u32[]{:S(2)}, u32[]{:S(2)}) collective-permute-start(bf16[8,4096]{1,0:T(8,128)(2,1)S(1)} %add_convert_fusion.7), channel_id=1, source_target_pairs={{0,4},{1,5},{2,6},{3,7},{4,0},{5,1},{6,2},{7,3},{8,12},{9,13},{10,... | collective-permute-start | bytes 196616 | tf_op jit(solution)/shard_map/ppermute | solution.py:24
  38.4 47.6 %copy-start = (bf16[8192]{0:T(1024)(128)(2,1)S(1)}, bf16[8192]{0:T(1024)(128)(2,1)}, u32[]{:S(2)}) copy-start(bf16[8192]{0:T(1024)(128)(2,1)} %param.9) | copy-start | bytes 49156
  38.4 10.2 %collective-permute-start.5 = (bf16[16,4096]{1,0:T(8,128)(2,1)S(1)}, bf16[16,4096]{1,0:T(8,128)(2,1)S(1)}, u32[]{:S(2)}, u32[]{:S(2)}) collective-permute-start(bf16[16,4096]{1,0:T(8,128)(2,1)S(1)} %pad_maximum_fusion.5), channel_id=1, source_target_pairs={{0,4},{1,5},{2,6},{3,7},{4,0},{5,1},{6,2},{7,3},{8,12},{9,13},{10,... | collective-permute-start | bytes 393224 | tf_op jit(solution)/shard_map/ppermute | solution.py:24
  42.1 29.1 %collective-permute-start.6 = (bf16[8,4096]{1,0:T(8,128)(2,1)S(1)}, bf16[8,4096]{1,0:T(8,128)(2,1)S(1)}, u32[]{:S(2)}, u32[]{:S(2)}) collective-permute-start(bf16[8,4096]{1,0:T(8,128)(2,1)S(1)} %get-tuple-element.61), channel_id=1, source_target_pairs={{0,2},{1,3},{2,0},{3,1},{4,6},{5,7},{6,4},{7,5},{8,10},{9,11},{10,... | collective-permute-start | bytes 196616 | tf_op jit(solution)/shard_map/ppermute | solution.py:24
  44.0 27.2 %collective-permute-start.7 = (bf16[8,4096]{1,0:T(8,128)(2,1)S(1)}, bf16[8,4096]{1,0:T(8,128)(2,1)S(1)}, u32[]{:S(2)}, u32[]{:S(2)}) collective-permute-start(bf16[8,4096]{1,0:T(8,128)(2,1)S(1)} %get-tuple-element.62), channel_id=1, source_target_pairs={{0,4},{1,5},{2,6},{3,7},{4,0},{5,1},{6,2},{7,3},{8,12},{9,13},{10,... | collective-permute-start | bytes 196616 | tf_op jit(solution)/shard_map/ppermute | solution.py:24
  46.6 8.9 %collective-permute-start.9 = (bf16[8,4096]{1,0:T(8,128)(2,1)S(1)}, bf16[8,4096]{1,0:T(8,128)(2,1)S(1)}, u32[]{:S(2)}, u32[]{:S(2)}) collective-permute-start(bf16[8,4096]{1,0:T(8,128)(2,1)S(1)} %add_convert_fusion.4), channel_id=1, source_target_pairs={{0,8},{1,9},{2,10},{3,11},{4,12},{5,13},{6,14},{7,15},{8,0},{9,1},... | collective-permute-start | bytes 196616 | tf_op jit(solution)/shard_map/ppermute | solution.py:24
  55.6 15.7 %collective-permute-start.10 = (bf16[8,4096]{1,0:T(8,128)(2,1)S(1)}, bf16[8,4096]{1,0:T(8,128)(2,1)S(1)}, u32[]{:S(2)}, u32[]{:S(2)}) collective-permute-start(bf16[8,4096]{1,0:T(8,128)(2,1)S(1)} %add_convert_fusion), channel_id=1, source_target_pairs={{0,16},{1,17},{2,18},{3,19},{4,20},{5,21},{6,22},{7,23},{8,24},{9,... | collective-permute-start | bytes 196616 | tf_op jit(solution)/shard_map/ppermute | solution.py:24
  65.5 9.4 %collective-permute-start.8 = (bf16[8,4096]{1,0:T(8,128)(2,1)S(1)}, bf16[8,4096]{1,0:T(8,128)(2,1)S(1)}, u32[]{:S(2)}, u32[]{:S(2)}) collective-permute-start(bf16[8,4096]{1,0:T(8,128)(2,1)S(1)} %add_convert_fusion.1), channel_id=1, source_target_pairs={{0,8},{1,9},{2,10},{3,11},{4,12},{5,13},{6,14},{7,15},{8,0},{9,1},... | collective-permute-start | bytes 196616 | tf_op jit(solution)/shard_map/ppermute | solution.py:24
  74.9 11.3 %collective-permute-start.11 = (bf16[8,4096]{1,0:T(8,128)(2,1)S(1)}, bf16[8,4096]{1,0:T(8,128)(2,1)S(1)}, u32[]{:S(2)}, u32[]{:S(2)}) collective-permute-start(bf16[8,4096]{1,0:T(8,128)(2,1)S(1)} %reduce-precision_convert_fusion.own), channel_id=1, source_target_pairs={{0,1},{1,0},{2,3},{3,2},{4,5},{5,4},{6,7},{7,6},{8,9},{9,8},{10,11... | collective-permute-start | bytes 196616 | tf_op jit(solution)/shard_map/ppermute | solution.py:28
  87.0 18.2 %collective-permute-start.12 = (bf16[8,4224]{1,0:T(8,128)(2,1)S(1)}, bf16[8,4224]{1,0:T(8,128)(2,1)S(1)}, u32[]{:S(2)}, u32[]{:S(2)}) collective-permute-start(bf16[8,4224]{1,0:T(8,128)(2,1)S(1)} %get-tuple-element.67), channel_id=1, source_target_pairs={{0,32},{1,33},{2,34},{3,35},{4,36},{5,37},{6,38},{7,39},{8,40},{9,... | collective-permute-start | bytes 202760 | tf_op jit(solution)/shard_map/ppermute | solution.py:37
  105.2 22.0 %collective-permute-start.15 = (bf16[8,4224]{1,0:T(8,128)(2,1)S(1)}, bf16[8,4224]{1,0:T(8,128)(2,1)S(1)}, u32[]{:S(2)}, u32[]{:S(2)}) collective-permute-start(bf16[8,4224]{1,0:T(8,128)(2,1)S(1)} %get-tuple-element.83), channel_id=1, source_target_pairs={{0,16},{1,17},{2,18},{3,19},{4,20},{5,21},{6,22},{7,23},{8,24},{9,... | collective-permute-start | bytes 202760 | tf_op jit(solution)/shard_map/ppermute | solution.py:24
  121.4 11.7 %collective-permute-start.16 = (bf16[8,4224]{1,0:T(8,128)(2,1)S(1)}, bf16[8,4224]{1,0:T(8,128)(2,1)S(1)}, u32[]{:S(2)}, u32[]{:S(2)}) collective-permute-start(bf16[8,4224]{1,0:T(8,128)(2,1)S(1)} %get-tuple-element.83), channel_id=1, source_target_pairs={{0,8},{1,9},{2,10},{3,11},{4,12},{5,13},{6,14},{7,15},{8,0},{9,1},... | collective-permute-start | bytes 202760 | tf_op jit(solution)/shard_map/ppermute | solution.py:24
  123.3 11.7 %collective-permute-start.14 = (bf16[8,4224]{1,0:T(8,128)(2,1)S(1)}, bf16[8,4224]{1,0:T(8,128)(2,1)S(1)}, u32[]{:S(2)}, u32[]{:S(2)}) collective-permute-start(bf16[8,4224]{1,0:T(8,128)(2,1)S(1)} %get-tuple-element.83), channel_id=1, source_target_pairs={{0,4},{1,5},{2,6},{3,7},{4,0},{5,1},{6,2},{7,3},{8,12},{9,13},{10,... | collective-permute-start | bytes 202760 | tf_op jit(solution)/shard_map/ppermute | solution.py:24
  125.3 17.7 %collective-permute-start.13 = (bf16[8,4224]{1,0:T(8,128)(2,1)S(1)}, bf16[8,4224]{1,0:T(8,128)(2,1)S(1)}, u32[]{:S(2)}, u32[]{:S(2)}) collective-permute-start(bf16[8,4224]{1,0:T(8,128)(2,1)S(1)} %get-tuple-element.83), channel_id=1, source_target_pairs={{0,2},{1,3},{2,0},{3,1},{4,6},{5,7},{6,4},{7,5},{8,10},{9,11},{10,... | collective-permute-start | bytes 202760 | tf_op jit(solution)/shard_map/ppermute | solution.py:24
  133.0 25.0 %collective-permute-start.18 = (bf16[16,4224]{1,0:T(8,128)(2,1)S(1)}, bf16[16,4224]{1,0:T(8,128)(2,1)S(1)}, u32[]{:S(2)}, u32[]{:S(2)}) collective-permute-start(bf16[16,4224]{1,0:T(8,128)(2,1)S(1)} %pad_maximum_fusion.4), channel_id=1, source_target_pairs={{0,4},{1,5},{2,6},{3,7},{4,0},{5,1},{6,2},{7,3},{8,12},{9,13},{10,... | collective-permute-start | bytes 405512 | tf_op jit(solution)/shard_map/ppermute | solution.py:24
  135.0 25.0 %collective-permute-start.17 = (bf16[24,4224]{1,0:T(8,128)(2,1)S(1)}, bf16[24,4224]{1,0:T(8,128)(2,1)S(1)}, u32[]{:S(2)}, u32[]{:S(2)}) collective-permute-start(bf16[24,4224]{1,0:T(8,128)(2,1)S(1)} %pad_maximum_fusion), channel_id=1, source_target_pairs={{0,2},{1,3},{2,0},{3,1},{4,6},{5,7},{6,4},{7,5},{8,10},{9,11},{10,... | collective-permute-start | bytes 608264 | tf_op jit(solution)/shard_map/ppermute | solution.py:24
  136.9 9.0 %collective-permute-start.19 = (bf16[8,4224]{1,0:T(8,128)(2,1)S(1)}, bf16[8,4224]{1,0:T(8,128)(2,1)S(1)}, u32[]{:S(2)}, u32[]{:S(2)}) collective-permute-start(bf16[8,4224]{1,0:T(8,128)(2,1)S(1)} %collective-permute-done.15), channel_id=1, source_target_pairs={{0,8},{1,9},{2,10},{3,11},{4,12},{5,13},{6,14},{7,15},{8,0},{9,1},... | collective-permute-start | bytes 202760 | tf_op jit(solution)/shard_map/ppermute | solution.py:24
  146.0 6.2 %collective-permute-start.21 = (bf16[8,4224]{1,0:T(8,128)(2,1)S(1)}, bf16[8,4224]{1,0:T(8,128)(2,1)S(1)}, u32[]{:S(2)}, u32[]{:S(2)}) collective-permute-start(bf16[8,4224]{1,0:T(8,128)(2,1)S(1)} %collective-permute-done.19), channel_id=1, source_target_pairs={{0,4},{1,5},{2,6},{3,7},{4,0},{5,1},{6,2},{7,3},{8,12},{9,13},{10,... | collective-permute-start | bytes 202760 | tf_op jit(solution)/shard_map/ppermute | solution.py:24
  152.1 13.3 %collective-permute-start.22 = (bf16[8,4224]{1,0:T(8,128)(2,1)S(1)}, bf16[8,4224]{1,0:T(8,128)(2,1)S(1)}, u32[]{:S(2)}, u32[]{:S(2)}) collective-permute-start(bf16[8,4224]{1,0:T(8,128)(2,1)S(1)} %collective-permute-done.21), channel_id=1, source_target_pairs={{0,2},{1,3},{2,0},{3,1},{4,6},{5,7},{6,4},{7,5},{8,10},{9,11},{10,... | collective-permute-start | bytes 202760 | tf_op jit(solution)/shard_map/ppermute | solution.py:24
  158.1 7.2 %collective-permute-start.20 = (bf16[24,4224]{1,0:T(8,128)(2,1)S(1)}, bf16[24,4224]{1,0:T(8,128)(2,1)S(1)}, u32[]{:S(2)}, u32[]{:S(2)}) collective-permute-start(bf16[24,4224]{1,0:T(8,128)(2,1)S(1)} %pad_maximum_fusion.1), channel_id=1, source_target_pairs={{0,2},{1,3},{2,0},{3,1},{4,6},{5,7},{6,4},{7,5},{8,10},{9,11},{10,... | collective-permute-start | bytes 608264 | tf_op jit(solution)/shard_map/ppermute | solution.py:24
  165.5 8.2 %collective-permute-start.23 = (bf16[128,4224]{1,0:T(8,128)(2,1)S(1)}, bf16[128,4224]{1,0:T(8,128)(2,1)S(1)}, u32[]{:S(2)}, u32[]{:S(2)}) collective-permute-start(bf16[128,4224]{1,0:T(8,128)(2,1)S(1)} %constant_dynamic-update-slice_fusion.a.twin), channel_id=1, source_target_pairs={{0,1},{1,0},{2,3},{3,2},{4,5},{5,4},{6,7},{7,6},{8,9},{9,8},{10,11... | collective-permute-start | bytes 3244040 | tf_op jit(solution)/shard_map/ppermute | solution.py:28

commit v4 on v3

--- a/solution.py
+++ b/solution.py
@@ -228,7 +228,7 @@
     a15 = across(out15, 1)
     out13, kept, incoming = apart(packed(block(13), block(11), block(7)), kept, incoming)
     a13 = across(out13, 1)
-    out9, kept, incoming = apart(packed(block(9), block(5), block(3)), kept, incoming)
+    out9, kept, incoming = apart(packed(block(9), block(5), block(3), block(1)), kept, incoming)
     a9 = across(out9, 1)
     out14, kept, incoming = apart(packed(block(14) + a15.astype(f32)), kept, incoming)
     a14 = across(out14, 2)
@@ -239,18 +239,17 @@
     a10 = across(out10, 2)
     out12, kept, incoming = apart(packed(block(12) + b13.astype(f32) + a14.astype(f32)), kept, incoming)
     a12 = across(out12, 4)
-    c9, c5, c3 = split(a9)
-    out1, out2, c9, c5, kept, incoming = apart(
-        packed(block(1)), packed(block(2) + c3.astype(f32)), c9, c5, kept, incoming
-    )
-    a1 = across(out1, 1)
-    a2 = across(out2, 2)
+    c9, c5, c3, a1 = split(a9)
     c10, c6 = split(a10)
     out4, c9, c10, kept, incoming = apart(
         packed(block(4) + c5.astype(f32) + c6.astype(f32)), c9, c10, kept, incoming
     )
     a4 = across(out4, 4)
-    a8 = across(packed(block(8) + c9.astype(f32) + c10.astype(f32) + a12.astype(f32)), 8)
+    out8, c3, kept, incoming = apart(
+        packed(block(8) + c9.astype(f32) + c10.astype(f32) + a12.astype(f32)), c3, kept, incoming
+    )
+    a8 = across(out8, 8)
+    a2 = across(packed(block(2) + c3.astype(f32)), 2)
     return block(0) + a1.astype(f32) + a2.astype(f32) + a4.astype(f32) + a8.astype(f32)
 
 

time: 177 us -> 173 us (0.977)
  starting transfers between devices: 113 us -> 100 us
  waiting for transfers between devices: 47.5 us -> 56.5 us
    ppermute x20 -> x19, waiting for transfers between devices: 33.1 us -> 42.1 us  [across(): return lax.ppermute(x, 'tp', [(i, i ^ 2 * d) for i in range(TP)])]
    ppermute x20 -> x19, starting transfers between devices: 78.7 us -> 71.4 us  [across(): return lax.ppermute(x, 'tp', [(i, i ^ 2 * d) for i in range(TP)])]
    ppermute x3, starting transfers between devices: 32.4 us -> 26.8 us  [other_core(): return lax.ppermute(x, 'tp', [(i, i ^ 1) for i in range(TP)])]
  transfers between devices with their start and end apart: 24 -> 23, of which waited for: 11 -> 12; matrix products, arithmetic and copies ran while one was open for 1% -> 1% of each run, Pallas kernels for 4% -> 4%
where the time goes in v4:
time: 173 us; the launch traced here: 172 us
  starting transfers between devices  100 us (58%)
  waiting for transfers between devices  56.5 us (33%)
  Pallas kernels  11.9 us (7%)
  between operations  1.81 us (1%)
    ppermute x19, starting transfers between devices, across(): return lax.ppermute(x, 'tp', [(i, i ^ 2 * d) for i in range(TP)])  71.4 us
    ppermute x19, waiting for transfers between devices, across(): return lax.ppermute(x, 'tp', [(i, i ^ 2 * d) for i in range(TP)])  42.1 us
    ppermute x3, starting transfers between devices, other_core(): return lax.ppermute(x, 'tp', [(i, i ^ 1) for i in range(TP)])  26.8 us
    ppermute x1, waiting for transfers between devices, next_section(): return lax.ppermute(x, ('section', 'tp'), pairs)  13.9 us
    pallas_call x2, Pallas kernels, out_proj(): pl.pallas_call(out_proj_body, out_shape=jax.ShapeDtypeStruct((TOK, HALF),...  5.4 us
  transfers between devices with their start and end apart: 23, of which 12 were waited for; matrix products, arithmetic and copies ran while one was open for 1% of the time, Pallas kernels for 4%

profile of v4, /device:TPU:1, one launch (start us, length us, event | category | flops | bytes accessed | tf_op | source)
XLA Modules:
  0.0 171.8 jit_solution(8816326146824082258)
XLA Ops:
  0.7 0.1 pad_add_fusion.ids
  0.7 2.7 %out_proj.3 = bf16[128,4096]{1,0:T(8,128)(2,1)S(1)} custom-call(s32[4]{0:T(128)S(1)} %pad_add_fusion.ids, bf16[128,256]{1,0:T(8,128)(2,1)} %bitcast.15, bf16[256,8192]{1,0:T(8,128)(2,1)} %weight.3, bf16[4,8192]{1,0:T(4,128)(2,1)} %bitcast.17), custom_call_target="tpu_custom_call" | custom-call | tf_op jit(solution)/shard_map/out_proj/pallas_call | solution.py:67
  3.4 16.0 %collective-permute-start = (bf16[128,4096]{1,0:T(8,128)(2,1)S(1)}, bf16[128,4096]{1,0:T(8,128)(2,1)S(1)}, u32[]{:S(2)}, u32[]{:S(2)}) collective-permute-start(bf16[128,4096]{1,0:T(8,128)(2,1)S(1)} %out_proj.3), channel_id=1, source_target_pairs={{0,1},{1,0},{2,3},{3,2},{4,5},{5,4},{6,7},{7,6},{8,9},{9,8},{10,11... | collective-permute-start | bytes 3145736 | tf_op jit(solution)/shard_map/ppermute | solution.py:28
  19.4 2.7 %out_proj.2 = f32[128,4096]{1,0:T(8,128)S(1)} custom-call(s32[4]{0:T(128)S(1)} %pad_add_fusion.ids, bf16[128,256]{1,0:T(8,128)(2,1)} %bitcast.16, bf16[256,8192]{1,0:T(8,128)(2,1)} %weight.3, bf16[4,8192]{1,0:T(4,128)(2,1)} %bitcast.18), custom_call_target="tpu_custom_call" | custom-call | tf_op jit(solution)/shard_map/out_proj/pallas_call | solution.py:67
  22.2 0.0 collective-permute-done
  22.2 1.9 %collective-permute-start.1 = (bf16[8,4096]{1,0:T(8,128)(2,1)S(1)}, bf16[8,4096]{1,0:T(8,128)(2,1)S(1)}, u32[]{:S(2)}, u32[]{:S(2)}) collective-permute-start(bf16[8,4096]{1,0:T(8,128)(2,1)S(1)} %fusion), channel_id=1, source_target_pairs={{0,2},{1,3},{2,0},{3,1},{4,6},{5,7},{6,4},{7,5},{8,10},{9,11},{10,... | collective-permute-start | bytes 196616 | tf_op jit(solution)/shard_map/ppermute | solution.py:24
  24.2 3.4 %collective-permute-start.2 = (bf16[24,4096]{1,0:T(8,128)(2,1)S(1)}, bf16[24,4096]{1,0:T(8,128)(2,1)S(1)}, u32[]{:S(2)}, u32[]{:S(2)}) collective-permute-start(bf16[24,4096]{1,0:T(8,128)(2,1)S(1)} %pad_maximum_fusion.3), channel_id=1, source_target_pairs={{0,2},{1,3},{2,0},{3,1},{4,6},{5,7},{6,4},{7,5},{8,10},{9,11},{10,... | collective-permute-start | bytes 589832 | tf_op jit(solution)/shard_map/ppermute | solution.py:24
  27.7 1.9 %collective-permute-start.4 = (bf16[32,4096]{1,0:T(8,128)(2,1)S(1)}, bf16[32,4096]{1,0:T(8,128)(2,1)S(1)}, u32[]{:S(2)}, u32[]{:S(2)}) collective-permute-start(bf16[32,4096]{1,0:T(8,128)(2,1)S(1)} %pad_maximum_fusion), channel_id=1, source_target_pairs={{0,2},{1,3},{2,0},{3,1},{4,6},{5,7},{6,4},{7,5},{8,10},{9,11},{10,... | collective-permute-start | bytes 786440 | tf_op jit(solution)/shard_map/ppermute | solution.py:24
  29.6 0.0 collective-permute-done.1
  29.6 1.9 %collective-permute-start.3 = (bf16[8,4096]{1,0:T(8,128)(2,1)S(1)}, bf16[8,4096]{1,0:T(8,128)(2,1)S(1)}, u32[]{:S(2)}, u32[]{:S(2)}) collective-permute-start(bf16[8,4096]{1,0:T(8,128)(2,1)S(1)} %add_convert_fusion.6), channel_id=1, source_target_pairs={{0,4},{1,5},{2,6},{3,7},{4,0},{5,1},{6,2},{7,3},{8,12},{9,13},{10,... | collective-permute-start | bytes 196616 | tf_op jit(solution)/shard_map/ppermute | solution.py:24
  31.6 1.0 collective-permute-done.2
  32.6 5.9 %collective-permute-done.3 = bf16[8,4096]{1,0:T(8,128)(2,1)S(1)} collective-permute-done((bf16[8,4096]{1,0:T(8,128)(2,1)S(1)}, bf16[8,4096]{1,0:T(8,128)(2,1)S(1)}, u32[]{:S(2)}, u32[]{:S(2)}) %collective-permute-start.3) | collective-permute-done | bytes 65568 | tf_op jit(solution)/shard_map/ppermute | solution.py:24
  38.6 0.0 copy-start
  38.6 1.9 %collective-permute-start.6 = (bf16[8,4096]{1,0:T(8,128)(2,1)S(1)}, bf16[8,4096]{1,0:T(8,128)(2,1)S(1)}, u32[]{:S(2)}, u32[]{:S(2)}) collective-permute-start(bf16[8,4096]{1,0:T(8,128)(2,1)S(1)} %add_convert_fusion.3), channel_id=1, source_target_pairs={{0,8},{1,9},{2,10},{3,11},{4,12},{5,13},{6,14},{7,15},{8,0},{9,1},... | collective-permute-start | bytes 196616 | tf_op jit(solution)/shard_map/ppermute | solution.py:24
  40.5 4.7 %collective-permute-start.5 = (bf16[16,4096]{1,0:T(8,128)(2,1)S(1)}, bf16[16,4096]{1,0:T(8,128)(2,1)S(1)}, u32[]{:S(2)}, u32[]{:S(2)}) collective-permute-start(bf16[16,4096]{1,0:T(8,128)(2,1)S(1)} %pad_maximum_fusion.5), channel_id=1, source_target_pairs={{0,4},{1,5},{2,6},{3,7},{4,0},{5,1},{6,2},{7,3},{8,12},{9,13},{10,... | collective-permute-start | bytes 393224 | tf_op jit(solution)/shard_map/ppermute | solution.py:24
  45.3 0.0 collective-permute-done.4
  45.3 8.8 %collective-permute-done.5 = bf16[16,4096]{1,0:T(8,128)(2,1)S(1)} collective-permute-done((bf16[16,4096]{1,0:T(8,128)(2,1)S(1)}, bf16[16,4096]{1,0:T(8,128)(2,1)S(1)}, u32[]{:S(2)}, u32[]{:S(2)}) %collective-permute-start.5) | collective-permute-done | bytes 131104 | tf_op jit(solution)/shard_map/ppermute | solution.py:24
  54.2 0.0 collective-permute-done.6
  54.3 1.9 %collective-permute-start.7 = (bf16[8,4096]{1,0:T(8,128)(2,1)S(1)}, bf16[8,4096]{1,0:T(8,128)(2,1)S(1)}, u32[]{:S(2)}, u32[]{:S(2)}) collective-permute-start(bf16[8,4096]{1,0:T(8,128)(2,1)S(1)} %add_convert_fusion), channel_id=1, source_target_pairs={{0,4},{1,5},{2,6},{3,7},{4,0},{5,1},{6,2},{7,3},{8,12},{9,13},{10,... | collective-permute-start | bytes 196616 | tf_op jit(solution)/shard_map/ppermute | solution.py:24
  56.2 6.3 %collective-permute-start.9 = (bf16[8,4096]{1,0:T(8,128)(2,1)S(1)}, bf16[8,4096]{1,0:T(8,128)(2,1)S(1)}, u32[]{:S(2)}, u32[]{:S(2)}) collective-permute-start(bf16[8,4096]{1,0:T(8,128)(2,1)S(1)} %add_convert_fusion.1), channel_id=1, source_target_pairs={{0,16},{1,17},{2,18},{3,19},{4,20},{5,21},{6,22},{7,23},{8,24},{9,... | collective-permute-start | bytes 196616 | tf_op jit(solution)/shard_map/ppermute | solution.py:24
  62.5 3.2 %collective-permute-start.8 = (bf16[8,4096]{1,0:T(8,128)(2,1)S(1)}, bf16[8,4096]{1,0:T(8,128)(2,1)S(1)}, u32[]{:S(2)}, u32[]{:S(2)}) collective-permute-start(bf16[8,4096]{1,0:T(8,128)(2,1)S(1)} %add_convert_fusion.2), channel_id=1, source_target_pairs={{0,8},{1,9},{2,10},{3,11},{4,12},{5,13},{6,14},{7,15},{8,0},{9,1},... | collective-permute-start | bytes 196616 | tf_op jit(solution)/shard_map/ppermute | solution.py:24
  65.7 0.0 collective-permute-done.7
  65.7 13.6 %collective-permute-done.9 = bf16[8,4096]{1,0:T(8,128)(2,1)S(1)} collective-permute-done((bf16[8,4096]{1,0:T(8,128)(2,1)S(1)}, bf16[8,4096]{1,0:T(8,128)(2,1)S(1)}, u32[]{:S(2)}, u32[]{:S(2)}) %collective-permute-start.9) | collective-permute-done | bytes 65568 | tf_op jit(solution)/shard_map/ppermute | solution.py:24
  79.3 0.0 collective-permute-done.8
  79.3 0.1 reduce-precision_convert_fusion.own
  79.4 2.6 %collective-permute-start.10 = (bf16[8,4096]{1,0:T(8,128)(2,1)S(1)}, bf16[8,4096]{1,0:T(8,128)(2,1)S(1)}, u32[]{:S(2)}, u32[]{:S(2)}) collective-permute-start(bf16[8,4096]{1,0:T(8,128)(2,1)S(1)} %reduce-precision_convert_fusion.own), channel_id=1, source_target_pairs={{0,1},{1,0},{2,3},{3,2},{4,5},{5,4},{6,7},{7,6},{8,9},{9,8},{10,11... | collective-permute-start | bytes 196616 | tf_op jit(solution)/shard_map/ppermute | solution.py:28
  82.6 0.0 copy-done
  82.7 0.2 collective-permute-done.10.twin
  82.9 0.8 cast.1
  83.6 1.9 %collective-permute-start.11 = (bf16[8,4224]{1,0:T(8,128)(2,1)S(1)}, bf16[8,4224]{1,0:T(8,128)(2,1)S(1)}, u32[]{:S(2)}, u32[]{:S(2)}) collective-permute-start(bf16[8,4224]{1,0:T(8,128)(2,1)S(1)} %get-tuple-element.63), channel_id=1, source_target_pairs={{0,32},{1,33},{2,34},{3,35},{4,36},{5,37},{6,38},{7,39},{8,40},{9,... | collective-permute-start | bytes 202760 | tf_op jit(solution)/shard_map/ppermute | solution.py:37
  85.6 2.3 %prefetch.1.weight = bf16[288,8192]{1,0:T(8,128)(2,1)S(1)} custom-call(bf16[288,8192]{1,0:T(8,128)(2,1)} %bitcast.14), custom_call_target="tpu_custom_call" | custom-call | tf_op jit(solution)/shard_map/prefetch/pallas_call | solution.py:136
  87.9 13.9 %collective-permute-done.11.arrived = bf16[8,4224]{1,0:T(8,128)(2,1)S(1)} collective-permute-done((bf16[8,4224]{1,0:T(8,128)(2,1)S(1)}, bf16[8,4224]{1,0:T(8,128)(2,1)S(1)}, u32[]{:S(2)}, u32[]{:S(2)}) %collective-permute-start.11) | collective-permute-done | bytes 67616 | tf_op jit(solution)/shard_map/ppermute | solution.py:37
  101.9 16.1 %collective-permute-start.14 = (bf16[8,4224]{1,0:T(8,128)(2,1)S(1)}, bf16[8,4224]{1,0:T(8,128)(2,1)S(1)}, u32[]{:S(2)}, u32[]{:S(2)}) collective-permute-start(bf16[8,4224]{1,0:T(8,128)(2,1)S(1)} %get-tuple-element.78), channel_id=1, source_target_pairs={{0,16},{1,17},{2,18},{3,19},{4,20},{5,21},{6,22},{7,23},{8,24},{9,... | collective-permute-start | bytes 202760 | tf_op jit(solution)/shard_map/ppermute | solution.py:24
  117.9 1.9 %collective-permute-start.15 = (bf16[8,4224]{1,0:T(8,128)(2,1)S(1)}, bf16[8,4224]{1,0:T(8,128)(2,1)S(1)}, u32[]{:S(2)}, u32[]{:S(2)}) collective-permute-start(bf16[8,4224]{1,0:T(8,128)(2,1)S(1)} %get-tuple-element.78), channel_id=1, source_target_pairs={{0,8},{1,9},{2,10},{3,11},{4,12},{5,13},{6,14},{7,15},{8,0},{9,1},... | collective-permute-start | bytes 202760 | tf_op jit(solution)/shard_map/ppermute | solution.py:24
  119.9 1.9 %collective-permute-start.13 = (bf16[8,4224]{1,0:T(8,128)(2,1)S(1)}, bf16[8,4224]{1,0:T(8,128)(2,1)S(1)}, u32[]{:S(2)}, u32[]{:S(2)}) collective-permute-start(bf16[8,4224]{1,0:T(8,128)(2,1)S(1)} %get-tuple-element.78), channel_id=1, source_target_pairs={{0,4},{1,5},{2,6},{3,7},{4,0},{5,1},{6,2},{7,3},{8,12},{9,13},{10,... | collective-permute-start | bytes 202760 | tf_op jit(solution)/shard_map/ppermute | solution.py:24
  121.8 2.6 %collective-permute-start.12 = (bf16[8,4224]{1,0:T(8,128)(2,1)S(1)}, bf16[8,4224]{1,0:T(8,128)(2,1)S(1)}, u32[]{:S(2)}, u32[]{:S(2)}) collective-permute-start(bf16[8,4224]{1,0:T(8,128)(2,1)S(1)} %get-tuple-element.78), channel_id=1, source_target_pairs={{0,2},{1,3},{2,0},{3,1},{4,6},{5,7},{6,4},{7,5},{8,10},{9,11},{10,... | collective-permute-start | bytes 202760 | tf_op jit(solution)/shard_map/ppermute | solution.py:24
  124.4 0.0 collective-permute-done.14
  124.4 2.8 %collective-permute-done.15 = bf16[8,4224]{1,0:T(8,128)(2,1)S(1)} collective-permute-done((bf16[8,4224]{1,0:T(8,128)(2,1)S(1)}, bf16[8,4224]{1,0:T(8,128)(2,1)S(1)}, u32[]{:S(2)}, u32[]{:S(2)}) %collective-permute-start.15) | collective-permute-done | bytes 67616 | tf_op jit(solution)/shard_map/ppermute | solution.py:24
  127.3 1.9 %collective-permute-start.17 = (bf16[16,4224]{1,0:T(8,128)(2,1)S(1)}, bf16[16,4224]{1,0:T(8,128)(2,1)S(1)}, u32[]{:S(2)}, u32[]{:S(2)}) collective-permute-start(bf16[16,4224]{1,0:T(8,128)(2,1)S(1)} %pad_maximum_fusion.4), channel_id=1, source_target_pairs={{0,4},{1,5},{2,6},{3,7},{4,0},{5,1},{6,2},{7,3},{8,12},{9,13},{10,... | collective-permute-start | bytes 405512 | tf_op jit(solution)/shard_map/ppermute | solution.py:24
  129.2 0.6 collective-permute-done.13
  129.8 1.9 %collective-permute-start.16 = (bf16[24,4224]{1,0:T(8,128)(2,1)S(1)}, bf16[24,4224]{1,0:T(8,128)(2,1)S(1)}, u32[]{:S(2)}, u32[]{:S(2)}) collective-permute-start(bf16[24,4224]{1,0:T(8,128)(2,1)S(1)} %pad_maximum_fusion.1), channel_id=1, source_target_pairs={{0,2},{1,3},{2,0},{3,1},{4,6},{5,7},{6,4},{7,5},{8,10},{9,11},{10,... | collective-permute-start | bytes 608264 | tf_op jit(solution)/shard_map/ppermute | solution.py:24
  131.8 7.0 %collective-permute-start.18 = (bf16[8,4224]{1,0:T(8,128)(2,1)S(1)}, bf16[8,4224]{1,0:T(8,128)(2,1)S(1)}, u32[]{:S(2)}, u32[]{:S(2)}) collective-permute-start(bf16[8,4224]{1,0:T(8,128)(2,1)S(1)} %collective-permute-done.14), channel_id=1, source_target_pairs={{0,8},{1,9},{2,10},{3,11},{4,12},{5,13},{6,14},{7,15},{8,0},{9,1},... | collective-permute-start | bytes 202760 | tf_op jit(solution)/shard_map/ppermute | solution.py:24
  138.7 0.0 collective-permute-done.12
  138.8 2.0 %collective-permute-done.18 = bf16[8,4224]{1,0:T(8,128)(2,1)S(1)} collective-permute-done((bf16[8,4224]{1,0:T(8,128)(2,1)S(1)}, bf16[8,4224]{1,0:T(8,128)(2,1)S(1)}, u32[]{:S(2)}, u32[]{:S(2)}) %collective-permute-start.18) | collective-permute-done | bytes 67616 | tf_op jit(solution)/shard_map/ppermute | solution.py:24
  140.8 3.6 %collective-permute-start.20 = (bf16[8,4224]{1,0:T(8,128)(2,1)S(1)}, bf16[8,4224]{1,0:T(8,128)(2,1)S(1)}, u32[]{:S(2)}, u32[]{:S(2)}) collective-permute-start(bf16[8,4224]{1,0:T(8,128)(2,1)S(1)} %collective-permute-done.18), channel_id=1, source_target_pairs={{0,4},{1,5},{2,6},{3,7},{4,0},{5,1},{6,2},{7,3},{8,12},{9,13},{10,... | collective-permute-start | bytes 202760 | tf_op jit(solution)/shard_map/ppermute | solution.py:24
  144.5 2.3 %collective-permute-done.20 = bf16[8,4224]{1,0:T(8,128)(2,1)S(1)} collective-permute-done((bf16[8,4224]{1,0:T(8,128)(2,1)S(1)}, bf16[8,4224]{1,0:T(8,128)(2,1)S(1)}, u32[]{:S(2)}, u32[]{:S(2)}) %collective-permute-start.20) | collective-permute-done | bytes 67616 | tf_op jit(solution)/shard_map/ppermute | solution.py:24
  146.8 5.3 %collective-permute-start.21 = (bf16[8,4224]{1,0:T(8,128)(2,1)S(1)}, bf16[8,4224]{1,0:T(8,128)(2,1)S(1)}, u32[]{:S(2)}, u32[]{:S(2)}) collective-permute-start(bf16[8,4224]{1,0:T(8,128)(2,1)S(1)} %collective-permute-done.20), channel_id=1, source_target_pairs={{0,2},{1,3},{2,0},{3,1},{4,6},{5,7},{6,4},{7,5},{8,10},{9,11},{10,... | collective-permute-start | bytes 202760 | tf_op jit(solution)/shard_map/ppermute | solution.py:24
  152.1 0.0 collective-permute-done.17
  152.2 1.9 %collective-permute-start.19 = (bf16[24,4224]{1,0:T(8,128)(2,1)S(1)}, bf16[24,4224]{1,0:T(8,128)(2,1)S(1)}, u32[]{:S(2)}, u32[]{:S(2)}) collective-permute-start(bf16[24,4224]{1,0:T(8,128)(2,1)S(1)} %pad_maximum_fusion.2), channel_id=1, source_target_pairs={{0,2},{1,3},{2,0},{3,1},{4,6},{5,7},{6,4},{7,5},{8,10},{9,11},{10,... | collective-permute-start | bytes 608264 | tf_op jit(solution)/shard_map/ppermute | solution.py:24
  154.1 0.0 collective-permute-done.16
  154.2 4.9 %collective-permute-done.19 = bf16[24,4224]{1,0:T(8,128)(2,1)S(1)} collective-permute-done((bf16[24,4224]{1,0:T(8,128)(2,1)S(1)}, bf16[24,4224]{1,0:T(8,128)(2,1)S(1)}, u32[]{:S(2)}, u32[]{:S(2)}) %collective-permute-start.19) | collective-permute-done | bytes 202784 | tf_op jit(solution)/shard_map/ppermute | solution.py:24
  159.2 0.0 collective-permute-done.21
  159.2 8.2 %collective-permute-start.22 = (bf16[128,4224]{1,0:T(8,128)(2,1)S(1)}, bf16[128,4224]{1,0:T(8,128)(2,1)S(1)}, u32[]{:S(2)}, u32[]{:S(2)}) collective-permute-start(bf16[128,4224]{1,0:T(8,128)(2,1)S(1)} %constant_dynamic-update-slice_fusion.a.twin), channel_id=1, source_target_pairs={{0,1},{1,0},{2,3},{3,2},{4,5},{5,4},{6,7},{7,6},{8,9},{9,8},{10,11... | collective-permute-start | bytes 3244040 | tf_op jit(solution)/shard_map/ppermute | solution.py:28
  167.5 0.7 maximum_select_fusion
  168.1 1.3 first_half.1.start
  169.5 0.3 collective-permute-done.22.a
  169.7 2.1 %second_half.1 = (bf16[288,128]{1,0:T(8,128)(2,1)}, f32[1]{0:T(128)}) custom-call(s32[4]{0:T(128)S(1)} %pad_add_fusion.ids, bf16[288,8192]{1,0:T(8,128)(2,1)S(1)} %prefetch.1.weight, bf16[128,4224]{1,0:T(8,128)(2,1)S(1)} %collective-permute-done.22.a, f32[288,128]{1,0:T(8,128)S(1)} %first_half.1.start, bf16[8,4224]{1,0:T(8,128)(2,1)S(1)} %collective-permute-done.11.arrived, ...), custom_call_target="tpu_custom_call" | custom-call | tf_op jit(solution)/shard_map/second_half/pallas_call | solution.py:193
  (38 shorter events, 0.7 us)
Async XLA Ops:
  3.4 18.8 %collective-permute-start = (bf16[128,4096]{1,0:T(8,128)(2,1)S(1)}, bf16[128,4096]{1,0:T(8,128)(2,1)S(1)}, u32[]{:S(2)}, u32[]{:S(2)}) collective-permute-start(bf16[128,4096]{1,0:T(8,128)(2,1)S(1)} %out_proj.3), channel_id=1, source_target_pairs={{0,1},{1,0},{2,3},{3,2},{4,5},{5,4},{6,7},{7,6},{8,9},{9,8},{10,11... | collective-permute-start | bytes 3145736 | tf_op jit(solution)/shard_map/ppermute | solution.py:28
  22.2 7.4 %collective-permute-start.1 = (bf16[8,4096]{1,0:T(8,128)(2,1)S(1)}, bf16[8,4096]{1,0:T(8,128)(2,1)S(1)}, u32[]{:S(2)}, u32[]{:S(2)}) collective-permute-start(bf16[8,4096]{1,0:T(8,128)(2,1)S(1)} %fusion), channel_id=1, source_target_pairs={{0,2},{1,3},{2,0},{3,1},{4,6},{5,7},{6,4},{7,5},{8,10},{9,11},{10,... | collective-permute-start | bytes 196616 | tf_op jit(solution)/shard_map/ppermute | solution.py:24
  24.2 8.3 %collective-permute-start.2 = (bf16[24,4096]{1,0:T(8,128)(2,1)S(1)}, bf16[24,4096]{1,0:T(8,128)(2,1)S(1)}, u32[]{:S(2)}, u32[]{:S(2)}) collective-permute-start(bf16[24,4096]{1,0:T(8,128)(2,1)S(1)} %pad_maximum_fusion.3), channel_id=1, source_target_pairs={{0,2},{1,3},{2,0},{3,1},{4,6},{5,7},{6,4},{7,5},{8,10},{9,11},{10,... | collective-permute-start | bytes 589832 | tf_op jit(solution)/shard_map/ppermute | solution.py:24
  27.7 17.6 %collective-permute-start.4 = (bf16[32,4096]{1,0:T(8,128)(2,1)S(1)}, bf16[32,4096]{1,0:T(8,128)(2,1)S(1)}, u32[]{:S(2)}, u32[]{:S(2)}) collective-permute-start(bf16[32,4096]{1,0:T(8,128)(2,1)S(1)} %pad_maximum_fusion), channel_id=1, source_target_pairs={{0,2},{1,3},{2,0},{3,1},{4,6},{5,7},{6,4},{7,5},{8,10},{9,11},{10,... | collective-permute-start | bytes 786440 | tf_op jit(solution)/shard_map/ppermute | solution.py:24
  29.6 8.9 %collective-permute-start.3 = (bf16[8,4096]{1,0:T(8,128)(2,1)S(1)}, bf16[8,4096]{1,0:T(8,128)(2,1)S(1)}, u32[]{:S(2)}, u32[]{:S(2)}) collective-permute-start(bf16[8,4096]{1,0:T(8,128)(2,1)S(1)} %add_convert_fusion.6), channel_id=1, source_target_pairs={{0,4},{1,5},{2,6},{3,7},{4,0},{5,1},{6,2},{7,3},{8,12},{9,13},{10,... | collective-permute-start | bytes 196616 | tf_op jit(solution)/shard_map/ppermute | solution.py:24
  38.6 44.0 %copy-start = (bf16[8192]{0:T(1024)(128)(2,1)S(1)}, bf16[8192]{0:T(1024)(128)(2,1)}, u32[]{:S(2)}) copy-start(bf16[8192]{0:T(1024)(128)(2,1)} %param.9) | copy-start | bytes 49156
  38.6 15.6 %collective-permute-start.6 = (bf16[8,4096]{1,0:T(8,128)(2,1)S(1)}, bf16[8,4096]{1,0:T(8,128)(2,1)S(1)}, u32[]{:S(2)}, u32[]{:S(2)}) collective-permute-start(bf16[8,4096]{1,0:T(8,128)(2,1)S(1)} %add_convert_fusion.3), channel_id=1, source_target_pairs={{0,8},{1,9},{2,10},{3,11},{4,12},{5,13},{6,14},{7,15},{8,0},{9,1},... | collective-permute-start | bytes 196616 | tf_op jit(solution)/shard_map/ppermute | solution.py:24
  40.5 13.6 %collective-permute-start.5 = (bf16[16,4096]{1,0:T(8,128)(2,1)S(1)}, bf16[16,4096]{1,0:T(8,128)(2,1)S(1)}, u32[]{:S(2)}, u32[]{:S(2)}) collective-permute-start(bf16[16,4096]{1,0:T(8,128)(2,1)S(1)} %pad_maximum_fusion.5), channel_id=1, source_target_pairs={{0,4},{1,5},{2,6},{3,7},{4,0},{5,1},{6,2},{7,3},{8,12},{9,13},{10,... | collective-permute-start | bytes 393224 | tf_op jit(solution)/shard_map/ppermute | solution.py:24
  54.3 11.5 %collective-permute-start.7 = (bf16[8,4096]{1,0:T(8,128)(2,1)S(1)}, bf16[8,4096]{1,0:T(8,128)(2,1)S(1)}, u32[]{:S(2)}, u32[]{:S(2)}) collective-permute-start(bf16[8,4096]{1,0:T(8,128)(2,1)S(1)} %add_convert_fusion), channel_id=1, source_target_pairs={{0,4},{1,5},{2,6},{3,7},{4,0},{5,1},{6,2},{7,3},{8,12},{9,13},{10,... | collective-permute-start | bytes 196616 | tf_op jit(solution)/shard_map/ppermute | solution.py:24
  56.2 23.1 %collective-permute-start.9 = (bf16[8,4096]{1,0:T(8,128)(2,1)S(1)}, bf16[8,4096]{1,0:T(8,128)(2,1)S(1)}, u32[]{:S(2)}, u32[]{:S(2)}) collective-permute-start(bf16[8,4096]{1,0:T(8,128)(2,1)S(1)} %add_convert_fusion.1), channel_id=1, source_target_pairs={{0,16},{1,17},{2,18},{3,19},{4,20},{5,21},{6,22},{7,23},{8,24},{9,... | collective-permute-start | bytes 196616 | tf_op jit(solution)/shard_map/ppermute | solution.py:24
  62.5 16.8 %collective-permute-start.8 = (bf16[8,4096]{1,0:T(8,128)(2,1)S(1)}, bf16[8,4096]{1,0:T(8,128)(2,1)S(1)}, u32[]{:S(2)}, u32[]{:S(2)}) collective-permute-start(bf16[8,4096]{1,0:T(8,128)(2,1)S(1)} %add_convert_fusion.2), channel_id=1, source_target_pairs={{0,8},{1,9},{2,10},{3,11},{4,12},{5,13},{6,14},{7,15},{8,0},{9,1},... | collective-permute-start | bytes 196616 | tf_op jit(solution)/shard_map/ppermute | solution.py:24
  79.4 3.5 %collective-permute-start.10 = (bf16[8,4096]{1,0:T(8,128)(2,1)S(1)}, bf16[8,4096]{1,0:T(8,128)(2,1)S(1)}, u32[]{:S(2)}, u32[]{:S(2)}) collective-permute-start(bf16[8,4096]{1,0:T(8,128)(2,1)S(1)} %reduce-precision_convert_fusion.own), channel_id=1, source_target_pairs={{0,1},{1,0},{2,3},{3,2},{4,5},{5,4},{6,7},{7,6},{8,9},{9,8},{10,11... | collective-permute-start | bytes 196616 | tf_op jit(solution)/shard_map/ppermute | solution.py:28
  83.6 18.2 %collective-permute-start.11 = (bf16[8,4224]{1,0:T(8,128)(2,1)S(1)}, bf16[8,4224]{1,0:T(8,128)(2,1)S(1)}, u32[]{:S(2)}, u32[]{:S(2)}) collective-permute-start(bf16[8,4224]{1,0:T(8,128)(2,1)S(1)} %get-tuple-element.63), channel_id=1, source_target_pairs={{0,32},{1,33},{2,34},{3,35},{4,36},{5,37},{6,38},{7,39},{8,40},{9,... | collective-permute-start | bytes 202760 | tf_op jit(solution)/shard_map/ppermute | solution.py:37
  101.9 22.6 %collective-permute-start.14 = (bf16[8,4224]{1,0:T(8,128)(2,1)S(1)}, bf16[8,4224]{1,0:T(8,128)(2,1)S(1)}, u32[]{:S(2)}, u32[]{:S(2)}) collective-permute-start(bf16[8,4224]{1,0:T(8,128)(2,1)S(1)} %get-tuple-element.78), channel_id=1, source_target_pairs={{0,16},{1,17},{2,18},{3,19},{4,20},{5,21},{6,22},{7,23},{8,24},{9,... | collective-permute-start | bytes 202760 | tf_op jit(solution)/shard_map/ppermute | solution.py:24
  117.9 9.3 %collective-permute-start.15 = (bf16[8,4224]{1,0:T(8,128)(2,1)S(1)}, bf16[8,4224]{1,0:T(8,128)(2,1)S(1)}, u32[]{:S(2)}, u32[]{:S(2)}) collective-permute-start(bf16[8,4224]{1,0:T(8,128)(2,1)S(1)} %get-tuple-element.78), channel_id=1, source_target_pairs={{0,8},{1,9},{2,10},{3,11},{4,12},{5,13},{6,14},{7,15},{8,0},{9,1},... | collective-permute-start | bytes 202760 | tf_op jit(solution)/shard_map/ppermute | solution.py:24
  119.9 9.9 %collective-permute-start.13 = (bf16[8,4224]{1,0:T(8,128)(2,1)S(1)}, bf16[8,4224]{1,0:T(8,128)(2,1)S(1)}, u32[]{:S(2)}, u32[]{:S(2)}) collective-permute-start(bf16[8,4224]{1,0:T(8,128)(2,1)S(1)} %get-tuple-element.78), channel_id=1, source_target_pairs={{0,4},{1,5},{2,6},{3,7},{4,0},{5,1},{6,2},{7,3},{8,12},{9,13},{10,... | collective-permute-start | bytes 202760 | tf_op jit(solution)/shard_map/ppermute | solution.py:24
  121.8 16.9 %collective-permute-start.12 = (bf16[8,4224]{1,0:T(8,128)(2,1)S(1)}, bf16[8,4224]{1,0:T(8,128)(2,1)S(1)}, u32[]{:S(2)}, u32[]{:S(2)}) collective-permute-start(bf16[8,4224]{1,0:T(8,128)(2,1)S(1)} %get-tuple-element.78), channel_id=1, source_target_pairs={{0,2},{1,3},{2,0},{3,1},{4,6},{5,7},{6,4},{7,5},{8,10},{9,11},{10,... | collective-permute-start | bytes 202760 | tf_op jit(solution)/shard_map/ppermute | solution.py:24
  127.3 24.9 %collective-permute-start.17 = (bf16[16,4224]{1,0:T(8,128)(2,1)S(1)}, bf16[16,4224]{1,0:T(8,128)(2,1)S(1)}, u32[]{:S(2)}, u32[]{:S(2)}) collective-permute-start(bf16[16,4224]{1,0:T(8,128)(2,1)S(1)} %pad_maximum_fusion.4), channel_id=1, source_target_pairs={{0,4},{1,5},{2,6},{3,7},{4,0},{5,1},{6,2},{7,3},{8,12},{9,13},{10,... | collective-permute-start | bytes 405512 | tf_op jit(solution)/shard_map/ppermute | solution.py:24
  129.8 24.3 %collective-permute-start.16 = (bf16[24,4224]{1,0:T(8,128)(2,1)S(1)}, bf16[24,4224]{1,0:T(8,128)(2,1)S(1)}, u32[]{:S(2)}, u32[]{:S(2)}) collective-permute-start(bf16[24,4224]{1,0:T(8,128)(2,1)S(1)} %pad_maximum_fusion.1), channel_id=1, source_target_pairs={{0,2},{1,3},{2,0},{3,1},{4,6},{5,7},{6,4},{7,5},{8,10},{9,11},{10,... | collective-permute-start | bytes 608264 | tf_op jit(solution)/shard_map/ppermute | solution.py:24
  131.8 9.0 %collective-permute-start.18 = (bf16[8,4224]{1,0:T(8,128)(2,1)S(1)}, bf16[8,4224]{1,0:T(8,128)(2,1)S(1)}, u32[]{:S(2)}, u32[]{:S(2)}) collective-permute-start(bf16[8,4224]{1,0:T(8,128)(2,1)S(1)} %collective-permute-done.14), channel_id=1, source_target_pairs={{0,8},{1,9},{2,10},{3,11},{4,12},{5,13},{6,14},{7,15},{8,0},{9,1},... | collective-permute-start | bytes 202760 | tf_op jit(solution)/shard_map/ppermute | solution.py:24
  140.8 6.0 %collective-permute-start.20 = (bf16[8,4224]{1,0:T(8,128)(2,1)S(1)}, bf16[8,4224]{1,0:T(8,128)(2,1)S(1)}, u32[]{:S(2)}, u32[]{:S(2)}) collective-permute-start(bf16[8,4224]{1,0:T(8,128)(2,1)S(1)} %collective-permute-done.18), channel_id=1, source_target_pairs={{0,4},{1,5},{2,6},{3,7},{4,0},{5,1},{6,2},{7,3},{8,12},{9,13},{10,... | collective-permute-start | bytes 202760 | tf_op jit(solution)/shard_map/ppermute | solution.py:24
  146.8 12.4 %collective-permute-start.21 = (bf16[8,4224]{1,0:T(8,128)(2,1)S(1)}, bf16[8,4224]{1,0:T(8,128)(2,1)S(1)}, u32[]{:S(2)}, u32[]{:S(2)}) collective-permute-start(bf16[8,4224]{1,0:T(8,128)(2,1)S(1)} %collective-permute-done.20), channel_id=1, source_target_pairs={{0,2},{1,3},{2,0},{3,1},{4,6},{5,7},{6,4},{7,5},{8,10},{9,11},{10,... | collective-permute-start | bytes 202760 | tf_op jit(solution)/shard_map/ppermute | solution.py:24
  152.2 6.9 %collective-permute-start.19 = (bf16[24,4224]{1,0:T(8,128)(2,1)S(1)}, bf16[24,4224]{1,0:T(8,128)(2,1)S(1)}, u32[]{:S(2)}, u32[]{:S(2)}) collective-permute-start(bf16[24,4224]{1,0:T(8,128)(2,1)S(1)} %pad_maximum_fusion.2), channel_id=1, source_target_pairs={{0,2},{1,3},{2,0},{3,1},{4,6},{5,7},{6,4},{7,5},{8,10},{9,11},{10,... | collective-permute-start | bytes 608264 | tf_op jit(solution)/shard_map/ppermute | solution.py:24
  159.2 10.5 %collective-permute-start.22 = (bf16[128,4224]{1,0:T(8,128)(2,1)S(1)}, bf16[128,4224]{1,0:T(8,128)(2,1)S(1)}, u32[]{:S(2)}, u32[]{:S(2)}) collective-permute-start(bf16[128,4224]{1,0:T(8,128)(2,1)S(1)} %constant_dynamic-update-slice_fusion.a.twin), channel_id=1, source_target_pairs={{0,1},{1,0},{2,3},{3,2},{4,5},{5,4},{6,7},{7,6},{8,9},{9,8},{10,11... | collective-permute-start | bytes 3244040 | tf_op jit(solution)/shard_map/ppermute | solution.py:28

commit v5 on v4

--- a/solution.py
+++ b/solution.py
@@ -245,9 +245,8 @@
         packed(block(4) + c5.astype(f32) + c6.astype(f32)), c9, c10, kept, incoming
     )
     a4 = across(out4, 4)
-    out8, c3, kept, incoming = apart(
-        packed(block(8) + c9.astype(f32) + c10.astype(f32) + a12.astype(f32)), c3, kept, incoming
-    )
+    total8 = packed(block(8) + c9.astype(f32) + c10.astype(f32) + a12.astype(f32))
+    out8, c3, kept, incoming = apart(total8, c3, kept, incoming)
     a8 = across(out8, 8)
     a2 = across(packed(block(2) + c3.astype(f32)), 2)
     return block(0) + a1.astype(f32) + a2.astype(f32) + a4.astype(f32) + a8.astype(f32)
@@ -255,12 +254,12 @@
 
 def gather_rounds(own):
     b = {0: own}
-    for d in (8, 4, 2, 1):
+    for d in (8, 4, 2):
         b[d] = across(own, d)
     b[12] = across(b[8], 4)
     two = cat(b[8], b[4])
     b[10], b[6] = split(across(two, 2))
-    b[9], b[5], b[3] = split(across(cat(b[8], b[4], b[2]), 1))
+    b[9], b[5], b[3], b[1] = split(across(cat(b[8], b[4], b[2], own), 1))
     b[14] = across(b[12], 2)
     b[13], b[11], b[7] = split(across(cat(b[12], b[10], b[6]), 1))
     b[15] = across(b[14], 1)

time: 173 us -> 173 us (level)
  starting transfers between devices: 100 us -> 102 us
    ppermute x19 -> x18, starting transfers between devices: 71.4 us -> 76.8 us  [across(): return lax.ppermute(x, 'tp', [(i, i ^ 2 * d) for i in range(TP)])]
    ppermute x3, starting transfers between devices: 26.8 us -> 22.9 us  [other_core(): return lax.ppermute(x, 'tp', [(i, i ^ 1) for i in range(TP)])]
    ppermute x19 -> x18, waiting for transfers between devices: 42.1 us -> 41.3 us  [across(): return lax.ppermute(x, 'tp', [(i, i ^ 2 * d) for i in range(TP)])]
  transfers between devices with their start and end apart: 23 -> 22, of which waited for: 12 -> 11; matrix products, arithmetic and copies ran while one was open for 1% -> 1% of each run, Pallas kernels for 4% -> 4%
where the time goes in v5:
time: 173 us
  starting transfers between devices  102 us (59%)
  waiting for transfers between devices  55.7 us (32%)
  Pallas kernels  11.9 us (7%)
  between operations  1.79 us (1%)
    ppermute x18, starting transfers between devices, across(): return lax.ppermute(x, 'tp', [(i, i ^ 2 * d) for i in range(TP)])  76.8 us
    ppermute x18, waiting for transfers between devices, across(): return lax.ppermute(x, 'tp', [(i, i ^ 2 * d) for i in range(TP)])  41.3 us
    ppermute x3, starting transfers between devices, other_core(): return lax.ppermute(x, 'tp', [(i, i ^ 1) for i in range(TP)])  22.9 us
    ppermute x1, waiting for transfers between devices, next_section(): return lax.ppermute(x, ('section', 'tp'), pairs)  13.9 us
    pallas_call x2, Pallas kernels, out_proj(): pl.pallas_call(out_proj_body, out_shape=jax.ShapeDtypeStruct((TOK, HALF),...  5.4 us
  transfers between devices with their start and end apart: 22, of which 11 were waited for; matrix products, arithmetic and copies ran while one was open for 1% of the time, Pallas kernels for 4%

profile of v5, /device:TPU:1, one launch (start us, length us, event | category | flops | bytes accessed | tf_op | source)
XLA Modules:
  0.0 172.5 jit_solution(2195504737388277579)
XLA Ops:
  0.7 0.1 pad_add_fusion.ids
  0.7 2.7 %out_proj.3 = bf16[128,4096]{1,0:T(8,128)(2,1)S(1)} custom-call(s32[4]{0:T(128)S(1)} %pad_add_fusion.ids, bf16[128,256]{1,0:T(8,128)(2,1)} %bitcast.15, bf16[256,8192]{1,0:T(8,128)(2,1)} %weight.3, bf16[4,8192]{1,0:T(4,128)(2,1)} %bitcast.17), custom_call_target="tpu_custom_call" | custom-call | tf_op jit(solution)/shard_map/out_proj/pallas_call | solution.py:67
  3.4 16.0 %collective-permute-start = (bf16[128,4096]{1,0:T(8,128)(2,1)S(1)}, bf16[128,4096]{1,0:T(8,128)(2,1)S(1)}, u32[]{:S(2)}, u32[]{:S(2)}) collective-permute-start(bf16[128,4096]{1,0:T(8,128)(2,1)S(1)} %out_proj.3), channel_id=1, source_target_pairs={{0,1},{1,0},{2,3},{3,2},{4,5},{5,4},{6,7},{7,6},{8,9},{9,8},{10,11... | collective-permute-start | bytes 3145736 | tf_op jit(solution)/shard_map/ppermute | solution.py:28
  19.4 2.7 %out_proj.2 = f32[128,4096]{1,0:T(8,128)S(1)} custom-call(s32[4]{0:T(128)S(1)} %pad_add_fusion.ids, bf16[128,256]{1,0:T(8,128)(2,1)} %bitcast.16, bf16[256,8192]{1,0:T(8,128)(2,1)} %weight.3, bf16[4,8192]{1,0:T(4,128)(2,1)} %bitcast.18), custom_call_target="tpu_custom_call" | custom-call | tf_op jit(solution)/shard_map/out_proj/pallas_call | solution.py:67
  22.2 0.0 collective-permute-done
  22.2 1.9 %collective-permute-start.1 = (bf16[8,4096]{1,0:T(8,128)(2,1)S(1)}, bf16[8,4096]{1,0:T(8,128)(2,1)S(1)}, u32[]{:S(2)}, u32[]{:S(2)}) collective-permute-start(bf16[8,4096]{1,0:T(8,128)(2,1)S(1)} %fusion), channel_id=1, source_target_pairs={{0,2},{1,3},{2,0},{3,1},{4,6},{5,7},{6,4},{7,5},{8,10},{9,11},{10,... | collective-permute-start | bytes 196616 | tf_op jit(solution)/shard_map/ppermute | solution.py:24
  24.2 3.4 %collective-permute-start.2 = (bf16[24,4096]{1,0:T(8,128)(2,1)S(1)}, bf16[24,4096]{1,0:T(8,128)(2,1)S(1)}, u32[]{:S(2)}, u32[]{:S(2)}) collective-permute-start(bf16[24,4096]{1,0:T(8,128)(2,1)S(1)} %pad_maximum_fusion.2), channel_id=1, source_target_pairs={{0,2},{1,3},{2,0},{3,1},{4,6},{5,7},{6,4},{7,5},{8,10},{9,11},{10,... | collective-permute-start | bytes 589832 | tf_op jit(solution)/shard_map/ppermute | solution.py:24
  27.7 1.9 %collective-permute-start.4 = (bf16[32,4096]{1,0:T(8,128)(2,1)S(1)}, bf16[32,4096]{1,0:T(8,128)(2,1)S(1)}, u32[]{:S(2)}, u32[]{:S(2)}) collective-permute-start(bf16[32,4096]{1,0:T(8,128)(2,1)S(1)} %pad_maximum_fusion), channel_id=1, source_target_pairs={{0,2},{1,3},{2,0},{3,1},{4,6},{5,7},{6,4},{7,5},{8,10},{9,11},{10,... | collective-permute-start | bytes 786440 | tf_op jit(solution)/shard_map/ppermute | solution.py:24
  29.6 0.0 collective-permute-done.1
  29.6 1.9 %collective-permute-start.3 = (bf16[8,4096]{1,0:T(8,128)(2,1)S(1)}, bf16[8,4096]{1,0:T(8,128)(2,1)S(1)}, u32[]{:S(2)}, u32[]{:S(2)}) collective-permute-start(bf16[8,4096]{1,0:T(8,128)(2,1)S(1)} %add_convert_fusion.6), channel_id=1, source_target_pairs={{0,4},{1,5},{2,6},{3,7},{4,0},{5,1},{6,2},{7,3},{8,12},{9,13},{10,... | collective-permute-start | bytes 196616 | tf_op jit(solution)/shard_map/ppermute | solution.py:24
  31.6 1.0 collective-permute-done.2
  32.6 5.9 %collective-permute-done.3 = bf16[8,4096]{1,0:T(8,128)(2,1)S(1)} collective-permute-done((bf16[8,4096]{1,0:T(8,128)(2,1)S(1)}, bf16[8,4096]{1,0:T(8,128)(2,1)S(1)}, u32[]{:S(2)}, u32[]{:S(2)}) %collective-permute-start.3) | collective-permute-done | bytes 65568 | tf_op jit(solution)/shard_map/ppermute | solution.py:24
  38.6 0.0 copy-start
  38.6 1.9 %collective-permute-start.6 = (bf16[8,4096]{1,0:T(8,128)(2,1)S(1)}, bf16[8,4096]{1,0:T(8,128)(2,1)S(1)}, u32[]{:S(2)}, u32[]{:S(2)}) collective-permute-start(bf16[8,4096]{1,0:T(8,128)(2,1)S(1)} %add_convert_fusion.3), channel_id=1, source_target_pairs={{0,8},{1,9},{2,10},{3,11},{4,12},{5,13},{6,14},{7,15},{8,0},{9,1},... | collective-permute-start | bytes 196616 | tf_op jit(solution)/shard_map/ppermute | solution.py:24
  40.5 4.7 %collective-permute-start.5 = (bf16[16,4096]{1,0:T(8,128)(2,1)S(1)}, bf16[16,4096]{1,0:T(8,128)(2,1)S(1)}, u32[]{:S(2)}, u32[]{:S(2)}) collective-permute-start(bf16[16,4096]{1,0:T(8,128)(2,1)S(1)} %pad_maximum_fusion.4), channel_id=1, source_target_pairs={{0,4},{1,5},{2,6},{3,7},{4,0},{5,1},{6,2},{7,3},{8,12},{9,13},{10,... | collective-permute-start | bytes 393224 | tf_op jit(solution)/shard_map/ppermute | solution.py:24
  45.3 0.0 collective-permute-done.4
  45.3 8.8 %collective-permute-done.5 = bf16[16,4096]{1,0:T(8,128)(2,1)S(1)} collective-permute-done((bf16[16,4096]{1,0:T(8,128)(2,1)S(1)}, bf16[16,4096]{1,0:T(8,128)(2,1)S(1)}, u32[]{:S(2)}, u32[]{:S(2)}) %collective-permute-start.5) | collective-permute-done | bytes 131104 | tf_op jit(solution)/shard_map/ppermute | solution.py:24
  54.2 0.0 collective-permute-done.6
  54.3 1.9 %collective-permute-start.7 = (bf16[8,4096]{1,0:T(8,128)(2,1)S(1)}, bf16[8,4096]{1,0:T(8,128)(2,1)S(1)}, u32[]{:S(2)}, u32[]{:S(2)}) collective-permute-start(bf16[8,4096]{1,0:T(8,128)(2,1)S(1)} %add_convert_fusion), channel_id=1, source_target_pairs={{0,4},{1,5},{2,6},{3,7},{4,0},{5,1},{6,2},{7,3},{8,12},{9,13},{10,... | collective-permute-start | bytes 196616 | tf_op jit(solution)/shard_map/ppermute | solution.py:24
  56.2 6.3 %collective-permute-start.9 = (bf16[8,4096]{1,0:T(8,128)(2,1)S(1)}, bf16[8,4096]{1,0:T(8,128)(2,1)S(1)}, u32[]{:S(2)}, u32[]{:S(2)}) collective-permute-start(bf16[8,4096]{1,0:T(8,128)(2,1)S(1)} %add_convert_fusion.1), channel_id=1, source_target_pairs={{0,16},{1,17},{2,18},{3,19},{4,20},{5,21},{6,22},{7,23},{8,24},{9,... | collective-permute-start | bytes 196616 | tf_op jit(solution)/shard_map/ppermute | solution.py:24
  62.5 3.2 %collective-permute-start.8 = (bf16[8,4096]{1,0:T(8,128)(2,1)S(1)}, bf16[8,4096]{1,0:T(8,128)(2,1)S(1)}, u32[]{:S(2)}, u32[]{:S(2)}) collective-permute-start(bf16[8,4096]{1,0:T(8,128)(2,1)S(1)} %add_convert_fusion.2), channel_id=1, source_target_pairs={{0,8},{1,9},{2,10},{3,11},{4,12},{5,13},{6,14},{7,15},{8,0},{9,1},... | collective-permute-start | bytes 196616 | tf_op jit(solution)/shard_map/ppermute | solution.py:24
  65.7 0.0 collective-permute-done.7
  65.7 13.6 %collective-permute-done.9 = bf16[8,4096]{1,0:T(8,128)(2,1)S(1)} collective-permute-done((bf16[8,4096]{1,0:T(8,128)(2,1)S(1)}, bf16[8,4096]{1,0:T(8,128)(2,1)S(1)}, u32[]{:S(2)}, u32[]{:S(2)}) %collective-permute-start.9) | collective-permute-done | bytes 65568 | tf_op jit(solution)/shard_map/ppermute | solution.py:24
  79.3 0.0 collective-permute-done.8
  79.3 0.1 reduce-precision_convert_fusion.own
  79.4 2.6 %collective-permute-start.10 = (bf16[8,4096]{1,0:T(8,128)(2,1)S(1)}, bf16[8,4096]{1,0:T(8,128)(2,1)S(1)}, u32[]{:S(2)}, u32[]{:S(2)}) collective-permute-start(bf16[8,4096]{1,0:T(8,128)(2,1)S(1)} %reduce-precision_convert_fusion.own), channel_id=1, source_target_pairs={{0,1},{1,0},{2,3},{3,2},{4,5},{5,4},{6,7},{7,6},{8,9},{9,8},{10,11... | collective-permute-start | bytes 196616 | tf_op jit(solution)/shard_map/ppermute | solution.py:28
  82.6 0.0 copy-done
  82.7 0.2 collective-permute-done.10.twin
  82.9 0.8 cast.1
  83.6 1.9 %collective-permute-start.11 = (bf16[8,4224]{1,0:T(8,128)(2,1)S(1)}, bf16[8,4224]{1,0:T(8,128)(2,1)S(1)}, u32[]{:S(2)}, u32[]{:S(2)}) collective-permute-start(bf16[8,4224]{1,0:T(8,128)(2,1)S(1)} %get-tuple-element.63), channel_id=1, source_target_pairs={{0,32},{1,33},{2,34},{3,35},{4,36},{5,37},{6,38},{7,39},{8,40},{9,... | collective-permute-start | bytes 202760 | tf_op jit(solution)/shard_map/ppermute | solution.py:37
  85.6 2.3 %prefetch.1.weight = bf16[288,8192]{1,0:T(8,128)(2,1)S(1)} custom-call(bf16[288,8192]{1,0:T(8,128)(2,1)} %bitcast.14), custom_call_target="tpu_custom_call" | custom-call | tf_op jit(solution)/shard_map/prefetch/pallas_call | solution.py:136
  87.9 13.9 %collective-permute-done.11.arrived = bf16[8,4224]{1,0:T(8,128)(2,1)S(1)} collective-permute-done((bf16[8,4224]{1,0:T(8,128)(2,1)S(1)}, bf16[8,4224]{1,0:T(8,128)(2,1)S(1)}, u32[]{:S(2)}, u32[]{:S(2)}) %collective-permute-start.11) | collective-permute-done | bytes 67616 | tf_op jit(solution)/shard_map/ppermute | solution.py:37
  101.9 10.1 %collective-permute-start.13 = (bf16[8,4224]{1,0:T(8,128)(2,1)S(1)}, bf16[8,4224]{1,0:T(8,128)(2,1)S(1)}, u32[]{:S(2)}, u32[]{:S(2)}) collective-permute-start(bf16[8,4224]{1,0:T(8,128)(2,1)S(1)} %get-tuple-element.78), channel_id=1, source_target_pairs={{0,8},{1,9},{2,10},{3,11},{4,12},{5,13},{6,14},{7,15},{8,0},{9,1},... | collective-permute-start | bytes 202760 | tf_op jit(solution)/shard_map/ppermute | solution.py:24
  112.0 7.9 %collective-permute-start.12 = (bf16[8,4224]{1,0:T(8,128)(2,1)S(1)}, bf16[8,4224]{1,0:T(8,128)(2,1)S(1)}, u32[]{:S(2)}, u32[]{:S(2)}) collective-permute-start(bf16[8,4224]{1,0:T(8,128)(2,1)S(1)} %get-tuple-element.78), channel_id=1, source_target_pairs={{0,16},{1,17},{2,18},{3,19},{4,20},{5,21},{6,22},{7,23},{8,24},{9,... | collective-permute-start | bytes 202760 | tf_op jit(solution)/shard_map/ppermute | solution.py:24
  119.9 1.9 %collective-permute-start.14 = (bf16[8,4224]{1,0:T(8,128)(2,1)S(1)}, bf16[8,4224]{1,0:T(8,128)(2,1)S(1)}, u32[]{:S(2)}, u32[]{:S(2)}) collective-permute-start(bf16[8,4224]{1,0:T(8,128)(2,1)S(1)} %get-tuple-element.78), channel_id=1, source_target_pairs={{0,4},{1,5},{2,6},{3,7},{4,0},{5,1},{6,2},{7,3},{8,12},{9,13},{10,... | collective-permute-start | bytes 202760 | tf_op jit(solution)/shard_map/ppermute | solution.py:24
  121.8 4.0 %collective-permute-done.12 = bf16[8,4224]{1,0:T(8,128)(2,1)S(1)} collective-permute-done((bf16[8,4224]{1,0:T(8,128)(2,1)S(1)}, bf16[8,4224]{1,0:T(8,128)(2,1)S(1)}, u32[]{:S(2)}, u32[]{:S(2)}) %collective-permute-start.12) | collective-permute-done | bytes 67616 | tf_op jit(solution)/shard_map/ppermute | solution.py:24
  125.8 6.0 %collective-permute-start.17 = (bf16[8,4224]{1,0:T(8,128)(2,1)S(1)}, bf16[8,4224]{1,0:T(8,128)(2,1)S(1)}, u32[]{:S(2)}, u32[]{:S(2)}) collective-permute-start(bf16[8,4224]{1,0:T(8,128)(2,1)S(1)} %collective-permute-done.12), channel_id=1, source_target_pairs={{0,8},{1,9},{2,10},{3,11},{4,12},{5,13},{6,14},{7,15},{8,0},{9,1},... | collective-permute-start | bytes 202760 | tf_op jit(solution)/shard_map/ppermute | solution.py:24
  131.8 0.0 collective-permute-done.13
  131.8 1.9 %collective-permute-start.16 = (bf16[16,4224]{1,0:T(8,128)(2,1)S(1)}, bf16[16,4224]{1,0:T(8,128)(2,1)S(1)}, u32[]{:S(2)}, u32[]{:S(2)}) collective-permute-start(bf16[16,4224]{1,0:T(8,128)(2,1)S(1)} %pad_maximum_fusion.3), channel_id=1, source_target_pairs={{0,4},{1,5},{2,6},{3,7},{4,0},{5,1},{6,2},{7,3},{8,12},{9,13},{10,... | collective-permute-start | bytes 405512 | tf_op jit(solution)/shard_map/ppermute | solution.py:24
  133.8 2.8 %collective-permute-done.17 = bf16[8,4224]{1,0:T(8,128)(2,1)S(1)} collective-permute-done((bf16[8,4224]{1,0:T(8,128)(2,1)S(1)}, bf16[8,4224]{1,0:T(8,128)(2,1)S(1)}, u32[]{:S(2)}, u32[]{:S(2)}) %collective-permute-start.17) | collective-permute-done | bytes 67616 | tf_op jit(solution)/shard_map/ppermute | solution.py:24
  136.6 3.1 %collective-permute-start.19 = (bf16[8,4224]{1,0:T(8,128)(2,1)S(1)}, bf16[8,4224]{1,0:T(8,128)(2,1)S(1)}, u32[]{:S(2)}, u32[]{:S(2)}) collective-permute-start(bf16[8,4224]{1,0:T(8,128)(2,1)S(1)} %collective-permute-done.17), channel_id=1, source_target_pairs={{0,4},{1,5},{2,6},{3,7},{4,0},{5,1},{6,2},{7,3},{8,12},{9,13},{10,... | collective-permute-start | bytes 202760 | tf_op jit(solution)/shard_map/ppermute | solution.py:24
  139.7 0.0 collective-permute-done.14
  139.7 12.8 %collective-permute-start.15 = (bf16[32,4224]{1,0:T(8,128)(2,1)S(1)}, bf16[32,4224]{1,0:T(8,128)(2,1)S(1)}, u32[]{:S(2)}, u32[]{:S(2)}) collective-permute-start(bf16[32,4224]{1,0:T(8,128)(2,1)S(1)} %maximum_maximum_fusion), channel_id=1, source_target_pairs={{0,2},{1,3},{2,0},{3,1},{4,6},{5,7},{6,4},{7,5},{8,10},{9,11},{10,... | collective-permute-start | bytes 811016 | tf_op jit(solution)/shard_map/ppermute | solution.py:24
  152.5 0.0 collective-permute-done.19
  152.5 3.9 %collective-permute-start.20 = (bf16[8,4224]{1,0:T(8,128)(2,1)S(1)}, bf16[8,4224]{1,0:T(8,128)(2,1)S(1)}, u32[]{:S(2)}, u32[]{:S(2)}) collective-permute-start(bf16[8,4224]{1,0:T(8,128)(2,1)S(1)} %collective-permute-done.19), channel_id=1, source_target_pairs={{0,2},{1,3},{2,0},{3,1},{4,6},{5,7},{6,4},{7,5},{8,10},{9,11},{10,... | collective-permute-start | bytes 202760 | tf_op jit(solution)/shard_map/ppermute | solution.py:24
  156.5 0.0 collective-permute-done.16
  156.5 1.9 %collective-permute-start.18 = (bf16[24,4224]{1,0:T(8,128)(2,1)S(1)}, bf16[24,4224]{1,0:T(8,128)(2,1)S(1)}, u32[]{:S(2)}, u32[]{:S(2)}) collective-permute-start(bf16[24,4224]{1,0:T(8,128)(2,1)S(1)} %pad_maximum_fusion.1), channel_id=1, source_target_pairs={{0,2},{1,3},{2,0},{3,1},{4,6},{5,7},{6,4},{7,5},{8,10},{9,11},{10,... | collective-permute-start | bytes 608264 | tf_op jit(solution)/shard_map/ppermute | solution.py:24
  158.4 0.4 collective-permute-done.15
  159.0 4.7 %collective-permute-done.18 = bf16[24,4224]{1,0:T(8,128)(2,1)S(1)} collective-permute-done((bf16[24,4224]{1,0:T(8,128)(2,1)S(1)}, bf16[24,4224]{1,0:T(8,128)(2,1)S(1)}, u32[]{:S(2)}, u32[]{:S(2)}) %collective-permute-start.18) | collective-permute-done | bytes 202784 | tf_op jit(solution)/shard_map/ppermute | solution.py:24
  163.8 0.0 collective-permute-done.20
  163.8 4.3 %collective-permute-start.21 = (bf16[128,4224]{1,0:T(8,128)(2,1)S(1)}, bf16[128,4224]{1,0:T(8,128)(2,1)S(1)}, u32[]{:S(2)}, u32[]{:S(2)}) collective-permute-start(bf16[128,4224]{1,0:T(8,128)(2,1)S(1)} %constant_dynamic-update-slice_fusion.a.twin), channel_id=1, source_target_pairs={{0,1},{1,0},{2,3},{3,2},{4,5},{5,4},{6,7},{7,6},{8,9},{9,8},{10,11... | collective-permute-start | bytes 3244040 | tf_op jit(solution)/shard_map/ppermute | solution.py:28
  168.2 0.7 maximum_select_fusion
  168.8 1.3 first_half.1.start
  170.2 0.3 collective-permute-done.21.a
  170.4 2.1 %second_half.1 = (bf16[288,128]{1,0:T(8,128)(2,1)}, f32[1]{0:T(128)}) custom-call(s32[4]{0:T(128)S(1)} %pad_add_fusion.ids, bf16[288,8192]{1,0:T(8,128)(2,1)S(1)} %prefetch.1.weight, bf16[128,4224]{1,0:T(8,128)(2,1)S(1)} %collective-permute-done.21.a, f32[288,128]{1,0:T(8,128)S(1)} %first_half.1.start, bf16[8,4224]{1,0:T(8,128)(2,1)S(1)} %collective-permute-done.11.arrived, ...), custom_call_target="tpu_custom_call" | custom-call | tf_op jit(solution)/shard_map/second_half/pallas_call | solution.py:193
  (38 shorter events, 0.7 us)
Async XLA Ops:
  3.4 18.8 %collective-permute-start = (bf16[128,4096]{1,0:T(8,128)(2,1)S(1)}, bf16[128,4096]{1,0:T(8,128)(2,1)S(1)}, u32[]{:S(2)}, u32[]{:S(2)}) collective-permute-start(bf16[128,4096]{1,0:T(8,128)(2,1)S(1)} %out_proj.3), channel_id=1, source_target_pairs={{0,1},{1,0},{2,3},{3,2},{4,5},{5,4},{6,7},{7,6},{8,9},{9,8},{10,11... | collective-permute-start | bytes 3145736 | tf_op jit(solution)/shard_map/ppermute | solution.py:28
  22.2 7.4 %collective-permute-start.1 = (bf16[8,4096]{1,0:T(8,128)(2,1)S(1)}, bf16[8,4096]{1,0:T(8,128)(2,1)S(1)}, u32[]{:S(2)}, u32[]{:S(2)}) collective-permute-start(bf16[8,4096]{1,0:T(8,128)(2,1)S(1)} %fusion), channel_id=1, source_target_pairs={{0,2},{1,3},{2,0},{3,1},{4,6},{5,7},{6,4},{7,5},{8,10},{9,11},{10,... | collective-permute-start | bytes 196616 | tf_op jit(solution)/shard_map/ppermute | solution.py:24
  24.2 8.3 %collective-permute-start.2 = (bf16[24,4096]{1,0:T(8,128)(2,1)S(1)}, bf16[24,4096]{1,0:T(8,128)(2,1)S(1)}, u32[]{:S(2)}, u32[]{:S(2)}) collective-permute-start(bf16[24,4096]{1,0:T(8,128)(2,1)S(1)} %pad_maximum_fusion.2), channel_id=1, source_target_pairs={{0,2},{1,3},{2,0},{3,1},{4,6},{5,7},{6,4},{7,5},{8,10},{9,11},{10,... | collective-permute-start | bytes 589832 | tf_op jit(solution)/shard_map/ppermute | solution.py:24
  27.7 17.6 %collective-permute-start.4 = (bf16[32,4096]{1,0:T(8,128)(2,1)S(1)}, bf16[32,4096]{1,0:T(8,128)(2,1)S(1)}, u32[]{:S(2)}, u32[]{:S(2)}) collective-permute-start(bf16[32,4096]{1,0:T(8,128)(2,1)S(1)} %pad_maximum_fusion), channel_id=1, source_target_pairs={{0,2},{1,3},{2,0},{3,1},{4,6},{5,7},{6,4},{7,5},{8,10},{9,11},{10,... | collective-permute-start | bytes 786440 | tf_op jit(solution)/shard_map/ppermute | solution.py:24
  29.6 8.9 %collective-permute-start.3 = (bf16[8,4096]{1,0:T(8,128)(2,1)S(1)}, bf16[8,4096]{1,0:T(8,128)(2,1)S(1)}, u32[]{:S(2)}, u32[]{:S(2)}) collective-permute-start(bf16[8,4096]{1,0:T(8,128)(2,1)S(1)} %add_convert_fusion.6), channel_id=1, source_target_pairs={{0,4},{1,5},{2,6},{3,7},{4,0},{5,1},{6,2},{7,3},{8,12},{9,13},{10,... | collective-permute-start | bytes 196616 | tf_op jit(solution)/shard_map/ppermute | solution.py:24
  38.6 44.0 %copy-start = (bf16[8192]{0:T(1024)(128)(2,1)S(1)}, bf16[8192]{0:T(1024)(128)(2,1)}, u32[]{:S(2)}) copy-start(bf16[8192]{0:T(1024)(128)(2,1)} %param.9) | copy-start | bytes 49156
  38.6 15.6 %collective-permute-start.6 = (bf16[8,4096]{1,0:T(8,128)(2,1)S(1)}, bf16[8,4096]{1,0:T(8,128)(2,1)S(1)}, u32[]{:S(2)}, u32[]{:S(2)}) collective-permute-start(bf16[8,4096]{1,0:T(8,128)(2,1)S(1)} %add_convert_fusion.3), channel_id=1, source_target_pairs={{0,8},{1,9},{2,10},{3,11},{4,12},{5,13},{6,14},{7,15},{8,0},{9,1},... | collective-permute-start | bytes 196616 | tf_op jit(solution)/shard_map/ppermute | solution.py:24
  40.5 13.6 %collective-permute-start.5 = (bf16[16,4096]{1,0:T(8,128)(2,1)S(1)}, bf16[16,4096]{1,0:T(8,128)(2,1)S(1)}, u32[]{:S(2)}, u32[]{:S(2)}) collective-permute-start(bf16[16,4096]{1,0:T(8,128)(2,1)S(1)} %pad_maximum_fusion.4), channel_id=1, source_target_pairs={{0,4},{1,5},{2,6},{3,7},{4,0},{5,1},{6,2},{7,3},{8,12},{9,13},{10,... | collective-permute-start | bytes 393224 | tf_op jit(solution)/shard_map/ppermute | solution.py:24
  54.3 11.5 %collective-permute-start.7 = (bf16[8,4096]{1,0:T(8,128)(2,1)S(1)}, bf16[8,4096]{1,0:T(8,128)(2,1)S(1)}, u32[]{:S(2)}, u32[]{:S(2)}) collective-permute-start(bf16[8,4096]{1,0:T(8,128)(2,1)S(1)} %add_convert_fusion), channel_id=1, source_target_pairs={{0,4},{1,5},{2,6},{3,7},{4,0},{5,1},{6,2},{7,3},{8,12},{9,13},{10,... | collective-permute-start | bytes 196616 | tf_op jit(solution)/shard_map/ppermute | solution.py:24
  56.2 23.1 %collective-permute-start.9 = (bf16[8,4096]{1,0:T(8,128)(2,1)S(1)}, bf16[8,4096]{1,0:T(8,128)(2,1)S(1)}, u32[]{:S(2)}, u32[]{:S(2)}) collective-permute-start(bf16[8,4096]{1,0:T(8,128)(2,1)S(1)} %add_convert_fusion.1), channel_id=1, source_target_pairs={{0,16},{1,17},{2,18},{3,19},{4,20},{5,21},{6,22},{7,23},{8,24},{9,... | collective-permute-start | bytes 196616 | tf_op jit(solution)/shard_map/ppermute | solution.py:24
  62.5 16.8 %collective-permute-start.8 = (bf16[8,4096]{1,0:T(8,128)(2,1)S(1)}, bf16[8,4096]{1,0:T(8,128)(2,1)S(1)}, u32[]{:S(2)}, u32[]{:S(2)}) collective-permute-start(bf16[8,4096]{1,0:T(8,128)(2,1)S(1)} %add_convert_fusion.2), channel_id=1, source_target_pairs={{0,8},{1,9},{2,10},{3,11},{4,12},{5,13},{6,14},{7,15},{8,0},{9,1},... | collective-permute-start | bytes 196616 | tf_op jit(solution)/shard_map/ppermute | solution.py:24
  79.4 3.5 %collective-permute-start.10 = (bf16[8,4096]{1,0:T(8,128)(2,1)S(1)}, bf16[8,4096]{1,0:T(8,128)(2,1)S(1)}, u32[]{:S(2)}, u32[]{:S(2)}) collective-permute-start(bf16[8,4096]{1,0:T(8,128)(2,1)S(1)} %reduce-precision_convert_fusion.own), channel_id=1, source_target_pairs={{0,1},{1,0},{2,3},{3,2},{4,5},{5,4},{6,7},{7,6},{8,9},{9,8},{10,11... | collective-permute-start | bytes 196616 | tf_op jit(solution)/shard_map/ppermute | solution.py:28
  83.6 18.2 %collective-permute-start.11 = (bf16[8,4224]{1,0:T(8,128)(2,1)S(1)}, bf16[8,4224]{1,0:T(8,128)(2,1)S(1)}, u32[]{:S(2)}, u32[]{:S(2)}) collective-permute-start(bf16[8,4224]{1,0:T(8,128)(2,1)S(1)} %get-tuple-element.63), channel_id=1, source_target_pairs={{0,32},{1,33},{2,34},{3,35},{4,36},{5,37},{6,38},{7,39},{8,40},{9,... | collective-permute-start | bytes 202760 | tf_op jit(solution)/shard_map/ppermute | solution.py:37
  101.9 29.9 %collective-permute-start.13 = (bf16[8,4224]{1,0:T(8,128)(2,1)S(1)}, bf16[8,4224]{1,0:T(8,128)(2,1)S(1)}, u32[]{:S(2)}, u32[]{:S(2)}) collective-permute-start(bf16[8,4224]{1,0:T(8,128)(2,1)S(1)} %get-tuple-element.78), channel_id=1, source_target_pairs={{0,8},{1,9},{2,10},{3,11},{4,12},{5,13},{6,14},{7,15},{8,0},{9,1},... | collective-permute-start | bytes 202760 | tf_op jit(solution)/shard_map/ppermute | solution.py:24
  112.0 13.8 %collective-permute-start.12 = (bf16[8,4224]{1,0:T(8,128)(2,1)S(1)}, bf16[8,4224]{1,0:T(8,128)(2,1)S(1)}, u32[]{:S(2)}, u32[]{:S(2)}) collective-permute-start(bf16[8,4224]{1,0:T(8,128)(2,1)S(1)} %get-tuple-element.78), channel_id=1, source_target_pairs={{0,16},{1,17},{2,18},{3,19},{4,20},{5,21},{6,22},{7,23},{8,24},{9,... | collective-permute-start | bytes 202760 | tf_op jit(solution)/shard_map/ppermute | solution.py:24
  119.9 19.8 %collective-permute-start.14 = (bf16[8,4224]{1,0:T(8,128)(2,1)S(1)}, bf16[8,4224]{1,0:T(8,128)(2,1)S(1)}, u32[]{:S(2)}, u32[]{:S(2)}) collective-permute-start(bf16[8,4224]{1,0:T(8,128)(2,1)S(1)} %get-tuple-element.78), channel_id=1, source_target_pairs={{0,4},{1,5},{2,6},{3,7},{4,0},{5,1},{6,2},{7,3},{8,12},{9,13},{10,... | collective-permute-start | bytes 202760 | tf_op jit(solution)/shard_map/ppermute | solution.py:24
  125.8 10.8 %collective-permute-start.17 = (bf16[8,4224]{1,0:T(8,128)(2,1)S(1)}, bf16[8,4224]{1,0:T(8,128)(2,1)S(1)}, u32[]{:S(2)}, u32[]{:S(2)}) collective-permute-start(bf16[8,4224]{1,0:T(8,128)(2,1)S(1)} %collective-permute-done.12), channel_id=1, source_target_pairs={{0,8},{1,9},{2,10},{3,11},{4,12},{5,13},{6,14},{7,15},{8,0},{9,1},... | collective-permute-start | bytes 202760 | tf_op jit(solution)/shard_map/ppermute | solution.py:24
  131.8 24.6 %collective-permute-start.16 = (bf16[16,4224]{1,0:T(8,128)(2,1)S(1)}, bf16[16,4224]{1,0:T(8,128)(2,1)S(1)}, u32[]{:S(2)}, u32[]{:S(2)}) collective-permute-start(bf16[16,4224]{1,0:T(8,128)(2,1)S(1)} %pad_maximum_fusion.3), channel_id=1, source_target_pairs={{0,4},{1,5},{2,6},{3,7},{4,0},{5,1},{6,2},{7,3},{8,12},{9,13},{10,... | collective-permute-start | bytes 405512 | tf_op jit(solution)/shard_map/ppermute | solution.py:24
  136.6 16.0 %collective-permute-start.19 = (bf16[8,4224]{1,0:T(8,128)(2,1)S(1)}, bf16[8,4224]{1,0:T(8,128)(2,1)S(1)}, u32[]{:S(2)}, u32[]{:S(2)}) collective-permute-start(bf16[8,4224]{1,0:T(8,128)(2,1)S(1)} %collective-permute-done.17), channel_id=1, source_target_pairs={{0,4},{1,5},{2,6},{3,7},{4,0},{5,1},{6,2},{7,3},{8,12},{9,13},{10,... | collective-permute-start | bytes 202760 | tf_op jit(solution)/shard_map/ppermute | solution.py:24
  139.7 19.1 %collective-permute-start.15 = (bf16[32,4224]{1,0:T(8,128)(2,1)S(1)}, bf16[32,4224]{1,0:T(8,128)(2,1)S(1)}, u32[]{:S(2)}, u32[]{:S(2)}) collective-permute-start(bf16[32,4224]{1,0:T(8,128)(2,1)S(1)} %maximum_maximum_fusion), channel_id=1, source_target_pairs={{0,2},{1,3},{2,0},{3,1},{4,6},{5,7},{6,4},{7,5},{8,10},{9,11},{10,... | collective-permute-start | bytes 811016 | tf_op jit(solution)/shard_map/ppermute | solution.py:24
  152.5 11.2 %collective-permute-start.20 = (bf16[8,4224]{1,0:T(8,128)(2,1)S(1)}, bf16[8,4224]{1,0:T(8,128)(2,1)S(1)}, u32[]{:S(2)}, u32[]{:S(2)}) collective-permute-start(bf16[8,4224]{1,0:T(8,128)(2,1)S(1)} %collective-permute-done.19), channel_id=1, source_target_pairs={{0,2},{1,3},{2,0},{3,1},{4,6},{5,7},{6,4},{7,5},{8,10},{9,11},{10,... | collective-permute-start | bytes 202760 | tf_op jit(solution)/shard_map/ppermute | solution.py:24
  156.5 7.1 %collective-permute-start.18 = (bf16[24,4224]{1,0:T(8,128)(2,1)S(1)}, bf16[24,4224]{1,0:T(8,128)(2,1)S(1)}, u32[]{:S(2)}, u32[]{:S(2)}) collective-permute-start(bf16[24,4224]{1,0:T(8,128)(2,1)S(1)} %pad_maximum_fusion.1), channel_id=1, source_target_pairs={{0,2},{1,3},{2,0},{3,1},{4,6},{5,7},{6,4},{7,5},{8,10},{9,11},{10,... | collective-permute-start | bytes 608264 | tf_op jit(solution)/shard_map/ppermute | solution.py:24
  163.8 6.7 %collective-permute-start.21 = (bf16[128,4224]{1,0:T(8,128)(2,1)S(1)}, bf16[128,4224]{1,0:T(8,128)(2,1)S(1)}, u32[]{:S(2)}, u32[]{:S(2)}) collective-permute-start(bf16[128,4224]{1,0:T(8,128)(2,1)S(1)} %constant_dynamic-update-slice_fusion.a.twin), channel_id=1, source_target_pairs={{0,1},{1,0},{2,3},{3,2},{4,5},{5,4},{6,7},{7,6},{8,9},{9,8},{10,11... | collective-permute-start | bytes 3244040 | tf_op jit(solution)/shard_map/ppermute | solution.py:28

commit v6 on v5

--- a/solution.py
+++ b/solution.py
@@ -224,20 +224,19 @@
         rows = slice(o * ROWS, (o + 1) * ROWS)
         return kept[rows] + incoming[rows].astype(f32)
 
-    out15, kept, incoming = apart(block(15).astype(bf16), kept, incoming)
-    a15 = across(out15, 1)
     out13, kept, incoming = apart(packed(block(13), block(11), block(7)), kept, incoming)
     a13 = across(out13, 1)
+    out14, out15, kept, incoming = apart(packed(block(14)), packed(block(15)), kept, incoming)
+    a14 = across(out14, 2)
+    a15 = across(out15, 3)
     out9, kept, incoming = apart(packed(block(9), block(5), block(3), block(1)), kept, incoming)
     a9 = across(out9, 1)
-    out14, kept, incoming = apart(packed(block(14) + a15.astype(f32)), kept, incoming)
-    a14 = across(out14, 2)
     b13, b11, b7 = split(a13)
     out10, b13, kept, incoming = apart(
         packed(block(10) + b11.astype(f32), block(6) + b7.astype(f32)), b13, kept, incoming
     )
     a10 = across(out10, 2)
-    out12, kept, incoming = apart(packed(block(12) + b13.astype(f32) + a14.astype(f32)), kept, incoming)
+    out12, kept, incoming = apart(packed(block(12) + b13.astype(f32) + a14.astype(f32) + a15.astype(f32)), kept, incoming)
     a12 = across(out12, 4)
     c9, c5, c3, a1 = split(a9)
     c10, c6 = split(a10)
@@ -262,7 +261,7 @@
     b[9], b[5], b[3], b[1] = split(across(cat(b[8], b[4], b[2], own), 1))
     b[14] = across(b[12], 2)
     b[13], b[11], b[7] = split(across(cat(b[12], b[10], b[6]), 1))
-    b[15] = across(b[14], 1)
+    b[15] = across(b[12], 3)
     return cat(*[b[o] for o in range(CHIPS)])
 
 

time: 173 us -> 170 us (0.983)
  the two profiles are of different devices: /device:TPU:1 before, /device:TPU:6 now
where the time goes in v6:
time: 170 us; the launch traced here: 168 us
  starting transfers between devices  97.8 us (58%)
  waiting for transfers between devices  54.6 us (32%)
  Pallas kernels  11.9 us (7%)
  between operations  1.81 us (1%)
    ppermute x18, starting transfers between devices, across(): return lax.ppermute(x, 'tp', [(i, i ^ 2 * d) for i in range(TP)])  88.5 us
    ppermute x18, waiting for transfers between devices, across(): return lax.ppermute(x, 'tp', [(i, i ^ 2 * d) for i in range(TP)])  41.2 us
    ppermute x1, waiting for transfers between devices, next_section(): return lax.ppermute(x, ('section', 'tp'), pairs)  12.2 us
    ppermute x3, starting transfers between devices, other_core(): return lax.ppermute(x, 'tp', [(i, i ^ 1) for i in range(TP)])  5.76 us
    pallas_call x2, Pallas kernels, out_proj(): pl.pallas_call(out_proj_body, out_shape=jax.ShapeDtypeStruct((TOK, HALF),...  5.4 us
    ppermute x1, starting transfers between devices, next_section(): return lax.ppermute(x, ('section', 'tp'), pairs)  3.48 us
  transfers between devices with their start and end apart: 22, of which 10 were waited for; matrix products, arithmetic and copies ran while one was open for 1% of the time, Pallas kernels for 4%

profile of v6, /device:TPU:6, one launch (start us, length us, event | category | flops | bytes accessed | tf_op | source)
XLA Modules:
  0.0 167.6 jit_solution(9638091092928877072)
XLA Ops:
  0.7 0.1 pad_add_fusion.ids
  0.7 2.7 %out_proj.3 = bf16[128,4096]{1,0:T(8,128)(2,1)S(1)} custom-call(s32[4]{0:T(128)S(1)} %pad_add_fusion.ids, bf16[128,256]{1,0:T(8,128)(2,1)} %bitcast.15, bf16[256,8192]{1,0:T(8,128)(2,1)} %weight.3, bf16[4,8192]{1,0:T(4,128)(2,1)} %bitcast.17), custom_call_target="tpu_custom_call" | custom-call | tf_op jit(solution)/shard_map/out_proj/pallas_call | solution.py:67
  3.4 1.9 %collective-permute-start = (bf16[128,4096]{1,0:T(8,128)(2,1)S(1)}, bf16[128,4096]{1,0:T(8,128)(2,1)S(1)}, u32[]{:S(2)}, u32[]{:S(2)}) collective-permute-start(bf16[128,4096]{1,0:T(8,128)(2,1)S(1)} %out_proj.3), channel_id=1, source_target_pairs={{0,1},{1,0},{2,3},{3,2},{4,5},{5,4},{6,7},{7,6},{8,9},{9,8},{10,11... | collective-permute-start | bytes 3145736 | tf_op jit(solution)/shard_map/ppermute | solution.py:28
  5.3 2.7 %out_proj.2 = f32[128,4096]{1,0:T(8,128)S(1)} custom-call(s32[4]{0:T(128)S(1)} %pad_add_fusion.ids, bf16[128,256]{1,0:T(8,128)(2,1)} %bitcast.16, bf16[256,8192]{1,0:T(8,128)(2,1)} %weight.3, bf16[4,8192]{1,0:T(4,128)(2,1)} %bitcast.18), custom_call_target="tpu_custom_call" | custom-call | tf_op jit(solution)/shard_map/out_proj/pallas_call | solution.py:67
  8.1 0.0 collective-permute-done
  8.2 5.2 %collective-permute-start.2 = (bf16[8,4096]{1,0:T(8,128)(2,1)S(1)}, bf16[8,4096]{1,0:T(8,128)(2,1)S(1)}, u32[]{:S(2)}, u32[]{:S(2)}) collective-permute-start(bf16[8,4096]{1,0:T(8,128)(2,1)S(1)} %get-tuple-element.43), channel_id=1, source_target_pairs={{0,4},{1,5},{2,6},{3,7},{4,0},{5,1},{6,2},{7,3},{8,12},{9,13},{10,... | collective-permute-start | bytes 196616 | tf_op jit(solution)/shard_map/ppermute | solution.py:24
  13.4 3.3 %collective-permute-start.3 = (bf16[8,4096]{1,0:T(8,128)(2,1)S(1)}, bf16[8,4096]{1,0:T(8,128)(2,1)S(1)}, u32[]{:S(2)}, u32[]{:S(2)}) collective-permute-start(bf16[8,4096]{1,0:T(8,128)(2,1)S(1)} %get-tuple-element.44), channel_id=1, source_target_pairs={{0,6},{1,7},{2,4},{3,5},{4,2},{5,3},{6,0},{7,1},{8,14},{9,15},{10,... | collective-permute-start | bytes 196616 | tf_op jit(solution)/shard_map/ppermute | solution.py:24
  16.7 2.5 %collective-permute-start.1 = (bf16[24,4096]{1,0:T(8,128)(2,1)S(1)}, bf16[24,4096]{1,0:T(8,128)(2,1)S(1)}, u32[]{:S(2)}, u32[]{:S(2)}) collective-permute-start(bf16[24,4096]{1,0:T(8,128)(2,1)S(1)} %pad_maximum_fusion.2), channel_id=1, source_target_pairs={{0,2},{1,3},{2,0},{3,1},{4,6},{5,7},{6,4},{7,5},{8,10},{9,11},{10,... | collective-permute-start | bytes 589832 | tf_op jit(solution)/shard_map/ppermute | solution.py:24
  19.2 3.4 %collective-permute-start.4 = (bf16[32,4096]{1,0:T(8,128)(2,1)S(1)}, bf16[32,4096]{1,0:T(8,128)(2,1)S(1)}, u32[]{:S(2)}, u32[]{:S(2)}) collective-permute-start(bf16[32,4096]{1,0:T(8,128)(2,1)S(1)} %pad_maximum_fusion), channel_id=1, source_target_pairs={{0,2},{1,3},{2,0},{3,1},{4,6},{5,7},{6,4},{7,5},{8,10},{9,11},{10,... | collective-permute-start | bytes 786440 | tf_op jit(solution)/shard_map/ppermute | solution.py:24
  22.6 3.7 %collective-permute-done.1 = bf16[24,4096]{1,0:T(8,128)(2,1)S(1)} collective-permute-done((bf16[24,4096]{1,0:T(8,128)(2,1)S(1)}, bf16[24,4096]{1,0:T(8,128)(2,1)S(1)}, u32[]{:S(2)}, u32[]{:S(2)}) %collective-permute-start.1) | collective-permute-done | bytes 196640 | tf_op jit(solution)/shard_map/ppermute | solution.py:24
  26.4 0.0 collective-permute-done.2
  26.4 0.0 collective-permute-done.3
  26.5 0.0 copy-start
  26.5 9.1 %collective-permute-start.6 = (bf16[8,4096]{1,0:T(8,128)(2,1)S(1)}, bf16[8,4096]{1,0:T(8,128)(2,1)S(1)}, u32[]{:S(2)}, u32[]{:S(2)}) collective-permute-start(bf16[8,4096]{1,0:T(8,128)(2,1)S(1)} %add_convert_fusion.3), channel_id=1, source_target_pairs={{0,8},{1,9},{2,10},{3,11},{4,12},{5,13},{6,14},{7,15},{8,0},{9,1},... | collective-permute-start | bytes 196616 | tf_op jit(solution)/shard_map/ppermute | solution.py:24
  35.6 3.9 %collective-permute-start.5 = (bf16[16,4096]{1,0:T(8,128)(2,1)S(1)}, bf16[16,4096]{1,0:T(8,128)(2,1)S(1)}, u32[]{:S(2)}, u32[]{:S(2)}) collective-permute-start(bf16[16,4096]{1,0:T(8,128)(2,1)S(1)} %pad_maximum_fusion.4), channel_id=1, source_target_pairs={{0,4},{1,5},{2,6},{3,7},{4,0},{5,1},{6,2},{7,3},{8,12},{9,13},{10,... | collective-permute-start | bytes 393224 | tf_op jit(solution)/shard_map/ppermute | solution.py:24
  39.5 0.0 collective-permute-done.4
  39.6 6.5 %collective-permute-done.5 = bf16[16,4096]{1,0:T(8,128)(2,1)S(1)} collective-permute-done((bf16[16,4096]{1,0:T(8,128)(2,1)S(1)}, bf16[16,4096]{1,0:T(8,128)(2,1)S(1)}, u32[]{:S(2)}, u32[]{:S(2)}) %collective-permute-start.5) | collective-permute-done | bytes 131104 | tf_op jit(solution)/shard_map/ppermute | solution.py:24
  46.1 0.0 collective-permute-done.6
  46.2 1.9 %collective-permute-start.7 = (bf16[8,4096]{1,0:T(8,128)(2,1)S(1)}, bf16[8,4096]{1,0:T(8,128)(2,1)S(1)}, u32[]{:S(2)}, u32[]{:S(2)}) collective-permute-start(bf16[8,4096]{1,0:T(8,128)(2,1)S(1)} %add_convert_fusion), channel_id=1, source_target_pairs={{0,4},{1,5},{2,6},{3,7},{4,0},{5,1},{6,2},{7,3},{8,12},{9,13},{10,... | collective-permute-start | bytes 196616 | tf_op jit(solution)/shard_map/ppermute | solution.py:24
  48.2 15.7 %collective-permute-start.9 = (bf16[8,4096]{1,0:T(8,128)(2,1)S(1)}, bf16[8,4096]{1,0:T(8,128)(2,1)S(1)}, u32[]{:S(2)}, u32[]{:S(2)}) collective-permute-start(bf16[8,4096]{1,0:T(8,128)(2,1)S(1)} %add_convert_fusion.1), channel_id=1, source_target_pairs={{0,16},{1,17},{2,18},{3,19},{4,20},{5,21},{6,22},{7,23},{8,24},{9,... | collective-permute-start | bytes 196616 | tf_op jit(solution)/shard_map/ppermute | solution.py:24
  63.9 4.1 %collective-permute-start.8 = (bf16[8,4096]{1,0:T(8,128)(2,1)S(1)}, bf16[8,4096]{1,0:T(8,128)(2,1)S(1)}, u32[]{:S(2)}, u32[]{:S(2)}) collective-permute-start(bf16[8,4096]{1,0:T(8,128)(2,1)S(1)} %add_convert_fusion.2), channel_id=1, source_target_pairs={{0,8},{1,9},{2,10},{3,11},{4,12},{5,13},{6,14},{7,15},{8,0},{9,1},... | collective-permute-start | bytes 196616 | tf_op jit(solution)/shard_map/ppermute | solution.py:24
  68.0 0.0 collective-permute-done.7
  68.0 4.7 %collective-permute-done.9 = bf16[8,4096]{1,0:T(8,128)(2,1)S(1)} collective-permute-done((bf16[8,4096]{1,0:T(8,128)(2,1)S(1)}, bf16[8,4096]{1,0:T(8,128)(2,1)S(1)}, u32[]{:S(2)}, u32[]{:S(2)}) %collective-permute-start.9) | collective-permute-done | bytes 65568 | tf_op jit(solution)/shard_map/ppermute | solution.py:24
  72.7 6.1 %collective-permute-done.8 = bf16[8,4096]{1,0:T(8,128)(2,1)S(1)} collective-permute-done((bf16[8,4096]{1,0:T(8,128)(2,1)S(1)}, bf16[8,4096]{1,0:T(8,128)(2,1)S(1)}, u32[]{:S(2)}, u32[]{:S(2)}) %collective-permute-start.8) | collective-permute-done | bytes 65568 | tf_op jit(solution)/shard_map/ppermute | solution.py:24
  78.8 0.1 reduce-precision_convert_fusion.own
  78.9 1.9 %collective-permute-start.10 = (bf16[8,4096]{1,0:T(8,128)(2,1)S(1)}, bf16[8,4096]{1,0:T(8,128)(2,1)S(1)}, u32[]{:S(2)}, u32[]{:S(2)}) collective-permute-start(bf16[8,4096]{1,0:T(8,128)(2,1)S(1)} %reduce-precision_convert_fusion.own), channel_id=1, source_target_pairs={{0,1},{1,0},{2,3},{3,2},{4,5},{5,4},{6,7},{7,6},{8,9},{9,8},{10,11... | collective-permute-start | bytes 196616 | tf_op jit(solution)/shard_map/ppermute | solution.py:28
  81.4 0.0 copy-done
  81.5 0.5 collective-permute-done.10.twin
  82.0 0.8 cast.1
  82.8 3.5 %collective-permute-start.11 = (bf16[8,4224]{1,0:T(8,128)(2,1)S(1)}, bf16[8,4224]{1,0:T(8,128)(2,1)S(1)}, u32[]{:S(2)}, u32[]{:S(2)}) collective-permute-start(bf16[8,4224]{1,0:T(8,128)(2,1)S(1)} %get-tuple-element.59), channel_id=1, source_target_pairs={{0,32},{1,33},{2,34},{3,35},{4,36},{5,37},{6,38},{7,39},{8,40},{9,... | collective-permute-start | bytes 202760 | tf_op jit(solution)/shard_map/ppermute | solution.py:37
  86.3 2.3 %prefetch.1.weight = bf16[288,8192]{1,0:T(8,128)(2,1)S(1)} custom-call(bf16[288,8192]{1,0:T(8,128)(2,1)} %bitcast.14), custom_call_target="tpu_custom_call" | custom-call | tf_op jit(solution)/shard_map/prefetch/pallas_call | solution.py:136
  88.6 12.2 %collective-permute-done.11.arrived = bf16[8,4224]{1,0:T(8,128)(2,1)S(1)} collective-permute-done((bf16[8,4224]{1,0:T(8,128)(2,1)S(1)}, bf16[8,4224]{1,0:T(8,128)(2,1)S(1)}, u32[]{:S(2)}, u32[]{:S(2)}) %collective-permute-start.11) | collective-permute-done | bytes 67616 | tf_op jit(solution)/shard_map/ppermute | solution.py:37
  100.8 7.8 %collective-permute-start.13 = (bf16[8,4224]{1,0:T(8,128)(2,1)S(1)}, bf16[8,4224]{1,0:T(8,128)(2,1)S(1)}, u32[]{:S(2)}, u32[]{:S(2)}) collective-permute-start(bf16[8,4224]{1,0:T(8,128)(2,1)S(1)} %get-tuple-element.76), channel_id=1, source_target_pairs={{0,8},{1,9},{2,10},{3,11},{4,12},{5,13},{6,14},{7,15},{8,0},{9,1},... | collective-permute-start | bytes 202760 | tf_op jit(solution)/shard_map/ppermute | solution.py:24
  108.7 7.6 %collective-permute-start.12 = (bf16[8,4224]{1,0:T(8,128)(2,1)S(1)}, bf16[8,4224]{1,0:T(8,128)(2,1)S(1)}, u32[]{:S(2)}, u32[]{:S(2)}) collective-permute-start(bf16[8,4224]{1,0:T(8,128)(2,1)S(1)} %get-tuple-element.76), channel_id=1, source_target_pairs={{0,16},{1,17},{2,18},{3,19},{4,20},{5,21},{6,22},{7,23},{8,24},{9,... | collective-permute-start | bytes 202760 | tf_op jit(solution)/shard_map/ppermute | solution.py:24
  116.3 1.9 %collective-permute-start.14 = (bf16[8,4224]{1,0:T(8,128)(2,1)S(1)}, bf16[8,4224]{1,0:T(8,128)(2,1)S(1)}, u32[]{:S(2)}, u32[]{:S(2)}) collective-permute-start(bf16[8,4224]{1,0:T(8,128)(2,1)S(1)} %get-tuple-element.76), channel_id=1, source_target_pairs={{0,4},{1,5},{2,6},{3,7},{4,0},{5,1},{6,2},{7,3},{8,12},{9,13},{10,... | collective-permute-start | bytes 202760 | tf_op jit(solution)/shard_map/ppermute | solution.py:24
  118.3 0.0 collective-permute-done.13
  118.3 8.3 %collective-permute-done.12 = bf16[8,4224]{1,0:T(8,128)(2,1)S(1)} collective-permute-done((bf16[8,4224]{1,0:T(8,128)(2,1)S(1)}, bf16[8,4224]{1,0:T(8,128)(2,1)S(1)}, u32[]{:S(2)}, u32[]{:S(2)}) %collective-permute-start.12) | collective-permute-done | bytes 67616 | tf_op jit(solution)/shard_map/ppermute | solution.py:24
  126.6 8.2 %collective-permute-start.16 = (bf16[16,4224]{1,0:T(8,128)(2,1)S(1)}, bf16[16,4224]{1,0:T(8,128)(2,1)S(1)}, u32[]{:S(2)}, u32[]{:S(2)}) collective-permute-start(bf16[16,4224]{1,0:T(8,128)(2,1)S(1)} %pad_maximum_fusion.3), channel_id=1, source_target_pairs={{0,4},{1,5},{2,6},{3,7},{4,0},{5,1},{6,2},{7,3},{8,12},{9,13},{10,... | collective-permute-start | bytes 405512 | tf_op jit(solution)/shard_map/ppermute | solution.py:24
  134.7 1.9 %collective-permute-start.17 = (bf16[8,4224]{1,0:T(8,128)(2,1)S(1)}, bf16[8,4224]{1,0:T(8,128)(2,1)S(1)}, u32[]{:S(2)}, u32[]{:S(2)}) collective-permute-start(bf16[8,4224]{1,0:T(8,128)(2,1)S(1)} %collective-permute-done.12), channel_id=1, source_target_pairs={{0,8},{1,9},{2,10},{3,11},{4,12},{5,13},{6,14},{7,15},{8,0},{9,1},... | collective-permute-start | bytes 202760 | tf_op jit(solution)/shard_map/ppermute | solution.py:24
  136.7 0.0 collective-permute-done.14
  136.7 1.9 %collective-permute-start.15 = (bf16[32,4224]{1,0:T(8,128)(2,1)S(1)}, bf16[32,4224]{1,0:T(8,128)(2,1)S(1)}, u32[]{:S(2)}, u32[]{:S(2)}) collective-permute-start(bf16[32,4224]{1,0:T(8,128)(2,1)S(1)} %maximum_maximum_fusion), channel_id=1, source_target_pairs={{0,2},{1,3},{2,0},{3,1},{4,6},{5,7},{6,4},{7,5},{8,10},{9,11},{10,... | collective-permute-start | bytes 811016 | tf_op jit(solution)/shard_map/ppermute | solution.py:24
  138.6 8.3 %collective-permute-done.17 = bf16[8,4224]{1,0:T(8,128)(2,1)S(1)} collective-permute-done((bf16[8,4224]{1,0:T(8,128)(2,1)S(1)}, bf16[8,4224]{1,0:T(8,128)(2,1)S(1)}, u32[]{:S(2)}, u32[]{:S(2)}) %collective-permute-start.17) | collective-permute-done | bytes 67616 | tf_op jit(solution)/shard_map/ppermute | solution.py:24
  146.9 1.9 %collective-permute-start.20 = (bf16[8,4224]{1,0:T(8,128)(2,1)S(1)}, bf16[8,4224]{1,0:T(8,128)(2,1)S(1)}, u32[]{:S(2)}, u32[]{:S(2)}) collective-permute-start(bf16[8,4224]{1,0:T(8,128)(2,1)S(1)} %collective-permute-done.17), channel_id=1, source_target_pairs={{0,6},{1,7},{2,4},{3,5},{4,2},{5,3},{6,0},{7,1},{8,14},{9,15},{10,... | collective-permute-start | bytes 202760 | tf_op jit(solution)/shard_map/ppermute | solution.py:24
  148.9 2.6 %collective-permute-start.19 = (bf16[8,4224]{1,0:T(8,128)(2,1)S(1)}, bf16[8,4224]{1,0:T(8,128)(2,1)S(1)}, u32[]{:S(2)}, u32[]{:S(2)}) collective-permute-start(bf16[8,4224]{1,0:T(8,128)(2,1)S(1)} %collective-permute-done.17), channel_id=1, source_target_pairs={{0,4},{1,5},{2,6},{3,7},{4,0},{5,1},{6,2},{7,3},{8,12},{9,13},{10,... | collective-permute-start | bytes 202760 | tf_op jit(solution)/shard_map/ppermute | solution.py:24
  151.5 0.0 collective-permute-done.16
  151.5 5.5 %collective-permute-start.18 = (bf16[24,4224]{1,0:T(8,128)(2,1)S(1)}, bf16[24,4224]{1,0:T(8,128)(2,1)S(1)}, u32[]{:S(2)}, u32[]{:S(2)}) collective-permute-start(bf16[24,4224]{1,0:T(8,128)(2,1)S(1)} %pad_maximum_fusion.1), channel_id=1, source_target_pairs={{0,2},{1,3},{2,0},{3,1},{4,6},{5,7},{6,4},{7,5},{8,10},{9,11},{10,... | collective-permute-start | bytes 608264 | tf_op jit(solution)/shard_map/ppermute | solution.py:24
  157.1 0.0 collective-permute-done.15
  157.2 3.6 %collective-permute-done.18 = bf16[24,4224]{1,0:T(8,128)(2,1)S(1)} collective-permute-done((bf16[24,4224]{1,0:T(8,128)(2,1)S(1)}, bf16[24,4224]{1,0:T(8,128)(2,1)S(1)}, u32[]{:S(2)}, u32[]{:S(2)}) %collective-permute-start.18) | collective-permute-done | bytes 202784 | tf_op jit(solution)/shard_map/ppermute | solution.py:24
  160.9 0.0 collective-permute-done.19
  160.9 0.0 collective-permute-done.20
  160.9 1.9 %collective-permute-start.21 = (bf16[128,4224]{1,0:T(8,128)(2,1)S(1)}, bf16[128,4224]{1,0:T(8,128)(2,1)S(1)}, u32[]{:S(2)}, u32[]{:S(2)}) collective-permute-start(bf16[128,4224]{1,0:T(8,128)(2,1)S(1)} %constant_dynamic-update-slice_fusion.a.twin), channel_id=1, source_target_pairs={{0,1},{1,0},{2,3},{3,2},{4,5},{5,4},{6,7},{7,6},{8,9},{9,8},{10,11... | collective-permute-start | bytes 3244040 | tf_op jit(solution)/shard_map/ppermute | solution.py:28
  162.9 0.7 maximum_select_fusion
  163.6 1.3 first_half.1.start
  164.9 0.6 collective-permute-done.21.a
  165.5 2.1 %second_half.1 = (bf16[288,128]{1,0:T(8,128)(2,1)}, f32[1]{0:T(128)}) custom-call(s32[4]{0:T(128)S(1)} %pad_add_fusion.ids, bf16[288,8192]{1,0:T(8,128)(2,1)S(1)} %prefetch.1.weight, bf16[128,4224]{1,0:T(8,128)(2,1)S(1)} %collective-permute-done.21.a, f32[288,128]{1,0:T(8,128)S(1)} %first_half.1.start, bf16[8,4224]{1,0:T(8,128)(2,1)S(1)} %collective-permute-done.11.arrived, ...), custom_call_target="tpu_custom_call" | custom-call | tf_op jit(solution)/shard_map/second_half/pallas_call | solution.py:193
  (37 shorter events, 0.7 us)
Async XLA Ops:
  3.4 4.7 %collective-permute-start = (bf16[128,4096]{1,0:T(8,128)(2,1)S(1)}, bf16[128,4096]{1,0:T(8,128)(2,1)S(1)}, u32[]{:S(2)}, u32[]{:S(2)}) collective-permute-start(bf16[128,4096]{1,0:T(8,128)(2,1)S(1)} %out_proj.3), channel_id=1, source_target_pairs={{0,1},{1,0},{2,3},{3,2},{4,5},{5,4},{6,7},{7,6},{8,9},{9,8},{10,11... | collective-permute-start | bytes 3145736 | tf_op jit(solution)/shard_map/ppermute | solution.py:28
  8.2 18.2 %collective-permute-start.2 = (bf16[8,4096]{1,0:T(8,128)(2,1)S(1)}, bf16[8,4096]{1,0:T(8,128)(2,1)S(1)}, u32[]{:S(2)}, u32[]{:S(2)}) collective-permute-start(bf16[8,4096]{1,0:T(8,128)(2,1)S(1)} %get-tuple-element.43), channel_id=1, source_target_pairs={{0,4},{1,5},{2,6},{3,7},{4,0},{5,1},{6,2},{7,3},{8,12},{9,13},{10,... | collective-permute-start | bytes 196616 | tf_op jit(solution)/shard_map/ppermute | solution.py:24
  13.4 13.0 %collective-permute-start.3 = (bf16[8,4096]{1,0:T(8,128)(2,1)S(1)}, bf16[8,4096]{1,0:T(8,128)(2,1)S(1)}, u32[]{:S(2)}, u32[]{:S(2)}) collective-permute-start(bf16[8,4096]{1,0:T(8,128)(2,1)S(1)} %get-tuple-element.44), channel_id=1, source_target_pairs={{0,6},{1,7},{2,4},{3,5},{4,2},{5,3},{6,0},{7,1},{8,14},{9,15},{10,... | collective-permute-start | bytes 196616 | tf_op jit(solution)/shard_map/ppermute | solution.py:24
  16.7 9.7 %collective-permute-start.1 = (bf16[24,4096]{1,0:T(8,128)(2,1)S(1)}, bf16[24,4096]{1,0:T(8,128)(2,1)S(1)}, u32[]{:S(2)}, u32[]{:S(2)}) collective-permute-start(bf16[24,4096]{1,0:T(8,128)(2,1)S(1)} %pad_maximum_fusion.2), channel_id=1, source_target_pairs={{0,2},{1,3},{2,0},{3,1},{4,6},{5,7},{6,4},{7,5},{8,10},{9,11},{10,... | collective-permute-start | bytes 589832 | tf_op jit(solution)/shard_map/ppermute | solution.py:24
  19.2 20.3 %collective-permute-start.4 = (bf16[32,4096]{1,0:T(8,128)(2,1)S(1)}, bf16[32,4096]{1,0:T(8,128)(2,1)S(1)}, u32[]{:S(2)}, u32[]{:S(2)}) collective-permute-start(bf16[32,4096]{1,0:T(8,128)(2,1)S(1)} %pad_maximum_fusion), channel_id=1, source_target_pairs={{0,2},{1,3},{2,0},{3,1},{4,6},{5,7},{6,4},{7,5},{8,10},{9,11},{10,... | collective-permute-start | bytes 786440 | tf_op jit(solution)/shard_map/ppermute | solution.py:24
  26.5 55.0 %copy-start = (bf16[8192]{0:T(1024)(128)(2,1)S(1)}, bf16[8192]{0:T(1024)(128)(2,1)}, u32[]{:S(2)}) copy-start(bf16[8192]{0:T(1024)(128)(2,1)} %param.9) | copy-start | bytes 49156
  26.5 19.6 %collective-permute-start.6 = (bf16[8,4096]{1,0:T(8,128)(2,1)S(1)}, bf16[8,4096]{1,0:T(8,128)(2,1)S(1)}, u32[]{:S(2)}, u32[]{:S(2)}) collective-permute-start(bf16[8,4096]{1,0:T(8,128)(2,1)S(1)} %add_convert_fusion.3), channel_id=1, source_target_pairs={{0,8},{1,9},{2,10},{3,11},{4,12},{5,13},{6,14},{7,15},{8,0},{9,1},... | collective-permute-start | bytes 196616 | tf_op jit(solution)/shard_map/ppermute | solution.py:24
  35.6 10.5 %collective-permute-start.5 = (bf16[16,4096]{1,0:T(8,128)(2,1)S(1)}, bf16[16,4096]{1,0:T(8,128)(2,1)S(1)}, u32[]{:S(2)}, u32[]{:S(2)}) collective-permute-start(bf16[16,4096]{1,0:T(8,128)(2,1)S(1)} %pad_maximum_fusion.4), channel_id=1, source_target_pairs={{0,4},{1,5},{2,6},{3,7},{4,0},{5,1},{6,2},{7,3},{8,12},{9,13},{10,... | collective-permute-start | bytes 393224 | tf_op jit(solution)/shard_map/ppermute | solution.py:24
  46.2 21.8 %collective-permute-start.7 = (bf16[8,4096]{1,0:T(8,128)(2,1)S(1)}, bf16[8,4096]{1,0:T(8,128)(2,1)S(1)}, u32[]{:S(2)}, u32[]{:S(2)}) collective-permute-start(bf16[8,4096]{1,0:T(8,128)(2,1)S(1)} %add_convert_fusion), channel_id=1, source_target_pairs={{0,4},{1,5},{2,6},{3,7},{4,0},{5,1},{6,2},{7,3},{8,12},{9,13},{10,... | collective-permute-start | bytes 196616 | tf_op jit(solution)/shard_map/ppermute | solution.py:24
  48.2 24.5 %collective-permute-start.9 = (bf16[8,4096]{1,0:T(8,128)(2,1)S(1)}, bf16[8,4096]{1,0:T(8,128)(2,1)S(1)}, u32[]{:S(2)}, u32[]{:S(2)}) collective-permute-start(bf16[8,4096]{1,0:T(8,128)(2,1)S(1)} %add_convert_fusion.1), channel_id=1, source_target_pairs={{0,16},{1,17},{2,18},{3,19},{4,20},{5,21},{6,22},{7,23},{8,24},{9,... | collective-permute-start | bytes 196616 | tf_op jit(solution)/shard_map/ppermute | solution.py:24
  63.9 14.9 %collective-permute-start.8 = (bf16[8,4096]{1,0:T(8,128)(2,1)S(1)}, bf16[8,4096]{1,0:T(8,128)(2,1)S(1)}, u32[]{:S(2)}, u32[]{:S(2)}) collective-permute-start(bf16[8,4096]{1,0:T(8,128)(2,1)S(1)} %add_convert_fusion.2), channel_id=1, source_target_pairs={{0,8},{1,9},{2,10},{3,11},{4,12},{5,13},{6,14},{7,15},{8,0},{9,1},... | collective-permute-start | bytes 196616 | tf_op jit(solution)/shard_map/ppermute | solution.py:24
  78.9 3.1 %collective-permute-start.10 = (bf16[8,4096]{1,0:T(8,128)(2,1)S(1)}, bf16[8,4096]{1,0:T(8,128)(2,1)S(1)}, u32[]{:S(2)}, u32[]{:S(2)}) collective-permute-start(bf16[8,4096]{1,0:T(8,128)(2,1)S(1)} %reduce-precision_convert_fusion.own), channel_id=1, source_target_pairs={{0,1},{1,0},{2,3},{3,2},{4,5},{5,4},{6,7},{7,6},{8,9},{9,8},{10,11... | collective-permute-start | bytes 196616 | tf_op jit(solution)/shard_map/ppermute | solution.py:28
  82.8 18.0 %collective-permute-start.11 = (bf16[8,4224]{1,0:T(8,128)(2,1)S(1)}, bf16[8,4224]{1,0:T(8,128)(2,1)S(1)}, u32[]{:S(2)}, u32[]{:S(2)}) collective-permute-start(bf16[8,4224]{1,0:T(8,128)(2,1)S(1)} %get-tuple-element.59), channel_id=1, source_target_pairs={{0,32},{1,33},{2,34},{3,35},{4,36},{5,37},{6,38},{7,39},{8,40},{9,... | collective-permute-start | bytes 202760 | tf_op jit(solution)/shard_map/ppermute | solution.py:37
  100.8 17.4 %collective-permute-start.13 = (bf16[8,4224]{1,0:T(8,128)(2,1)S(1)}, bf16[8,4224]{1,0:T(8,128)(2,1)S(1)}, u32[]{:S(2)}, u32[]{:S(2)}) collective-permute-start(bf16[8,4224]{1,0:T(8,128)(2,1)S(1)} %get-tuple-element.76), channel_id=1, source_target_pairs={{0,8},{1,9},{2,10},{3,11},{4,12},{5,13},{6,14},{7,15},{8,0},{9,1},... | collective-permute-start | bytes 202760 | tf_op jit(solution)/shard_map/ppermute | solution.py:24
  108.7 17.9 %collective-permute-start.12 = (bf16[8,4224]{1,0:T(8,128)(2,1)S(1)}, bf16[8,4224]{1,0:T(8,128)(2,1)S(1)}, u32[]{:S(2)}, u32[]{:S(2)}) collective-permute-start(bf16[8,4224]{1,0:T(8,128)(2,1)S(1)} %get-tuple-element.76), channel_id=1, source_target_pairs={{0,16},{1,17},{2,18},{3,19},{4,20},{5,21},{6,22},{7,23},{8,24},{9,... | collective-permute-start | bytes 202760 | tf_op jit(solution)/shard_map/ppermute | solution.py:24
  116.3 20.3 %collective-permute-start.14 = (bf16[8,4224]{1,0:T(8,128)(2,1)S(1)}, bf16[8,4224]{1,0:T(8,128)(2,1)S(1)}, u32[]{:S(2)}, u32[]{:S(2)}) collective-permute-start(bf16[8,4224]{1,0:T(8,128)(2,1)S(1)} %get-tuple-element.76), channel_id=1, source_target_pairs={{0,4},{1,5},{2,6},{3,7},{4,0},{5,1},{6,2},{7,3},{8,12},{9,13},{10,... | collective-permute-start | bytes 202760 | tf_op jit(solution)/shard_map/ppermute | solution.py:24
  126.6 24.9 %collective-permute-start.16 = (bf16[16,4224]{1,0:T(8,128)(2,1)S(1)}, bf16[16,4224]{1,0:T(8,128)(2,1)S(1)}, u32[]{:S(2)}, u32[]{:S(2)}) collective-permute-start(bf16[16,4224]{1,0:T(8,128)(2,1)S(1)} %pad_maximum_fusion.3), channel_id=1, source_target_pairs={{0,4},{1,5},{2,6},{3,7},{4,0},{5,1},{6,2},{7,3},{8,12},{9,13},{10,... | collective-permute-start | bytes 405512 | tf_op jit(solution)/shard_map/ppermute | solution.py:24
  134.7 12.2 %collective-permute-start.17 = (bf16[8,4224]{1,0:T(8,128)(2,1)S(1)}, bf16[8,4224]{1,0:T(8,128)(2,1)S(1)}, u32[]{:S(2)}, u32[]{:S(2)}) collective-permute-start(bf16[8,4224]{1,0:T(8,128)(2,1)S(1)} %collective-permute-done.12), channel_id=1, source_target_pairs={{0,8},{1,9},{2,10},{3,11},{4,12},{5,13},{6,14},{7,15},{8,0},{9,1},... | collective-permute-start | bytes 202760 | tf_op jit(solution)/shard_map/ppermute | solution.py:24
  136.7 20.4 %collective-permute-start.15 = (bf16[32,4224]{1,0:T(8,128)(2,1)S(1)}, bf16[32,4224]{1,0:T(8,128)(2,1)S(1)}, u32[]{:S(2)}, u32[]{:S(2)}) collective-permute-start(bf16[32,4224]{1,0:T(8,128)(2,1)S(1)} %maximum_maximum_fusion), channel_id=1, source_target_pairs={{0,2},{1,3},{2,0},{3,1},{4,6},{5,7},{6,4},{7,5},{8,10},{9,11},{10,... | collective-permute-start | bytes 811016 | tf_op jit(solution)/shard_map/ppermute | solution.py:24
  146.9 14.0 %collective-permute-start.20 = (bf16[8,4224]{1,0:T(8,128)(2,1)S(1)}, bf16[8,4224]{1,0:T(8,128)(2,1)S(1)}, u32[]{:S(2)}, u32[]{:S(2)}) collective-permute-start(bf16[8,4224]{1,0:T(8,128)(2,1)S(1)} %collective-permute-done.17), channel_id=1, source_target_pairs={{0,6},{1,7},{2,4},{3,5},{4,2},{5,3},{6,0},{7,1},{8,14},{9,15},{10,... | collective-permute-start | bytes 202760 | tf_op jit(solution)/shard_map/ppermute | solution.py:24
  148.9 12.0 %collective-permute-start.19 = (bf16[8,4224]{1,0:T(8,128)(2,1)S(1)}, bf16[8,4224]{1,0:T(8,128)(2,1)S(1)}, u32[]{:S(2)}, u32[]{:S(2)}) collective-permute-start(bf16[8,4224]{1,0:T(8,128)(2,1)S(1)} %collective-permute-done.17), channel_id=1, source_target_pairs={{0,4},{1,5},{2,6},{3,7},{4,0},{5,1},{6,2},{7,3},{8,12},{9,13},{10,... | collective-permute-start | bytes 202760 | tf_op jit(solution)/shard_map/ppermute | solution.py:24
  151.5 9.2 %collective-permute-start.18 = (bf16[24,4224]{1,0:T(8,128)(2,1)S(1)}, bf16[24,4224]{1,0:T(8,128)(2,1)S(1)}, u32[]{:S(2)}, u32[]{:S(2)}) collective-permute-start(bf16[24,4224]{1,0:T(8,128)(2,1)S(1)} %pad_maximum_fusion.1), channel_id=1, source_target_pairs={{0,2},{1,3},{2,0},{3,1},{4,6},{5,7},{6,4},{7,5},{8,10},{9,11},{10,... | collective-permute-start | bytes 608264 | tf_op jit(solution)/shard_map/ppermute | solution.py:24
  160.9 4.6 %collective-permute-start.21 = (bf16[128,4224]{1,0:T(8,128)(2,1)S(1)}, bf16[128,4224]{1,0:T(8,128)(2,1)S(1)}, u32[]{:S(2)}, u32[]{:S(2)}) collective-permute-start(bf16[128,4224]{1,0:T(8,128)(2,1)S(1)} %constant_dynamic-update-slice_fusion.a.twin), channel_id=1, source_target_pairs={{0,1},{1,0},{2,3},{3,2},{4,5},{5,4},{6,7},{7,6},{8,9},{9,8},{10,11... | collective-permute-start | bytes 3244040 | tf_op jit(solution)/shard_map/ppermute | solution.py:28

commit v7 on v5

--- a/solution.py
+++ b/solution.py
@@ -254,14 +254,14 @@
 
 def gather_rounds(own):
     b = {0: own}
-    for d in (8, 4, 2):
+    for d in (8, 4):
         b[d] = across(own, d)
     b[12] = across(b[8], 4)
-    two = cat(b[8], b[4])
-    b[10], b[6] = split(across(two, 2))
-    b[9], b[5], b[3], b[1] = split(across(cat(b[8], b[4], b[2], own), 1))
+    three = cat(b[8], b[4], own)
+    b[10], b[6], b[2] = split(across(three, 2))
+    b[9], b[5], b[1] = split(across(three, 1))
     b[14] = across(b[12], 2)
-    b[13], b[11], b[7] = split(across(cat(b[12], b[10], b[6]), 1))
+    b[13], b[11], b[7], b[3] = split(across(cat(b[12], b[10], b[6], b[2]), 1))
     b[15] = across(b[14], 1)
     return cat(*[b[o] for o in range(CHIPS)])
 

time: 173 us -> 167 us (0.965)
  starting transfers between devices: 102 us -> 89.7 us
  waiting for transfers between devices: 55.7 us -> 61.2 us
    ppermute x18 -> x17, starting transfers between devices: 76.8 us -> 65.9 us  [across(): return lax.ppermute(x, 'tp', [(i, i ^ 2 * d) for i in range(TP)])]
    ppermute x18 -> x17, waiting for transfers between devices: 41.3 us -> 44.4 us  [across(): return lax.ppermute(x, 'tp', [(i, i ^ 2 * d) for i in range(TP)])]
    ppermute x1, waiting for transfers between devices: 13.9 us -> 16.3 us  [next_section(): return lax.ppermute(x, ('section', 'tp'), pairs)]
  transfers between devices with their start and end apart: 22 -> 21, of which waited for: 11 -> 10; matrix products, arithmetic and copies ran while one was open for 1% -> 1% of each run, Pallas kernels for 4% -> 4%
where the time goes in v7:
time: 167 us; the launch traced here: 166 us
  starting transfers between devices  89.7 us (54%)
  waiting for transfers between devices  61.2 us (37%)
  Pallas kernels  11.9 us (7%)
  between operations  1.79 us (1%)
    ppermute x17, starting transfers between devices, across(): return lax.ppermute(x, 'tp', [(i, i ^ 2 * d) for i in range(TP)])  65.9 us
    ppermute x17, waiting for transfers between devices, across(): return lax.ppermute(x, 'tp', [(i, i ^ 2 * d) for i in range(TP)])  44.4 us
    ppermute x3, starting transfers between devices, other_core(): return lax.ppermute(x, 'tp', [(i, i ^ 1) for i in range(TP)])  21.9 us
    ppermute x1, waiting for transfers between devices, next_section(): return lax.ppermute(x, ('section', 'tp'), pairs)  16.3 us
    pallas_call x2, Pallas kernels, out_proj(): pl.pallas_call(out_proj_body, out_shape=jax.ShapeDtypeStruct((TOK, HALF),...  5.4 us
  transfers between devices with their start and end apart: 21, of which 10 were waited for; matrix products, arithmetic and copies ran while one was open for 1% of the time, Pallas kernels for 4%

profile of v7, /device:TPU:1, one launch (start us, length us, event | category | flops | bytes accessed | tf_op | source)
XLA Modules:
  0.0 166.1 jit_solution(13427489167222183524)
XLA Ops:
  0.7 0.1 pad_add_fusion.ids
  0.7 2.7 %out_proj.3 = bf16[128,4096]{1,0:T(8,128)(2,1)S(1)} custom-call(s32[4]{0:T(128)S(1)} %pad_add_fusion.ids, bf16[128,256]{1,0:T(8,128)(2,1)} %bitcast.15, bf16[256,8192]{1,0:T(8,128)(2,1)} %weight.3, bf16[4,8192]{1,0:T(4,128)(2,1)} %bitcast.17), custom_call_target="tpu_custom_call" | custom-call | tf_op jit(solution)/shard_map/out_proj/pallas_call | solution.py:67
  3.4 16.0 %collective-permute-start = (bf16[128,4096]{1,0:T(8,128)(2,1)S(1)}, bf16[128,4096]{1,0:T(8,128)(2,1)S(1)}, u32[]{:S(2)}, u32[]{:S(2)}) collective-permute-start(bf16[128,4096]{1,0:T(8,128)(2,1)S(1)} %out_proj.3), channel_id=1, source_target_pairs={{0,1},{1,0},{2,3},{3,2},{4,5},{5,4},{6,7},{7,6},{8,9},{9,8},{10,11... | collective-permute-start | bytes 3145736 | tf_op jit(solution)/shard_map/ppermute | solution.py:28
  19.4 2.7 %out_proj.2 = f32[128,4096]{1,0:T(8,128)S(1)} custom-call(s32[4]{0:T(128)S(1)} %pad_add_fusion.ids, bf16[128,256]{1,0:T(8,128)(2,1)} %bitcast.16, bf16[256,8192]{1,0:T(8,128)(2,1)} %weight.3, bf16[4,8192]{1,0:T(4,128)(2,1)} %bitcast.18), custom_call_target="tpu_custom_call" | custom-call | tf_op jit(solution)/shard_map/out_proj/pallas_call | solution.py:67
  22.2 0.0 collective-permute-done
  22.2 1.9 %collective-permute-start.1 = (bf16[8,4096]{1,0:T(8,128)(2,1)S(1)}, bf16[8,4096]{1,0:T(8,128)(2,1)S(1)}, u32[]{:S(2)}, u32[]{:S(2)}) collective-permute-start(bf16[8,4096]{1,0:T(8,128)(2,1)S(1)} %fusion), channel_id=1, source_target_pairs={{0,2},{1,3},{2,0},{3,1},{4,6},{5,7},{6,4},{7,5},{8,10},{9,11},{10,... | collective-permute-start | bytes 196616 | tf_op jit(solution)/shard_map/ppermute | solution.py:24
  24.2 3.4 %collective-permute-start.2 = (bf16[24,4096]{1,0:T(8,128)(2,1)S(1)}, bf16[24,4096]{1,0:T(8,128)(2,1)S(1)}, u32[]{:S(2)}, u32[]{:S(2)}) collective-permute-start(bf16[24,4096]{1,0:T(8,128)(2,1)S(1)} %pad_maximum_fusion.2), channel_id=1, source_target_pairs={{0,2},{1,3},{2,0},{3,1},{4,6},{5,7},{6,4},{7,5},{8,10},{9,11},{10,... | collective-permute-start | bytes 589832 | tf_op jit(solution)/shard_map/ppermute | solution.py:24
  27.7 1.9 %collective-permute-start.4 = (bf16[32,4096]{1,0:T(8,128)(2,1)S(1)}, bf16[32,4096]{1,0:T(8,128)(2,1)S(1)}, u32[]{:S(2)}, u32[]{:S(2)}) collective-permute-start(bf16[32,4096]{1,0:T(8,128)(2,1)S(1)} %pad_maximum_fusion.1), channel_id=1, source_target_pairs={{0,2},{1,3},{2,0},{3,1},{4,6},{5,7},{6,4},{7,5},{8,10},{9,11},{10,... | collective-permute-start | bytes 786440 | tf_op jit(solution)/shard_map/ppermute | solution.py:24
  29.6 0.0 collective-permute-done.1
  29.6 1.9 %collective-permute-start.3 = (bf16[8,4096]{1,0:T(8,128)(2,1)S(1)}, bf16[8,4096]{1,0:T(8,128)(2,1)S(1)}, u32[]{:S(2)}, u32[]{:S(2)}) collective-permute-start(bf16[8,4096]{1,0:T(8,128)(2,1)S(1)} %add_convert_fusion.6), channel_id=1, source_target_pairs={{0,4},{1,5},{2,6},{3,7},{4,0},{5,1},{6,2},{7,3},{8,12},{9,13},{10,... | collective-permute-start | bytes 196616 | tf_op jit(solution)/shard_map/ppermute | solution.py:24
  31.6 1.0 collective-permute-done.2
  32.6 5.9 %collective-permute-done.3 = bf16[8,4096]{1,0:T(8,128)(2,1)S(1)} collective-permute-done((bf16[8,4096]{1,0:T(8,128)(2,1)S(1)}, bf16[8,4096]{1,0:T(8,128)(2,1)S(1)}, u32[]{:S(2)}, u32[]{:S(2)}) %collective-permute-start.3) | collective-permute-done | bytes 65568 | tf_op jit(solution)/shard_map/ppermute | solution.py:24
  38.6 0.0 copy-start
  38.6 1.9 %collective-permute-start.6 = (bf16[8,4096]{1,0:T(8,128)(2,1)S(1)}, bf16[8,4096]{1,0:T(8,128)(2,1)S(1)}, u32[]{:S(2)}, u32[]{:S(2)}) collective-permute-start(bf16[8,4096]{1,0:T(8,128)(2,1)S(1)} %add_convert_fusion.3), channel_id=1, source_target_pairs={{0,8},{1,9},{2,10},{3,11},{4,12},{5,13},{6,14},{7,15},{8,0},{9,1},... | collective-permute-start | bytes 196616 | tf_op jit(solution)/shard_map/ppermute | solution.py:24
  40.5 4.7 %collective-permute-start.5 = (bf16[16,4096]{1,0:T(8,128)(2,1)S(1)}, bf16[16,4096]{1,0:T(8,128)(2,1)S(1)}, u32[]{:S(2)}, u32[]{:S(2)}) collective-permute-start(bf16[16,4096]{1,0:T(8,128)(2,1)S(1)} %pad_maximum_fusion.3), channel_id=1, source_target_pairs={{0,4},{1,5},{2,6},{3,7},{4,0},{5,1},{6,2},{7,3},{8,12},{9,13},{10,... | collective-permute-start | bytes 393224 | tf_op jit(solution)/shard_map/ppermute | solution.py:24
  45.3 0.0 collective-permute-done.4
  45.3 8.8 %collective-permute-done.5 = bf16[16,4096]{1,0:T(8,128)(2,1)S(1)} collective-permute-done((bf16[16,4096]{1,0:T(8,128)(2,1)S(1)}, bf16[16,4096]{1,0:T(8,128)(2,1)S(1)}, u32[]{:S(2)}, u32[]{:S(2)}) %collective-permute-start.5) | collective-permute-done | bytes 131104 | tf_op jit(solution)/shard_map/ppermute | solution.py:24
  54.2 0.0 collective-permute-done.6
  54.3 1.9 %collective-permute-start.7 = (bf16[8,4096]{1,0:T(8,128)(2,1)S(1)}, bf16[8,4096]{1,0:T(8,128)(2,1)S(1)}, u32[]{:S(2)}, u32[]{:S(2)}) collective-permute-start(bf16[8,4096]{1,0:T(8,128)(2,1)S(1)} %add_convert_fusion), channel_id=1, source_target_pairs={{0,4},{1,5},{2,6},{3,7},{4,0},{5,1},{6,2},{7,3},{8,12},{9,13},{10,... | collective-permute-start | bytes 196616 | tf_op jit(solution)/shard_map/ppermute | solution.py:24
  56.2 6.3 %collective-permute-start.9 = (bf16[8,4096]{1,0:T(8,128)(2,1)S(1)}, bf16[8,4096]{1,0:T(8,128)(2,1)S(1)}, u32[]{:S(2)}, u32[]{:S(2)}) collective-permute-start(bf16[8,4096]{1,0:T(8,128)(2,1)S(1)} %add_convert_fusion.1), channel_id=1, source_target_pairs={{0,16},{1,17},{2,18},{3,19},{4,20},{5,21},{6,22},{7,23},{8,24},{9,... | collective-permute-start | bytes 196616 | tf_op jit(solution)/shard_map/ppermute | solution.py:24
  62.5 3.2 %collective-permute-start.8 = (bf16[8,4096]{1,0:T(8,128)(2,1)S(1)}, bf16[8,4096]{1,0:T(8,128)(2,1)S(1)}, u32[]{:S(2)}, u32[]{:S(2)}) collective-permute-start(bf16[8,4096]{1,0:T(8,128)(2,1)S(1)} %add_convert_fusion.2), channel_id=1, source_target_pairs={{0,8},{1,9},{2,10},{3,11},{4,12},{5,13},{6,14},{7,15},{8,0},{9,1},... | collective-permute-start | bytes 196616 | tf_op jit(solution)/shard_map/ppermute | solution.py:24
  65.7 0.0 collective-permute-done.7
  65.7 13.6 %collective-permute-done.9 = bf16[8,4096]{1,0:T(8,128)(2,1)S(1)} collective-permute-done((bf16[8,4096]{1,0:T(8,128)(2,1)S(1)}, bf16[8,4096]{1,0:T(8,128)(2,1)S(1)}, u32[]{:S(2)}, u32[]{:S(2)}) %collective-permute-start.9) | collective-permute-done | bytes 65568 | tf_op jit(solution)/shard_map/ppermute | solution.py:24
  79.3 0.0 collective-permute-done.8
  79.3 0.1 reduce-precision_convert_fusion.own
  79.4 2.6 %collective-permute-start.10 = (bf16[8,4096]{1,0:T(8,128)(2,1)S(1)}, bf16[8,4096]{1,0:T(8,128)(2,1)S(1)}, u32[]{:S(2)}, u32[]{:S(2)}) collective-permute-start(bf16[8,4096]{1,0:T(8,128)(2,1)S(1)} %reduce-precision_convert_fusion.own), channel_id=1, source_target_pairs={{0,1},{1,0},{2,3},{3,2},{4,5},{5,4},{6,7},{7,6},{8,9},{9,8},{10,11... | collective-permute-start | bytes 196616 | tf_op jit(solution)/shard_map/ppermute | solution.py:28
  82.6 0.0 copy-done
  82.7 0.2 collective-permute-done.10.twin
  82.9 0.8 cast.1
  83.6 1.9 %collective-permute-start.11 = (bf16[8,4224]{1,0:T(8,128)(2,1)S(1)}, bf16[8,4224]{1,0:T(8,128)(2,1)S(1)}, u32[]{:S(2)}, u32[]{:S(2)}) collective-permute-start(bf16[8,4224]{1,0:T(8,128)(2,1)S(1)} %get-tuple-element.63), channel_id=1, source_target_pairs={{0,32},{1,33},{2,34},{3,35},{4,36},{5,37},{6,38},{7,39},{8,40},{9,... | collective-permute-start | bytes 202760 | tf_op jit(solution)/shard_map/ppermute | solution.py:37
  85.5 16.3 %collective-permute-done.11.arrived = bf16[8,4224]{1,0:T(8,128)(2,1)S(1)} collective-permute-done((bf16[8,4224]{1,0:T(8,128)(2,1)S(1)}, bf16[8,4224]{1,0:T(8,128)(2,1)S(1)}, u32[]{:S(2)}, u32[]{:S(2)}) %collective-permute-start.11) | collective-permute-done | bytes 67616 | tf_op jit(solution)/shard_map/ppermute | solution.py:37
  101.9 16.1 %collective-permute-start.12 = (bf16[8,4224]{1,0:T(8,128)(2,1)S(1)}, bf16[8,4224]{1,0:T(8,128)(2,1)S(1)}, u32[]{:S(2)}, u32[]{:S(2)}) collective-permute-start(bf16[8,4224]{1,0:T(8,128)(2,1)S(1)} %get-tuple-element.78), channel_id=1, source_target_pairs={{0,16},{1,17},{2,18},{3,19},{4,20},{5,21},{6,22},{7,23},{8,24},{9,... | collective-permute-start | bytes 202760 | tf_op jit(solution)/shard_map/ppermute | solution.py:24
  117.9 1.9 %collective-permute-start.13 = (bf16[8,4224]{1,0:T(8,128)(2,1)S(1)}, bf16[8,4224]{1,0:T(8,128)(2,1)S(1)}, u32[]{:S(2)}, u32[]{:S(2)}) collective-permute-start(bf16[8,4224]{1,0:T(8,128)(2,1)S(1)} %get-tuple-element.78), channel_id=1, source_target_pairs={{0,8},{1,9},{2,10},{3,11},{4,12},{5,13},{6,14},{7,15},{8,0},{9,1},... | collective-permute-start | bytes 202760 | tf_op jit(solution)/shard_map/ppermute | solution.py:24
  119.9 2.3 %prefetch.1.weight = bf16[288,8192]{1,0:T(8,128)(2,1)S(1)} custom-call(bf16[288,8192]{1,0:T(8,128)(2,1)} %bitcast.14), custom_call_target="tpu_custom_call" | custom-call | tf_op jit(solution)/shard_map/prefetch/pallas_call | solution.py:136
  122.2 0.0 collective-permute-done.12
  122.2 7.3 %collective-permute-start.16 = (bf16[8,4224]{1,0:T(8,128)(2,1)S(1)}, bf16[8,4224]{1,0:T(8,128)(2,1)S(1)}, u32[]{:S(2)}, u32[]{:S(2)}) collective-permute-start(bf16[8,4224]{1,0:T(8,128)(2,1)S(1)} %collective-permute-done.12), channel_id=1, source_target_pairs={{0,8},{1,9},{2,10},{3,11},{4,12},{5,13},{6,14},{7,15},{8,0},{9,1},... | collective-permute-start | bytes 202760 | tf_op jit(solution)/shard_map/ppermute | solution.py:24
  129.5 1.2 collective-permute-done.13
  130.7 1.9 %collective-permute-start.15 = (bf16[24,4224]{1,0:T(8,128)(2,1)S(1)}, bf16[24,4224]{1,0:T(8,128)(2,1)S(1)}, u32[]{:S(2)}, u32[]{:S(2)}) collective-permute-start(bf16[24,4224]{1,0:T(8,128)(2,1)S(1)} %maximum_maximum_fusion), channel_id=1, source_target_pairs={{0,4},{1,5},{2,6},{3,7},{4,0},{5,1},{6,2},{7,3},{8,12},{9,13},{10,... | collective-permute-start | bytes 608264 | tf_op jit(solution)/shard_map/ppermute | solution.py:24
  132.6 0.0 collective-permute-done.16
  132.6 4.3 %collective-permute-start.18 = (bf16[8,4224]{1,0:T(8,128)(2,1)S(1)}, bf16[8,4224]{1,0:T(8,128)(2,1)S(1)}, u32[]{:S(2)}, u32[]{:S(2)}) collective-permute-start(bf16[8,4224]{1,0:T(8,128)(2,1)S(1)} %collective-permute-done.16), channel_id=1, source_target_pairs={{0,4},{1,5},{2,6},{3,7},{4,0},{5,1},{6,2},{7,3},{8,12},{9,13},{10,... | collective-permute-start | bytes 202760 | tf_op jit(solution)/shard_map/ppermute | solution.py:24
  136.9 2.0 %collective-permute-start.14 = (bf16[24,4224]{1,0:T(8,128)(2,1)S(1)}, bf16[24,4224]{1,0:T(8,128)(2,1)S(1)}, u32[]{:S(2)}, u32[]{:S(2)}) collective-permute-start(bf16[24,4224]{1,0:T(8,128)(2,1)S(1)} %maximum_maximum_fusion), channel_id=1, source_target_pairs={{0,2},{1,3},{2,0},{3,1},{4,6},{5,7},{6,4},{7,5},{8,10},{9,11},{10,... | collective-permute-start | bytes 608264 | tf_op jit(solution)/shard_map/ppermute | solution.py:24
  139.0 7.9 %collective-permute-done.18 = bf16[8,4224]{1,0:T(8,128)(2,1)S(1)} collective-permute-done((bf16[8,4224]{1,0:T(8,128)(2,1)S(1)}, bf16[8,4224]{1,0:T(8,128)(2,1)S(1)}, u32[]{:S(2)}, u32[]{:S(2)}) %collective-permute-start.18) | collective-permute-done | bytes 67616 | tf_op jit(solution)/shard_map/ppermute | solution.py:24
  146.9 1.9 %collective-permute-start.19 = (bf16[8,4224]{1,0:T(8,128)(2,1)S(1)}, bf16[8,4224]{1,0:T(8,128)(2,1)S(1)}, u32[]{:S(2)}, u32[]{:S(2)}) collective-permute-start(bf16[8,4224]{1,0:T(8,128)(2,1)S(1)} %collective-permute-done.18), channel_id=1, source_target_pairs={{0,2},{1,3},{2,0},{3,1},{4,6},{5,7},{6,4},{7,5},{8,10},{9,11},{10,... | collective-permute-start | bytes 202760 | tf_op jit(solution)/shard_map/ppermute | solution.py:24
  148.8 0.0 collective-permute-done.15
  148.8 3.4 %collective-permute-start.17 = (bf16[32,4224]{1,0:T(8,128)(2,1)S(1)}, bf16[32,4224]{1,0:T(8,128)(2,1)S(1)}, u32[]{:S(2)}, u32[]{:S(2)}) collective-permute-start(bf16[32,4224]{1,0:T(8,128)(2,1)S(1)} %pad_maximum_fusion), channel_id=1, source_target_pairs={{0,2},{1,3},{2,0},{3,1},{4,6},{5,7},{6,4},{7,5},{8,10},{9,11},{10,... | collective-permute-start | bytes 811016 | tf_op jit(solution)/shard_map/ppermute | solution.py:24
  152.2 0.0 collective-permute-done.14
  152.2 6.0 %collective-permute-done.17 = bf16[32,4224]{1,0:T(8,128)(2,1)S(1)} collective-permute-done((bf16[32,4224]{1,0:T(8,128)(2,1)S(1)}, bf16[32,4224]{1,0:T(8,128)(2,1)S(1)}, u32[]{:S(2)}, u32[]{:S(2)}) %collective-permute-start.17) | collective-permute-done | bytes 270368 | tf_op jit(solution)/shard_map/ppermute | solution.py:24
  158.4 0.0 collective-permute-done.19
  158.5 3.3 %collective-permute-start.20 = (bf16[128,4224]{1,0:T(8,128)(2,1)S(1)}, bf16[128,4224]{1,0:T(8,128)(2,1)S(1)}, u32[]{:S(2)}, u32[]{:S(2)}) collective-permute-start(bf16[128,4224]{1,0:T(8,128)(2,1)S(1)} %constant_dynamic-update-slice_fusion.a.twin), channel_id=1, source_target_pairs={{0,1},{1,0},{2,3},{3,2},{4,5},{5,4},{6,7},{7,6},{8,9},{9,8},{10,11... | collective-permute-start | bytes 3244040 | tf_op jit(solution)/shard_map/ppermute | solution.py:28
  161.8 0.7 maximum_select_fusion
  162.4 1.3 first_half.1.start
  163.8 0.3 collective-permute-done.20.a
  164.0 2.1 %second_half.1 = (bf16[288,128]{1,0:T(8,128)(2,1)}, f32[1]{0:T(128)}) custom-call(s32[4]{0:T(128)S(1)} %pad_add_fusion.ids, bf16[288,8192]{1,0:T(8,128)(2,1)S(1)} %prefetch.1.weight, bf16[128,4224]{1,0:T(8,128)(2,1)S(1)} %collective-permute-done.20.a, f32[288,128]{1,0:T(8,128)S(1)} %first_half.1.start, bf16[8,4224]{1,0:T(8,128)(2,1)S(1)} %collective-permute-done.11.arrived, ...), custom_call_target="tpu_custom_call" | custom-call | tf_op jit(solution)/shard_map/second_half/pallas_call | solution.py:193
  (37 shorter events, 0.7 us)
Async XLA Ops:
  3.4 18.8 %collective-permute-start = (bf16[128,4096]{1,0:T(8,128)(2,1)S(1)}, bf16[128,4096]{1,0:T(8,128)(2,1)S(1)}, u32[]{:S(2)}, u32[]{:S(2)}) collective-permute-start(bf16[128,4096]{1,0:T(8,128)(2,1)S(1)} %out_proj.3), channel_id=1, source_target_pairs={{0,1},{1,0},{2,3},{3,2},{4,5},{5,4},{6,7},{7,6},{8,9},{9,8},{10,11... | collective-permute-start | bytes 3145736 | tf_op jit(solution)/shard_map/ppermute | solution.py:28
  22.2 7.4 %collective-permute-start.1 = (bf16[8,4096]{1,0:T(8,128)(2,1)S(1)}, bf16[8,4096]{1,0:T(8,128)(2,1)S(1)}, u32[]{:S(2)}, u32[]{:S(2)}) collective-permute-start(bf16[8,4096]{1,0:T(8,128)(2,1)S(1)} %fusion), channel_id=1, source_target_pairs={{0,2},{1,3},{2,0},{3,1},{4,6},{5,7},{6,4},{7,5},{8,10},{9,11},{10,... | collective-permute-start | bytes 196616 | tf_op jit(solution)/shard_map/ppermute | solution.py:24
  24.2 8.3 %collective-permute-start.2 = (bf16[24,4096]{1,0:T(8,128)(2,1)S(1)}, bf16[24,4096]{1,0:T(8,128)(2,1)S(1)}, u32[]{:S(2)}, u32[]{:S(2)}) collective-permute-start(bf16[24,4096]{1,0:T(8,128)(2,1)S(1)} %pad_maximum_fusion.2), channel_id=1, source_target_pairs={{0,2},{1,3},{2,0},{3,1},{4,6},{5,7},{6,4},{7,5},{8,10},{9,11},{10,... | collective-permute-start | bytes 589832 | tf_op jit(solution)/shard_map/ppermute | solution.py:24
  27.7 17.6 %collective-permute-start.4 = (bf16[32,4096]{1,0:T(8,128)(2,1)S(1)}, bf16[32,4096]{1,0:T(8,128)(2,1)S(1)}, u32[]{:S(2)}, u32[]{:S(2)}) collective-permute-start(bf16[32,4096]{1,0:T(8,128)(2,1)S(1)} %pad_maximum_fusion.1), channel_id=1, source_target_pairs={{0,2},{1,3},{2,0},{3,1},{4,6},{5,7},{6,4},{7,5},{8,10},{9,11},{10,... | collective-permute-start | bytes 786440 | tf_op jit(solution)/shard_map/ppermute | solution.py:24
  29.6 8.9 %collective-permute-start.3 = (bf16[8,4096]{1,0:T(8,128)(2,1)S(1)}, bf16[8,4096]{1,0:T(8,128)(2,1)S(1)}, u32[]{:S(2)}, u32[]{:S(2)}) collective-permute-start(bf16[8,4096]{1,0:T(8,128)(2,1)S(1)} %add_convert_fusion.6), channel_id=1, source_target_pairs={{0,4},{1,5},{2,6},{3,7},{4,0},{5,1},{6,2},{7,3},{8,12},{9,13},{10,... | collective-permute-start | bytes 196616 | tf_op jit(solution)/shard_map/ppermute | solution.py:24
  38.6 44.0 %copy-start = (bf16[8192]{0:T(1024)(128)(2,1)S(1)}, bf16[8192]{0:T(1024)(128)(2,1)}, u32[]{:S(2)}) copy-start(bf16[8192]{0:T(1024)(128)(2,1)} %param.9) | copy-start | bytes 49156
  38.6 15.6 %collective-permute-start.6 = (bf16[8,4096]{1,0:T(8,128)(2,1)S(1)}, bf16[8,4096]{1,0:T(8,128)(2,1)S(1)}, u32[]{:S(2)}, u32[]{:S(2)}) collective-permute-start(bf16[8,4096]{1,0:T(8,128)(2,1)S(1)} %add_convert_fusion.3), channel_id=1, source_target_pairs={{0,8},{1,9},{2,10},{3,11},{4,12},{5,13},{6,14},{7,15},{8,0},{9,1},... | collective-permute-start | bytes 196616 | tf_op jit(solution)/shard_map/ppermute | solution.py:24
  40.5 13.6 %collective-permute-start.5 = (bf16[16,4096]{1,0:T(8,128)(2,1)S(1)}, bf16[16,4096]{1,0:T(8,128)(2,1)S(1)}, u32[]{:S(2)}, u32[]{:S(2)}) collective-permute-start(bf16[16,4096]{1,0:T(8,128)(2,1)S(1)} %pad_maximum_fusion.3), channel_id=1, source_target_pairs={{0,4},{1,5},{2,6},{3,7},{4,0},{5,1},{6,2},{7,3},{8,12},{9,13},{10,... | collective-permute-start | bytes 393224 | tf_op jit(solution)/shard_map/ppermute | solution.py:24
  54.3 11.5 %collective-permute-start.7 = (bf16[8,4096]{1,0:T(8,128)(2,1)S(1)}, bf16[8,4096]{1,0:T(8,128)(2,1)S(1)}, u32[]{:S(2)}, u32[]{:S(2)}) collective-permute-start(bf16[8,4096]{1,0:T(8,128)(2,1)S(1)} %add_convert_fusion), channel_id=1, source_target_pairs={{0,4},{1,5},{2,6},{3,7},{4,0},{5,1},{6,2},{7,3},{8,12},{9,13},{10,... | collective-permute-start | bytes 196616 | tf_op jit(solution)/shard_map/ppermute | solution.py:24
  56.2 23.1 %collective-permute-start.9 = (bf16[8,4096]{1,0:T(8,128)(2,1)S(1)}, bf16[8,4096]{1,0:T(8,128)(2,1)S(1)}, u32[]{:S(2)}, u32[]{:S(2)}) collective-permute-start(bf16[8,4096]{1,0:T(8,128)(2,1)S(1)} %add_convert_fusion.1), channel_id=1, source_target_pairs={{0,16},{1,17},{2,18},{3,19},{4,20},{5,21},{6,22},{7,23},{8,24},{9,... | collective-permute-start | bytes 196616 | tf_op jit(solution)/shard_map/ppermute | solution.py:24
  62.5 16.8 %collective-permute-start.8 = (bf16[8,4096]{1,0:T(8,128)(2,1)S(1)}, bf16[8,4096]{1,0:T(8,128)(2,1)S(1)}, u32[]{:S(2)}, u32[]{:S(2)}) collective-permute-start(bf16[8,4096]{1,0:T(8,128)(2,1)S(1)} %add_convert_fusion.2), channel_id=1, source_target_pairs={{0,8},{1,9},{2,10},{3,11},{4,12},{5,13},{6,14},{7,15},{8,0},{9,1},... | collective-permute-start | bytes 196616 | tf_op jit(solution)/shard_map/ppermute | solution.py:24
  79.4 3.5 %collective-permute-start.10 = (bf16[8,4096]{1,0:T(8,128)(2,1)S(1)}, bf16[8,4096]{1,0:T(8,128)(2,1)S(1)}, u32[]{:S(2)}, u32[]{:S(2)}) collective-permute-start(bf16[8,4096]{1,0:T(8,128)(2,1)S(1)} %reduce-precision_convert_fusion.own), channel_id=1, source_target_pairs={{0,1},{1,0},{2,3},{3,2},{4,5},{5,4},{6,7},{7,6},{8,9},{9,8},{10,11... | collective-permute-start | bytes 196616 | tf_op jit(solution)/shard_map/ppermute | solution.py:28
  83.6 18.2 %collective-permute-start.11 = (bf16[8,4224]{1,0:T(8,128)(2,1)S(1)}, bf16[8,4224]{1,0:T(8,128)(2,1)S(1)}, u32[]{:S(2)}, u32[]{:S(2)}) collective-permute-start(bf16[8,4224]{1,0:T(8,128)(2,1)S(1)} %get-tuple-element.63), channel_id=1, source_target_pairs={{0,32},{1,33},{2,34},{3,35},{4,36},{5,37},{6,38},{7,39},{8,40},{9,... | collective-permute-start | bytes 202760 | tf_op jit(solution)/shard_map/ppermute | solution.py:37
  101.9 20.4 %collective-permute-start.12 = (bf16[8,4224]{1,0:T(8,128)(2,1)S(1)}, bf16[8,4224]{1,0:T(8,128)(2,1)S(1)}, u32[]{:S(2)}, u32[]{:S(2)}) collective-permute-start(bf16[8,4224]{1,0:T(8,128)(2,1)S(1)} %get-tuple-element.78), channel_id=1, source_target_pairs={{0,16},{1,17},{2,18},{3,19},{4,20},{5,21},{6,22},{7,23},{8,24},{9,... | collective-permute-start | bytes 202760 | tf_op jit(solution)/shard_map/ppermute | solution.py:24
  117.9 12.7 %collective-permute-start.13 = (bf16[8,4224]{1,0:T(8,128)(2,1)S(1)}, bf16[8,4224]{1,0:T(8,128)(2,1)S(1)}, u32[]{:S(2)}, u32[]{:S(2)}) collective-permute-start(bf16[8,4224]{1,0:T(8,128)(2,1)S(1)} %get-tuple-element.78), channel_id=1, source_target_pairs={{0,8},{1,9},{2,10},{3,11},{4,12},{5,13},{6,14},{7,15},{8,0},{9,1},... | collective-permute-start | bytes 202760 | tf_op jit(solution)/shard_map/ppermute | solution.py:24
  122.2 10.4 %collective-permute-start.16 = (bf16[8,4224]{1,0:T(8,128)(2,1)S(1)}, bf16[8,4224]{1,0:T(8,128)(2,1)S(1)}, u32[]{:S(2)}, u32[]{:S(2)}) collective-permute-start(bf16[8,4224]{1,0:T(8,128)(2,1)S(1)} %collective-permute-done.12), channel_id=1, source_target_pairs={{0,8},{1,9},{2,10},{3,11},{4,12},{5,13},{6,14},{7,15},{8,0},{9,1},... | collective-permute-start | bytes 202760 | tf_op jit(solution)/shard_map/ppermute | solution.py:24
  130.7 18.1 %collective-permute-start.15 = (bf16[24,4224]{1,0:T(8,128)(2,1)S(1)}, bf16[24,4224]{1,0:T(8,128)(2,1)S(1)}, u32[]{:S(2)}, u32[]{:S(2)}) collective-permute-start(bf16[24,4224]{1,0:T(8,128)(2,1)S(1)} %maximum_maximum_fusion), channel_id=1, source_target_pairs={{0,4},{1,5},{2,6},{3,7},{4,0},{5,1},{6,2},{7,3},{8,12},{9,13},{10,... | collective-permute-start | bytes 608264 | tf_op jit(solution)/shard_map/ppermute | solution.py:24
  132.6 14.2 %collective-permute-start.18 = (bf16[8,4224]{1,0:T(8,128)(2,1)S(1)}, bf16[8,4224]{1,0:T(8,128)(2,1)S(1)}, u32[]{:S(2)}, u32[]{:S(2)}) collective-permute-start(bf16[8,4224]{1,0:T(8,128)(2,1)S(1)} %collective-permute-done.16), channel_id=1, source_target_pairs={{0,4},{1,5},{2,6},{3,7},{4,0},{5,1},{6,2},{7,3},{8,12},{9,13},{10,... | collective-permute-start | bytes 202760 | tf_op jit(solution)/shard_map/ppermute | solution.py:24
  136.9 15.3 %collective-permute-start.14 = (bf16[24,4224]{1,0:T(8,128)(2,1)S(1)}, bf16[24,4224]{1,0:T(8,128)(2,1)S(1)}, u32[]{:S(2)}, u32[]{:S(2)}) collective-permute-start(bf16[24,4224]{1,0:T(8,128)(2,1)S(1)} %maximum_maximum_fusion), channel_id=1, source_target_pairs={{0,2},{1,3},{2,0},{3,1},{4,6},{5,7},{6,4},{7,5},{8,10},{9,11},{10,... | collective-permute-start | bytes 608264 | tf_op jit(solution)/shard_map/ppermute | solution.py:24
  146.9 11.6 %collective-permute-start.19 = (bf16[8,4224]{1,0:T(8,128)(2,1)S(1)}, bf16[8,4224]{1,0:T(8,128)(2,1)S(1)}, u32[]{:S(2)}, u32[]{:S(2)}) collective-permute-start(bf16[8,4224]{1,0:T(8,128)(2,1)S(1)} %collective-permute-done.18), channel_id=1, source_target_pairs={{0,2},{1,3},{2,0},{3,1},{4,6},{5,7},{6,4},{7,5},{8,10},{9,11},{10,... | collective-permute-start | bytes 202760 | tf_op jit(solution)/shard_map/ppermute | solution.py:24
  148.8 9.4 %collective-permute-start.17 = (bf16[32,4224]{1,0:T(8,128)(2,1)S(1)}, bf16[32,4224]{1,0:T(8,128)(2,1)S(1)}, u32[]{:S(2)}, u32[]{:S(2)}) collective-permute-start(bf16[32,4224]{1,0:T(8,128)(2,1)S(1)} %pad_maximum_fusion), channel_id=1, source_target_pairs={{0,2},{1,3},{2,0},{3,1},{4,6},{5,7},{6,4},{7,5},{8,10},{9,11},{10,... | collective-permute-start | bytes 811016 | tf_op jit(solution)/shard_map/ppermute | solution.py:24
  158.5 5.6 %collective-permute-start.20 = (bf16[128,4224]{1,0:T(8,128)(2,1)S(1)}, bf16[128,4224]{1,0:T(8,128)(2,1)S(1)}, u32[]{:S(2)}, u32[]{:S(2)}) collective-permute-start(bf16[128,4224]{1,0:T(8,128)(2,1)S(1)} %constant_dynamic-update-slice_fusion.a.twin), channel_id=1, source_target_pairs={{0,1},{1,0},{2,3},{3,2},{4,5},{5,4},{6,7},{7,6},{8,9},{9,8},{10,11... | collective-permute-start | bytes 3244040 | tf_op jit(solution)/shard_map/ppermute | solution.py:28
